TPU v7x, 32 devices: a whole 2x2x4 slice. The times are simulated.
32 devices in a mesh: jobs: 2 (over x), seq: 16 (over z, y, core).
Axes of the slice: x: 2, y: 2, z: 4, core: 2. Of those that a mesh axis runs over, the one named last changes fastest.
Arguments:
- queries: bfloat16 [1024, 4096], P(('jobs', 'seq')), parts along dimension 0, may hold values from -12 to 12
- keys: bfloat16 [1024, 4096], P(('jobs', 'seq')), parts along dimension 0, may hold values from -6 to 6
- values: bfloat16 [1024, 4096], P(('jobs', 'seq')), parts along dimension 0, may hold values from -6 to 6
- live_counts: int32 [2, 16], P('jobs', 'seq'), parts along dimension 0, may hold values from 4 to 16, as said below
- merge_dest: int32 [2, 1024], P('jobs', 'seq'), parts along dimension 0, may hold values from 0 to 15, as said below
- latents: float32 [2, 1024, 64], P('jobs', 'seq'), parts along dimension 0, may hold values from -6 to 6
- guidance: float32 [2], P('jobs'), parts along dimension 0, may hold values from 3 to 6
- step_index: int32 [2], P('jobs'), parts along dimension 0, may hold values from 0 to 980
- out_weight: bfloat16 [4096, 64], replicated, may hold values from -0.09375 to 0.09375
Outputs:
- denoised: float32 [2, 1024, 64], P('jobs', 'seq'), parts along dimension 0
- merged_next: float32 [2, 256, 64], P('jobs', 'seq'), parts along dimension 0
There are 2 independent parts, one for each index of `jobs`. A program takes and returns all parts, laid end to end along the dimension named above; an argument that names none is the same for every part. Nothing has to cross between parts.
Inputs may be any that keep to these rules, and one draw needn't show every extreme that they name: `live_counts`: in every video some merge group has exactly 16 live slots. `merge_dest`: each token names a slot of its own merge group below that group's live count, and every live slot is named by at least one token.
All inputs are finite; a program needn't handle non-finite values.
Results may differ from a plain program's by a relative error of at most 0.0031.
Values may be sent and summed in bfloat16 or wider, within the bound.
No kernel may reach another device: no remote copies, remote signals or barrier semaphores. Data moves between devices by JAX's collectives and lax.ppermute only.
A program may use at most 64 MiB of HBM per device.

v0:
```python
import math

import jax
import jax.numpy as jnp
from jax import lax
from jax.sharding import PartitionSpec as P

HEADS = 32
HD = 128
TIMESTEPS = 1000
STRIDE = 20


neg_big = -1e30
shift_value = 5.0


def sigma_of(step_value):
    frac = 1.0 - step_value / TIMESTEPS
    return shift_value * frac / (1.0 + (shift_value - 1.0) * frac)


def attend_branch(query_rows, key_rows, value_rows, key_live, score_scale):
    total_rows = query_rows.shape[0]
    block_rows = 512 if total_rows % 512 == 0 else total_rows

    def one_block(query_block):
        scores = (
            lax.dot_general(
                query_block, key_rows, (((1,), (1,)), ((), ())), preferred_element_type=jnp.float32
            )
            * score_scale
        )
        scores = jnp.where(key_live[None, :], scores, neg_big)
        row_top = jnp.max(scores, axis=-1, keepdims=True)
        weights = jnp.exp(scores - row_top)
        probabilities = (weights / jnp.sum(weights, axis=-1, keepdims=True)).astype(jnp.bfloat16)
        return jnp.dot(probabilities, value_rows, preferred_element_type=jnp.float32).astype(
            jnp.bfloat16
        )

    blocks = query_rows.reshape(total_rows // block_rows, block_rows, query_rows.shape[1])
    return lax.map(one_block, blocks).reshape(total_rows, query_rows.shape[1])


def local(
    queries, keys, values, live_counts, merge_dest, latents, guidance, step_index, out_weight
):
    groups = lax.axis_size("seq")
    device = lax.axis_index("seq")
    pair_count = groups // 2
    local_rows, columns = queries.shape
    cap_half = local_rows // 2
    videos = guidance.shape[0]
    feature_width = columns // videos
    per_device = columns // groups
    item_count = per_device // HD
    branch_slots = groups * cap_half
    score_scale = 1.0 / math.sqrt(HD)
    counts_all = lax.all_gather(live_counts, "seq", axis=1, tiled=True)
    query_in, key_in, value_in = (
        lax.all_to_all(queries, "seq", split_axis=1, concat_axis=0, tiled=True),
        lax.all_to_all(keys, "seq", split_axis=1, concat_axis=0, tiled=True),
        lax.all_to_all(values, "seq", split_axis=1, concat_axis=0, tiled=True),
    )
    count_grid = counts_all.reshape(videos, 2, pair_count).transpose(0, 2, 1)
    live_slots = (
        jnp.arange(cap_half, dtype=jnp.int32)[None, None, None, :] < count_grid[..., None]
    ).reshape(videos, branch_slots)
    guided_parts = []
    head_numbers = []
    for item_index in range(item_count):
        global_item = device * item_count + item_index
        video_index = global_item // HEADS
        key_live = live_slots[video_index]
        col_start = item_index * HD
        branch_outs = []
        for branch_no in range(2):
            row_start = branch_no * branch_slots
            branch_outs.append(
                attend_branch(
                    query_in[row_start : row_start + branch_slots, col_start : col_start + HD],
                    key_in[row_start : row_start + branch_slots, col_start : col_start + HD],
                    value_in[row_start : row_start + branch_slots, col_start : col_start + HD],
                    key_live,
                    score_scale,
                )
            )
        conditioned = branch_outs[0].astype(jnp.float32)
        uncond = branch_outs[1].astype(jnp.float32)
        guided_parts.append(
            (uncond + guidance[video_index] * (conditioned - uncond)).astype(jnp.bfloat16)
        )
        head_numbers.append(global_item % HEADS)
    stacked = jnp.concatenate(guided_parts, axis=1)
    ordered = (
        stacked.reshape(pair_count, 2, cap_half, per_device)
        .transpose(1, 0, 2, 3)
        .reshape(groups * cap_half, per_device)
    )
    mixed = lax.all_to_all(ordered, "seq", split_axis=0, concat_axis=1, tiled=True)
    merged = jnp.einsum(
        "jva,ac->vjc",
        mixed.reshape(cap_half, videos, feature_width),
        out_weight,
        preferred_element_type=jnp.float32,
    )
    onehot = (merge_dest[..., None] == jnp.arange(cap_half, dtype=jnp.int32)).astype(jnp.float32)
    velocity = jnp.einsum("vrj,vjc->vrc", onehot, merged, precision=lax.Precision.HIGHEST)
    step_value = step_index.astype(jnp.float32)
    sigma_now = sigma_of(step_value)
    sigma_next = sigma_of(step_value + float(STRIDE))
    denoised = latents - sigma_now[:, None, None] * velocity
    advanced = latents + (sigma_next - sigma_now)[:, None, None] * velocity
    slot_sums = jnp.einsum("vrj,vrc->vjc", onehot, advanced, precision=lax.Precision.HIGHEST)
    slot_tally = jnp.sum(onehot, axis=1)
    merged_next = slot_sums / jnp.maximum(slot_tally, 1.0)[..., None]
    return (denoised, merged_next)


def solution(mesh):
    placed = (
        P(("jobs", "seq"), None),
        P(("jobs", "seq"), None),
        P(("jobs", "seq"), None),
        P("jobs", "seq"),
        P("jobs", "seq"),
        P("jobs", "seq", None),
        P("jobs"),
        P("jobs"),
        P(),
    )
    return jax.shard_map(
        local,
        mesh=mesh,
        in_specs=placed,
        out_specs=(P("jobs", "seq", None), P("jobs", "seq", None)),
        check_vma=False,
    )
```

profile of v0, /device:TPU:0, one launch (start us, length us, event | category | flops | bytes accessed | tf_op | source)
XLA Modules:
  0.0 69.5 jit_solution(11512666287636155792)
XLA Ops:
  0.6 1.7 %copy.78 = bf16[4,16,8,256]{3,2,0,1:T(8,128)(2,1)} copy(bf16[4,16,8,256]{3,2,1,0:T(8,128)(2,1)} %bitcast.66) | data formatting | bytes 524288 | tf_op jit(solution)/shard_map/all_to_all | solution.py:62
  2.4 7.5 %all-to-all-start = ((bf16[32,16,256]{2,0,1:T(8,128)(2,1)}), bf16[32,16,256]{2,0,1:T(8,128)(2,1)S(1)}, u32[]{:S(2)}, u32[]{:S(2)}) async-start(bf16[32,16,256]{2,0,1:T(8,128)(2,1)} %bitcast.62), calls=%async_computation | async-start | bytes 524288 | tf_op jit(solution)/shard_map/all_to_all | solution.py:62
  9.9 0.7 %copy.77 = bf16[4,16,8,256]{3,2,0,1:T(8,128)(2,1)} copy(bf16[4,16,8,256]{3,2,1,0:T(8,128)(2,1)S(1)} %bitcast.67) | data formatting | bytes 524288 | tf_op jit(solution)/shard_map/all_to_all | solution.py:63
  10.7 9.3 %all-to-all-done = bf16[32,16,256]{2,0,1:T(8,128)(2,1)S(1)} async-done(((bf16[32,16,256]{2,0,1:T(8,128)(2,1)}), bf16[32,16,256]{2,0,1:T(8,128)(2,1)S(1)}, u32[]{:S(2)}, u32[]{:S(2)}) %all-to-all-start) | async-done | bytes 262176 | tf_op jit(solution)/shard_map/all_to_all | solution.py:62
  19.9 3.7 %all-to-all-start.1 = ((bf16[32,16,256]{2,0,1:T(8,128)(2,1)}), bf16[32,16,256]{2,0,1:T(8,128)(2,1)S(1)}, u32[]{:S(2)}, u32[]{:S(2)}) async-start(bf16[32,16,256]{2,0,1:T(8,128)(2,1)} %bitcast.61), calls=%async_computation.1 | async-start | bytes 524288 | tf_op jit(solution)/shard_map/all_to_all | solution.py:63
  24.3 0.6 copy-done.5
  24.9 0.6 dynamic-slice.4
  25.5 0.7 bitcast_dynamic-update-slice_fusion
  26.2 12.4 %all-reduce = s32[16]{0:T(128)S(1)} all-reduce(s32[16]{0:T(128)S(1)} %bitcast_dynamic-update-slice_fusion), channel_id=1, replica_groups=mesh['jobs'=2,'seq'=16] {'seq'}, use_global_device_ids=true, to_apply=%add | all-reduce | flops 16 | bytes 128
  38.6 0.1 reshape.221
  38.7 0.1 copy.42
  38.8 0.1 lt.36
  38.9 0.7 %copy.76 = bf16[4,16,8,256]{3,2,0,1:T(8,128)(2,1)} copy(bf16[4,16,8,256]{3,2,1,0:T(8,128)(2,1)S(1)} %bitcast.68) | data formatting | bytes 524288 | tf_op jit(solution)/shard_map/all_to_all | solution.py:64
  40.3 3.5 %all-to-all-start.2 = ((bf16[32,16,256]{2,0,1:T(8,128)(2,1)}), bf16[32,16,256]{2,0,1:T(8,128)(2,1)S(1)}, u32[]{:S(2)}, u32[]{:S(2)}) async-start(bf16[32,16,256]{2,0,1:T(8,128)(2,1)} %bitcast.60), calls=%async_computation.2 | async-start | bytes 524288 | tf_op jit(solution)/shard_map/all_to_all | solution.py:64
  43.9 0.2 fusion.35
  44.1 0.2 fusion.36
  44.4 0.2 fusion.37
  44.6 0.2 fusion.38
  44.8 9.0 %all-to-all-done.2 = bf16[32,16,256]{2,0,1:T(8,128)(2,1)S(1)} async-done(((bf16[32,16,256]{2,0,1:T(8,128)(2,1)}), bf16[32,16,256]{2,0,1:T(8,128)(2,1)S(1)}, u32[]{:S(2)}, u32[]{:S(2)}) %all-to-all-start.2) | async-done | bytes 262176 | tf_op jit(solution)/shard_map/all_to_all | solution.py:64
  53.8 0.2 convolution_convert_fusion
  54.2 0.2 convolution_convert_fusion.1
  54.5 0.2 convolution_convert_fusion.2
  54.8 0.2 convolution_convert_fusion.3
  55.1 0.7 pad_maximum_fusion
  55.8 3.5 %all-to-all-start.3 = ((bf16[16,16,256]{2,1,0:T(8,128)(2,1)}), bf16[16,16,256]{2,1,0:T(8,128)(2,1)S(1)}, u32[]{:S(2)}, u32[]{:S(2)}) async-start(bf16[16,16,256]{2,1,0:T(8,128)(2,1)} %bitcast.23), calls=%async_computation.3 | async-start | bytes 262144 | tf_op jit(solution)/shard_map/all_to_all | solution.py:101
  59.3 0.6 copy-done.4
  59.9 0.1 convert_reduce_fusion
  60.8 6.3 %all-to-all-done.3 = bf16[16,16,256]{2,1,0:T(8,128)(2,1)S(1)} async-done(((bf16[16,16,256]{2,1,0:T(8,128)(2,1)}), bf16[16,16,256]{2,1,0:T(8,128)(2,1)S(1)}, u32[]{:S(2)}, u32[]{:S(2)}) %all-to-all-start.3) | async-done | bytes 131104 | tf_op jit(solution)/shard_map/all_to_all | solution.py:101
  67.2 0.2 fusion.39
  67.4 0.5 copy-done.3
  67.9 0.8 %bitcast_subtract_fusion = (f32[1,64,64]{2,1,0:T(8,128)}, f32[64,64]{1,0:T(8,128)S(1)}) fusion(f32[1,64,64]{2,1,0:T(8,128)S(1)} %copy-done.3, f32[]{:T(128)} %bitcast, f32[16,64]{1,0:T(8,128)S(1)} %fusion.39, s32[64]{0:T(128)S(1)} %bitcast.86), kind=kOutput, calls=%fused_computation.52 | convolution fusion | flops 795648 | bytes 53508 | tf_op jit(solution)/shard_map/vrj,vjc->vrc/dot_general | solution.py:109
  68.8 0.7 %fusion.4 = f32[1,16,64]{2,1,0:T(8,128)} fusion(f32[1,64,64]{2,1,0:T(8,128)S(1)} %copy-done.3, f32[64,64]{1,0:T(8,128)S(1)} %get-tuple-element.65, f32[]{:T(128)} %bitcast.27, f32[16]{0:T(128)S(1)} %broadcast_maximum_fusion, s32[64]{0:T(128)S(1)} %bitcast.87), kind=kOutput, calls=%fused_computation.13 | convolution fusion | flops 796672 | bytes 37188 | tf_op jit(solution)/shard_map/vrj,vrc->vjc/dot_general | solution.py:115
  (19 shorter events, 0.5 us)
Async XLA Ops:
  0.6 66.5 %copy-start = (bf16[4096,64]{0,1:T(8,128)(2,1)S(1)}, bf16[4096,64]{0,1:T(8,128)(2,1)}, u32[]{:S(2)}) copy-start(bf16[4096,64]{0,1:T(8,128)(2,1)} %param.17) | copy-start | bytes 1572868
  2.4 7.6 %copy-start.1 = (bf16[32,4096]{1,0:T(8,128)(2,1)S(1)}, bf16[32,4096]{1,0:T(8,128)(2,1)}, u32[]{:S(2)}) copy-start(bf16[32,4096]{1,0:T(8,128)(2,1)} %param.10) | copy-start | bytes 786436
  2.4 17.6 %all-to-all-start = ((bf16[32,16,256]{2,0,1:T(8,128)(2,1)}), bf16[32,16,256]{2,0,1:T(8,128)(2,1)S(1)}, u32[]{:S(2)}, u32[]{:S(2)}) async-start(bf16[32,16,256]{2,0,1:T(8,128)(2,1)} %bitcast.62), calls=%async_computation | async-start | bytes 524288 | tf_op jit(solution)/shard_map/all_to_all | solution.py:62
  19.9 19.0 %copy-start.2 = (bf16[32,4096]{1,0:T(8,128)(2,1)S(1)}, bf16[32,4096]{1,0:T(8,128)(2,1)}, u32[]{:S(2)}) copy-start(bf16[32,4096]{1,0:T(8,128)(2,1)} %param.11) | copy-start | bytes 786436
  19.9 20.4 %all-to-all-start.1 = ((bf16[32,16,256]{2,0,1:T(8,128)(2,1)}), bf16[32,16,256]{2,0,1:T(8,128)(2,1)S(1)}, u32[]{:S(2)}, u32[]{:S(2)}) async-start(bf16[32,16,256]{2,0,1:T(8,128)(2,1)} %bitcast.61), calls=%async_computation.1 | async-start | bytes 524288 | tf_op jit(solution)/shard_map/all_to_all | solution.py:63
  24.3 0.7 copy-start.5
  40.3 13.5 %all-to-all-start.2 = ((bf16[32,16,256]{2,0,1:T(8,128)(2,1)}), bf16[32,16,256]{2,0,1:T(8,128)(2,1)S(1)}, u32[]{:S(2)}, u32[]{:S(2)}) async-start(bf16[32,16,256]{2,0,1:T(8,128)(2,1)} %bitcast.60), calls=%async_computation.2 | async-start | bytes 524288 | tf_op jit(solution)/shard_map/all_to_all | solution.py:64
  55.8 11.4 %all-to-all-start.3 = ((bf16[16,16,256]{2,1,0:T(8,128)(2,1)}), bf16[16,16,256]{2,1,0:T(8,128)(2,1)S(1)}, u32[]{:S(2)}, u32[]{:S(2)}) async-start(bf16[16,16,256]{2,1,0:T(8,128)(2,1)} %bitcast.23), calls=%async_computation.3 | async-start | bytes 262144 | tf_op jit(solution)/shard_map/all_to_all | solution.py:101
  59.3 0.7 copy-start.4
  67.2 0.8 %copy-start.3 = (f32[1,64,64]{2,1,0:T(8,128)S(1)}, f32[1,64,64]{2,1,0:T(8,128)}, u32[]{:S(2)}) copy-start(f32[1,64,64]{2,1,0:T(8,128)} %param.14) | copy-start | bytes 49156
where the time goes:
time: 70.2 us; the launch traced here: 69.5 us
  waiting for transfers between devices  24.6 us (35%)
  starting transfers between devices  18.3 us (26%)
  blocking collectives  12.4 us (18%)
  local copies, waits for them, and re-layouts  6.53 us (9%)
  matrix products  3.66 us (5%)
  between operations  2.84 us (4%)
  other arithmetic  1.2 us (2%)
    unnamed x1, blocking collectives  12.4 us
    all_to_all x1, waiting for transfers between devices, local(): lax.all_to_all(queries, 'seq', split_axis=1, concat_axis=0, tiled=True)  9.28 us
    all_to_all x1, waiting for transfers between devices, local(): lax.all_to_all(values, 'seq', split_axis=1, concat_axis=0, tiled=True)  9.02 us
    all_to_all x1, starting transfers between devices, local(): lax.all_to_all(queries, 'seq', split_axis=1, concat_axis=0, tiled=True)  7.55 us
    all_to_all x1, waiting for transfers between devices, local(): lax.all_to_all(ordered, 'seq', split_axis=0, concat_axis=1, tiled=True)  6.34 us
    all_to_all x1, starting transfers between devices, local(): lax.all_to_all(keys, 'seq', split_axis=1, concat_axis=0, tiled=True)  3.66 us
    all_to_all x1, starting transfers between devices, local(): lax.all_to_all(values, 'seq', split_axis=1, concat_axis=0, tiled=True)  3.54 us
    all_to_all x1, starting transfers between devices, local(): lax.all_to_all(ordered, 'seq', split_axis=0, concat_axis=1, tiled=True)  3.51 us
  transfers between devices with their start and end apart: 4, of which 3 were waited for; matrix products, arithmetic and copies ran while one was open for 6% of the time, Pallas kernels for 0%

commit v1 on v0

v1 whole, which is shorter than its diff:
```python
import functools
import math

import jax
import jax.numpy as jnp
from jax import lax
from jax.experimental import pallas as pl
from jax.experimental.pallas import tpu as pltpu
from jax.sharding import PartitionSpec as P

HEADS = 32
HD = 128
TIMESTEPS = 1000
STRIDE = 20

neg_big = -1e30
shift_value = 5.0
dead_mark = 64.0


def sigma_of(step_value):
    frac = 1.0 - step_value / TIMESTEPS
    return shift_value * frac / (1.0 + (shift_value - 1.0) * frac)


def pack_kernel(own_ref, other_ref, place_ref, query_ref, key_ref, value_ref, out_ref):
    half, triple, per_device = out_ref.shape
    rows = triple // 3
    cap_half = rows // 2
    first_branch = place_ref[0] == 0
    row = lax.broadcasted_iota(jnp.int32, (rows, HD), 0)
    marks = []
    for video in range(own_ref.shape[0]):
        own, other = own_ref[video, 0], other_ref[video, 0]
        low = jnp.where(first_branch, own, other)
        high = jnp.where(first_branch, other, own)
        end = jnp.where(row < cap_half, low, cap_half + high)
        marks.append(jnp.where(row < end, 1.0, 0.0).astype(jnp.bfloat16))
    for item in range(half * per_device // HD):
        dest, column = divmod(item * HD, per_device)
        keep = marks[item // HEADS]
        source = slice(item * HD, (item + 1) * HD)
        target = slice(column, column + HD)
        key_tile = key_ref[:, source]
        out_ref[dest, :rows, target] = query_ref[:, source]
        out_ref[dest, rows : 2 * rows, target] = key_tile * keep + dead_mark * (1.0 - keep)
        out_ref[dest, 2 * rows :, target] = value_ref[:, source]


def attend_kernel(place_ref, guidance_ref, packed_ref, weight_ref, out_ref, *, score_scale):
    half, triple, per_device = packed_ref.shape
    rows = triple // 3
    cap_half = rows // 2
    channels = weight_ref.shape[0]
    slots = half * rows
    video = place_ref[2]
    scale = guidance_ref[video]
    factor = jnp.where(place_ref[0] == 0, scale, 1.0 - scale)
    if out_ref.shape[2] > 1:
        out_ref[...] = jnp.zeros_like(out_ref)
    block = 8 if half % 8 == 0 else half
    for start in range(0, half, block):
        total = jnp.zeros((channels, block * rows), jnp.float32)
        for item in range(per_device // HD):
            span = slice(item * HD, (item + 1) * HD)
            query = packed_ref[start : start + block, :rows, span].reshape(block * rows, HD)
            key = packed_ref[:, rows : 2 * rows, span].reshape(slots, HD)
            value = packed_ref[:, 2 * rows :, span].reshape(slots, HD)
            scores = (
                lax.dot_general(
                    key, query, (((1,), (1,)), ((), ())), preferred_element_type=jnp.float32
                )
                * score_scale
            )
            dead = key[:, :1].astype(jnp.float32) > 0.5 * dead_mark
            scores = jnp.where(dead, neg_big, scores)
            weights = jnp.exp(scores - jnp.max(scores, axis=0, keepdims=True))
            probabilities = (weights / jnp.sum(weights, axis=0, keepdims=True)).astype(jnp.bfloat16)
            attended = lax.dot_general(
                value, probabilities, (((0,), (0,)), ((), ())), preferred_element_type=jnp.float32
            ).astype(jnp.bfloat16)
            total += jnp.dot(weight_ref[:, span], attended, preferred_element_type=jnp.float32)
        part = (total * factor).T.reshape(block, 2, 2, cap_half // 2, channels)
        part = jnp.concatenate([part[:, :, 0], part[:, :, 1]], axis=-1)
        for group in range(2):
            out_ref[group, start : start + block, video] = part[:, group]


def finish_kernel(step_ref, parts_ref, dest_ref, latents_ref, denoised_ref, merged_ref):
    videos, tokens = dest_ref.shape
    channels = latents_ref.shape[2]
    cap_half = merged_ref.shape[1]
    for video in range(videos):
        lanes = jnp.sum(parts_ref[:, video], axis=0)
        merged = jnp.concatenate([lanes[:, :channels], lanes[:, channels:]], axis=0)
        slot = lax.broadcasted_iota(jnp.int32, (cap_half, tokens), 0)
        onehot = (dest_ref[video : video + 1, :] == slot).astype(jnp.float32)
        tally = jnp.sum(onehot, axis=1, keepdims=True)
        latents = latents_ref[video]
        latent_sums = jnp.dot(
            onehot, latents, precision=lax.Precision.HIGHEST, preferred_element_type=jnp.float32
        )
        velocity = lax.dot_general(
            onehot,
            merged,
            (((0,), (0,)), ((), ())),
            precision=lax.Precision.HIGHEST,
            preferred_element_type=jnp.float32,
        )
        step_value = jnp.full((1, channels), step_ref[video], jnp.int32).astype(jnp.float32)
        sigma_now = sigma_of(step_value)
        sigma_next = sigma_of(step_value + float(STRIDE))
        denoised_ref[video] = latents - sigma_now * velocity
        merged_ref[video] = (latent_sums + (sigma_next - sigma_now) * (tally * merged)) / jnp.maximum(
            tally, 1.0
        )


def local(
    queries, keys, values, live_counts, merge_dest, latents, guidance, step_index, out_weight
):
    groups = lax.axis_size("seq")
    device = lax.axis_index("seq")
    half = groups // 2
    rows, columns = queries.shape
    videos = guidance.shape[0]
    width, channels = out_weight.shape
    per_device = columns // half
    cap_half = rows // 2
    tokens = merge_dest.shape[1]
    seat = device % half
    place = jnp.stack(
        [device // half, (seat * per_device % width) // per_device, seat * per_device // width]
    ).astype(jnp.int32)
    smem = pl.BlockSpec(memory_space=pltpu.SMEM)
    vmem = pl.BlockSpec(memory_space=pltpu.VMEM)

    other_counts = lax.ppermute(live_counts, "seq", [(i, (i + half) % groups) for i in range(groups)])
    packed = pl.pallas_call(
        pack_kernel,
        out_shape=jax.ShapeDtypeStruct((half, 3 * rows, per_device), queries.dtype),
        in_specs=[smem, smem, smem, vmem, vmem, vmem],
        out_specs=vmem,
        name="pack",
    )(live_counts, other_counts, place, queries, keys, values)
    branches = [list(range(half)), list(range(half, groups))]
    gathered = lax.all_to_all(packed, "seq", 0, 0, axis_index_groups=branches, tiled=True)
    parts = pl.pallas_call(
        functools.partial(attend_kernel, score_scale=1.0 / math.sqrt(HD)),
        out_shape=jax.ShapeDtypeStruct(
            (2, half, videos, cap_half // 2, 2 * channels), jnp.float32
        ),
        grid_spec=pltpu.PrefetchScalarGridSpec(
            num_scalar_prefetch=1,
            grid=(1,),
            in_specs=[
                pl.BlockSpec(memory_space=pltpu.SMEM),
                pl.BlockSpec((half, 3 * rows, per_device), lambda i, place: (0, 0, 0)),
                pl.BlockSpec((channels, per_device), lambda i, place: (0, place[1])),
            ],
            out_specs=pl.BlockSpec(
                (2, half, videos, cap_half // 2, 2 * channels), lambda i, place: (0, 0, 0, 0, 0)
            ),
        ),
        name="attend",
    )(place, guidance, gathered, out_weight.T)
    parts = parts.reshape(groups, videos, cap_half // 2, 2 * channels)
    parts = lax.all_to_all(parts, "seq", 0, 0, tiled=True)
    return pl.pallas_call(
        finish_kernel,
        out_shape=(
            jax.ShapeDtypeStruct((videos, tokens, channels), jnp.float32),
            jax.ShapeDtypeStruct((videos, cap_half, channels), jnp.float32),
        ),
        in_specs=[smem, vmem, vmem, vmem],
        out_specs=(vmem, vmem),
        name="finish",
    )(step_index, parts, merge_dest, latents)


def solution(mesh):
    placed = (
        P(("jobs", "seq"), None),
        P(("jobs", "seq"), None),
        P(("jobs", "seq"), None),
        P("jobs", "seq"),
        P("jobs", "seq"),
        P("jobs", "seq", None),
        P("jobs"),
        P("jobs"),
        P(),
    )
    return jax.shard_map(
        local,
        mesh=mesh,
        in_specs=placed,
        out_specs=(P("jobs", "seq", None), P("jobs", "seq", None)),
        check_vma=False,
    )
```

time: 70.2 us -> 44.3 us (0.63)
  blocking collectives: 12.4 us -> 0 us
  Pallas kernels: 0 us -> 8.43 us
  waiting for transfers between devices: 24.6 us -> 17.6 us
  starting transfers between devices: 18.3 us -> 13.1 us
  local copies, waits for them, and re-layouts: 6.53 us -> 1.52 us
  matrix products: 3.66 us -> 0 us
    unnamed x1 -> x0, blocking collectives: 12.4 us -> none
    all_to_all x4 -> x2, starting transfers between devices: 18.3 us -> 9.01 us  [the longest x1 4.87 us: local(): parts = lax.all_to_all(parts, 'seq', 0, 0, tiled=True)]
    pallas_call x0 -> x3, Pallas kernels: none -> 8.43 us  [the longest x1 3.92 us: local(): pl.pallas_call(functools.partial(attend_kernel, score_scale=1.0 / math.sq...]
    all_to_all x4 -> x2, waiting for transfers between devices: 24.6 us -> 17.3 us  [the longest x1 11 us: local(): lax.all_to_all(packed, 'seq', 0, 0, axis_index_groups=branches, tiled=True)]
    ppermute x0 -> x1, starting transfers between devices: none -> 4.13 us  [local(): lax.ppermute(live_counts, 'seq', [(i, (i + half) % groups) for i in range...]
    dot_general x11 -> x0, matrix products: 3.66 us -> none  [the longest x4 0.96 us: one_block(): jnp.dot(probabilities, value_rows, preferred_element_type=jnp.float32)]
    all_to_all x3 -> x0, local copies, waits for them, and re-layouts: 3.18 us -> none  [the longest x1 1.73 us: local(): lax.all_to_all(queries, 'seq', split_axis=1, concat_axis=0, tiled=True)]
    unnamed x15 -> x4, local copies, waits for them, and re-layouts: 3.08 us -> 1.52 us
  transfers between devices with their start and end apart: 4 -> 3, of which waited for: 3 -> 3; matrix products, arithmetic and copies ran while one was open for 6% -> 1% of each run, Pallas kernels for 0% -> 0%
where the time goes in v1:
time: 44.3 us; the launch traced here: 43.9 us
  waiting for transfers between devices  17.6 us (40%)
  starting transfers between devices  13.1 us (30%)
  Pallas kernels  8.43 us (19%)
  between operations  2.66 us (6%)
  local copies, waits for them, and re-layouts  1.52 us (3%)
  other arithmetic  0.62 us (1%)
    all_to_all x1, waiting for transfers between devices, local(): lax.all_to_all(packed, 'seq', 0, 0, axis_index_groups=branches, tiled=True)  11 us
    all_to_all x1, waiting for transfers between devices, local(): parts = lax.all_to_all(parts, 'seq', 0, 0, tiled=True)  6.25 us
    all_to_all x1, starting transfers between devices, local(): parts = lax.all_to_all(parts, 'seq', 0, 0, tiled=True)  4.87 us
    all_to_all x1, starting transfers between devices, local(): lax.all_to_all(packed, 'seq', 0, 0, axis_index_groups=branches, tiled=True)  4.14 us
    ppermute x1, starting transfers between devices, local(): lax.ppermute(live_counts, 'seq', [(i, (i + half) % groups) for i in range...  4.13 us
    pallas_call x1, Pallas kernels, local(): pl.pallas_call(functools.partial(attend_kernel, score_scale=1.0 / math.sq...  3.92 us
    pallas_call x1, Pallas kernels, local(): pl.pallas_call(pack_kernel, out_shape=jax.ShapeDtypeStruct((half, 3 * row...  2.76 us
    pallas_call x1, Pallas kernels, local(): pl.pallas_call(finish_kernel, out_shape=(jax.ShapeDtypeStruct((videos, to...  1.76 us
  transfers between devices with their start and end apart: 3, of which 3 were waited for; matrix products, arithmetic and copies ran while one was open for 1% of the time, Pallas kernels for 0%

profile of v1, /device:TPU:0, one launch (start us, length us, event | category | flops | bytes accessed | tf_op | source)
XLA Modules:
  0.0 43.9 jit_solution(10967337148016217231)
XLA Ops:
  0.6 4.1 %collective-permute-start = (s32[1,1]{1,0:T(1,128)}, s32[1,1]{1,0:T(1,128)}, u32[]{:S(2)}, u32[]{:S(2)}) collective-permute-start(s32[1,1]{1,0:T(1,128)} %param.12), channel_id=1, source_target_pairs={{0,8},{1,9},{2,10},{3,11},{4,12},{5,13},{6,14},{7,15},{8,0},{9,1},... | collective-permute-start | bytes 20 | tf_op jit(solution)/shard_map/ppermute | solution.py:138
  5.5 0.6 %pad_add_fusion.place_ref = s32[3]{0:T(128)} fusion(s32[1]{0:T(128)} %bitcast.2, s32[1]{0:T(128)} %bitcast.1, s32[1]{0:T(128)} %bitcast), kind=kLoop, calls=%fused_computation | loop fusion | flops 6 | bytes 24 | tf_op jit(solution)/shard_map/stack | solution.py:132
  6.1 0.3 collective-permute-done.other_ref
  6.4 2.8 %pack.1 = bf16[8,96,512]{2,1,0:T(8,128)(2,1)} custom-call(s32[1,1]{1,0:T(1,128)S(6)} %copy.11.own_ref, s32[1,1]{1,0:T(1,128)} %collective-permute-done.other_ref, s32[3]{0:T(128)} %pad_add_fusion.place_ref, bf16[32,4096]{1,0:T(8,128)(2,1)} %query_ref.1, bf16[32,4096]{1,0:T(8,128)(2,1)} %key_ref.1, bf16[32,4096]{1,0:T(8,128)(2,1)} %value_ref.1), custom_call_target="tpu_custom_call" | custom-call | tf_op jit(solution)/shard_map/pack/pallas_call | solution.py:139
  9.2 4.1 %all-to-all-start = ((bf16[8,96,512]{2,1,0:T(8,128)(2,1)}), bf16[8,96,512]{2,1,0:T(8,128)(2,1)S(1)}, u32[]{:S(2)}, u32[]{:S(2)}) async-start(bf16[8,96,512]{2,1,0:T(8,128)(2,1)} %pack.1), calls=%async_computation | async-start | bytes 1572864 | tf_op jit(solution)/shard_map/all_to_all | solution.py:147
  13.9 11.0 %all-to-all-done.packed_ref = bf16[8,96,512]{2,1,0:T(8,128)(2,1)S(1)} async-done(((bf16[8,96,512]{2,1,0:T(8,128)(2,1)}), bf16[8,96,512]{2,1,0:T(8,128)(2,1)S(1)}, u32[]{:S(2)}, u32[]{:S(2)}) %all-to-all-start) | async-done | bytes 786464 | tf_op jit(solution)/shard_map/all_to_all | solution.py:147
  25.0 0.0 copy-start
  25.0 0.9 %copy-done = bf16[8,96,512]{2,1,0:T(8,128)(2,1)} copy-done((bf16[8,96,512]{2,1,0:T(8,128)(2,1)}, bf16[8,96,512]{2,1,0:T(8,128)(2,1)S(1)}, u32[]{:S(2)}) %copy-start) | copy-done | bytes 786456
  25.8 3.9 %attend.1 = f32[2,8,1,8,128]{4,3,2,1,0:T(8,128)} custom-call(s32[3]{0:T(128)} %pad_add_fusion.place_ref, f32[1]{0:T(128)S(6)} %copy.12.guidance_ref, bf16[8,96,512]{2,1,0:T(8,128)(2,1)} %copy-done, bf16[64,4096]{1,0:T(8,128)(2,1)} %bitcast.5), custom_call_target="tpu_custom_call" | custom-call | tf_op jit(solution)/shard_map/attend/pallas_call | solution.py:148
  29.8 4.9 %all-to-all-start.1 = ((f32[16,1,8,128]{3,2,1,0:T(8,128)}), f32[16,1,8,128]{3,2,1,0:T(8,128)S(1)}, u32[]{:S(2)}, u32[]{:S(2)}) async-start(f32[16,1,8,128]{3,2,1,0:T(8,128)} %bitcast.6), calls=%async_computation.1 | async-start | bytes 131072 | tf_op jit(solution)/shard_map/all_to_all | solution.py:168
  35.3 6.2 %all-to-all-done.1.parts_ref = f32[16,1,8,128]{3,2,1,0:T(8,128)S(1)} async-done(((f32[16,1,8,128]{3,2,1,0:T(8,128)}), f32[16,1,8,128]{3,2,1,0:T(8,128)S(1)}, u32[]{:S(2)}, u32[]{:S(2)}) %all-to-all-start.1) | async-done | bytes 65568 | tf_op jit(solution)/shard_map/all_to_all | solution.py:168
  41.5 0.0 copy-start.1
  41.5 0.6 %copy-done.1 = f32[16,1,8,128]{3,2,1,0:T(8,128)} copy-done((f32[16,1,8,128]{3,2,1,0:T(8,128)}, f32[16,1,8,128]{3,2,1,0:T(8,128)S(1)}, u32[]{:S(2)}) %copy-start.1) | copy-done | bytes 65560
  42.2 1.8 %finish.1 = (f32[1,64,64]{2,1,0:T(8,128)}, f32[1,16,64]{2,1,0:T(8,128)}) custom-call(s32[1]{0:T(128)S(6)} %copy.13.step_ref, f32[16,1,8,128]{3,2,1,0:T(8,128)} %copy-done.1, s32[1,64]{1,0:T(1,128)} %dest_ref.1, f32[1,64,64]{2,1,0:T(8,128)} %latents_ref.1), custom_call_target="tpu_custom_call" | custom-call | tf_op jit(solution)/shard_map/finish/pallas_call | solution.py:169
Async XLA Ops:
  0.6 5.8 %collective-permute-start = (s32[1,1]{1,0:T(1,128)}, s32[1,1]{1,0:T(1,128)}, u32[]{:S(2)}, u32[]{:S(2)}) collective-permute-start(s32[1,1]{1,0:T(1,128)} %param.12), channel_id=1, source_target_pairs={{0,8},{1,9},{2,10},{3,11},{4,12},{5,13},{6,14},{7,15},{8,0},{9,1},... | collective-permute-start | bytes 20 | tf_op jit(solution)/shard_map/ppermute | solution.py:138
  9.2 15.8 %all-to-all-start = ((bf16[8,96,512]{2,1,0:T(8,128)(2,1)}), bf16[8,96,512]{2,1,0:T(8,128)(2,1)S(1)}, u32[]{:S(2)}, u32[]{:S(2)}) async-start(bf16[8,96,512]{2,1,0:T(8,128)(2,1)} %pack.1), calls=%async_computation | async-start | bytes 1572864 | tf_op jit(solution)/shard_map/all_to_all | solution.py:147
  25.0 0.9 %copy-start = (bf16[8,96,512]{2,1,0:T(8,128)(2,1)}, bf16[8,96,512]{2,1,0:T(8,128)(2,1)S(1)}, u32[]{:S(2)}) copy-start(bf16[8,96,512]{2,1,0:T(8,128)(2,1)S(1)} %all-to-all-done.packed_ref) | copy-start | bytes 2359300
  29.8 11.8 %all-to-all-start.1 = ((f32[16,1,8,128]{3,2,1,0:T(8,128)}), f32[16,1,8,128]{3,2,1,0:T(8,128)S(1)}, u32[]{:S(2)}, u32[]{:S(2)}) async-start(f32[16,1,8,128]{3,2,1,0:T(8,128)} %bitcast.6), calls=%async_computation.1 | async-start | bytes 131072 | tf_op jit(solution)/shard_map/all_to_all | solution.py:168
  41.5 0.6 %copy-start.1 = (f32[16,1,8,128]{3,2,1,0:T(8,128)}, f32[16,1,8,128]{3,2,1,0:T(8,128)S(1)}, u32[]{:S(2)}) copy-start(f32[16,1,8,128]{3,2,1,0:T(8,128)S(1)} %all-to-all-done.1.parts_ref) | copy-start | bytes 196612

commit v2 on v1

v2 whole, which is shorter than its diff:
```python
import functools
import math

import jax
import jax.numpy as jnp
from jax import lax
from jax.experimental import pallas as pl
from jax.experimental.pallas import tpu as pltpu
from jax.sharding import PartitionSpec as P

HEADS = 32
HD = 128
TIMESTEPS = 1000
STRIDE = 20

neg_big = -1e30
shift_value = 5.0
small = pltpu.CompilerParams(vmem_limit_bytes=16 * 2**20)
large = pltpu.CompilerParams(vmem_limit_bytes=32 * 2**20)
def sigma_of(step_value):
    frac = 1.0 - step_value / TIMESTEPS
    return shift_value * frac / (1.0 + (shift_value - 1.0) * frac)


def pack_kernel(query_ref, key_ref, value_ref, out_ref, sems):
    half, triple, per_device = out_ref.shape
    rows = triple // 3
    copies = []
    for part, source in enumerate((query_ref, key_ref, value_ref)):
        for dest in range(half):
            copy = pltpu.make_async_copy(
                source.at[:, pl.ds(dest * per_device, per_device)],
                out_ref.at[dest, pl.ds(part * rows, rows), :],
                sems.at[part, dest],
            )
            copy.start()
            copies.append(copy)
    for copy in copies:
        copy.wait()


def attend_kernel(
    device_ref, guidance_ref, counts_ref, packed_ref, weight_ref, out_ref, *, score_scale
):
    half, triple, per_device = packed_ref.shape
    rows = triple // 3
    cap_half = rows // 2
    channels, width = weight_ref.shape
    slots = half * rows
    device = device_ref[0]
    seat = lax.rem(device, half)
    video = seat * per_device // width
    scale = guidance_ref[video]
    factor = jnp.where(device < half, scale, 1.0 - scale)
    slot = lax.broadcasted_iota(jnp.int32, (cap_half, 1), 0)
    mask = jnp.concatenate(
        [
            jnp.where(slot < counts_ref[video, group * half + pair], 0.0, neg_big)
            for pair in range(half)
            for group in range(2)
        ],
        axis=0,
    )
    weight = weight_ref[:, pl.ds(pl.multiple_of(lax.rem(seat * per_device, width), HD), per_device)]
    if out_ref.shape[2] > 1:
        out_ref[...] = jnp.zeros_like(out_ref)
    block = 8 if half % 8 == 0 else half
    for start in range(0, half, block):
        attended = []
        for item in range(per_device // HD):
            span = slice(item * HD, (item + 1) * HD)
            query = packed_ref[start : start + block, :rows, span].reshape(block * rows, HD)
            key = packed_ref[:, rows : 2 * rows, span].reshape(slots, HD)
            value = packed_ref[:, 2 * rows :, span].reshape(slots, HD)
            scores = (
                lax.dot_general(
                    key, query, (((1,), (1,)), ((), ())), preferred_element_type=jnp.float32
                )
                * score_scale
            )
            scores = scores + mask
            weights = jnp.exp(scores - jnp.max(scores, axis=0, keepdims=True))
            probabilities = (weights / jnp.sum(weights, axis=0, keepdims=True)).astype(jnp.bfloat16)
            attended.append(
                lax.dot_general(
                    value,
                    probabilities,
                    (((0,), (0,)), ((), ())),
                    preferred_element_type=jnp.float32,
                ).astype(jnp.bfloat16)
            )
        total = jnp.dot(
            weight, jnp.concatenate(attended, axis=0), preferred_element_type=jnp.float32
        )
        part = (total * factor).T.reshape(block, 2, 2, cap_half // 2, channels)
        part = jnp.concatenate([part[:, :, 0], part[:, :, 1]], axis=-1)
        for group in range(2):
            out_ref[group, start : start + block, video] = part[:, group]


def prepare_kernel(
    step_ref, dest_ref, latents_ref, spread_ref, means_ref, gains_ref, sigma_ref
):
    videos, tokens = dest_ref.shape
    channels = latents_ref.shape[2]
    cap_half = means_ref.shape[1]
    for video in range(videos):
        slot = lax.broadcasted_iota(jnp.int32, (cap_half, tokens), 0)
        onehot = (dest_ref[video : video + 1, :] == slot).astype(jnp.float32)
        tally = jnp.sum(onehot, axis=1, keepdims=True)
        count = jnp.maximum(tally, 1.0)
        latent_sums = jnp.dot(
            onehot,
            latents_ref[video],
            precision=lax.Precision.HIGHEST,
            preferred_element_type=jnp.float32,
        )
        step_value = jnp.full((1, channels), step_ref[video], jnp.int32).astype(jnp.float32)
        sigma_now = sigma_of(step_value)
        sigma_next = sigma_of(step_value + float(STRIDE))
        spread_ref[video] = jnp.concatenate([onehot] * 3, axis=0).T.astype(jnp.bfloat16)
        means_ref[video] = latent_sums / count
        gains_ref[video] = (sigma_next - sigma_now) * (tally / count)
        sigma_ref[video] = jnp.broadcast_to(sigma_now, sigma_ref.shape[1:])


def finish_kernel(
    parts_ref, spread_ref, means_ref, gains_ref, sigma_ref, latents_ref, denoised_ref, merged_ref
):
    videos, _, channels = latents_ref.shape
    for video in range(videos):
        lanes = jnp.sum(parts_ref[:, video], axis=0)
        merged = jnp.concatenate([lanes[:, :channels], lanes[:, channels:]], axis=0)
        merged_ref[video] = means_ref[video] + gains_ref[video] * merged
        top = merged.astype(jnp.bfloat16)
        rest = merged - top.astype(jnp.float32)
        middle = rest.astype(jnp.bfloat16)
        bottom = (rest - middle.astype(jnp.float32)).astype(jnp.bfloat16)
        velocity = jnp.dot(
            spread_ref[video],
            jnp.concatenate([top, middle, bottom], axis=0),
            preferred_element_type=jnp.float32,
        )
        denoised_ref[video] = latents_ref[video] - sigma_ref[video, :1] * velocity


def local(
    queries, keys, values, live_counts, merge_dest, latents, guidance, step_index, out_weight
):
    groups = lax.axis_size("seq")
    device = lax.axis_index("seq")
    half = groups // 2
    rows, columns = queries.shape
    videos = guidance.shape[0]
    channels = out_weight.shape[1]
    per_device = columns // half
    cap_half = rows // 2
    tokens = merge_dest.shape[1]
    smem = pl.BlockSpec(memory_space=pltpu.SMEM)
    vmem = pl.BlockSpec(memory_space=pltpu.VMEM)
    hbm = pl.BlockSpec(memory_space=pl.ANY)
    f32 = jnp.float32

    packed = pl.pallas_call(
        pack_kernel,
        out_shape=jax.ShapeDtypeStruct((half, 3 * rows, per_device), queries.dtype),
        in_specs=[hbm, hbm, hbm],
        out_specs=hbm,
        scratch_shapes=[pltpu.SemaphoreType.DMA((3, half))],
        compiler_params=small,
        name="pack",
    )(*(pltpu.with_memory_space_constraint(part, pltpu.HBM) for part in (queries, keys, values)))
    branches = [list(range(half)), list(range(half, groups))]
    gathered = lax.all_to_all(packed, "seq", 0, 0, axis_index_groups=branches, tiled=True)
    seats = lax.broadcasted_iota(jnp.int32, (videos, groups), 1)
    counts = lax.psum(jnp.where(seats == device, live_counts, 0), "seq")
    parts = pl.pallas_call(
        functools.partial(attend_kernel, score_scale=1.0 / math.sqrt(HD)),
        out_shape=jax.ShapeDtypeStruct((2, half, videos, cap_half // 2, 2 * channels), f32),
        in_specs=[smem, smem, smem, vmem, vmem],
        out_specs=vmem,
        compiler_params=large,
        name="attend",
    )(device.reshape(1), guidance, counts, gathered, out_weight.T)
    parts = parts.reshape(groups, videos, cap_half // 2, 2 * channels)
    parts = lax.all_to_all(parts, "seq", 0, 0, tiled=True)
    prepared = pl.pallas_call(
        prepare_kernel,
        out_shape=(
            jax.ShapeDtypeStruct((videos, tokens, 3 * cap_half), jnp.bfloat16),
            jax.ShapeDtypeStruct((videos, cap_half, channels), f32),
            jax.ShapeDtypeStruct((videos, cap_half, channels), f32),
            jax.ShapeDtypeStruct((videos, 8, channels), f32),
        ),
        in_specs=[smem, vmem, vmem],
        out_specs=(vmem, vmem, vmem, vmem),
        compiler_params=small,
        name="prepare",
    )(step_index, merge_dest, latents)
    return pl.pallas_call(
        finish_kernel,
        out_shape=(
            jax.ShapeDtypeStruct((videos, tokens, channels), f32),
            jax.ShapeDtypeStruct((videos, cap_half, channels), f32),
        ),
        in_specs=[vmem] * 6,
        out_specs=(vmem, vmem),
        compiler_params=small,
        name="finish",
    )(parts, *prepared, latents)


def solution(mesh):
    placed = (
        P(("jobs", "seq"), None),
        P(("jobs", "seq"), None),
        P(("jobs", "seq"), None),
        P("jobs", "seq"),
        P("jobs", "seq"),
        P("jobs", "seq", None),
        P("jobs"),
        P("jobs"),
        P(),
    )
    return jax.shard_map(
        local,
        mesh=mesh,
        in_specs=placed,
        out_specs=(P("jobs", "seq", None), P("jobs", "seq", None)),
        check_vma=False,
    )
```

time: 44.3 us -> 65.5 us (1.48)
  Pallas kernels: 8.43 us -> 29 us
  blocking collectives: 0 us -> 18.3 us
  waiting for transfers between devices: 17.6 us -> 6.03 us
  starting transfers between devices: 13.1 us -> 9.06 us
  local copies, waits for them, and re-layouts: 1.52 us -> 0.02 us
    pallas_call x1, Pallas kernels: 2.76 us -> 25.1 us  [local(): pl.pallas_call(pack_kernel, out_shape=jax.ShapeDtypeStruct((half, 3 * row...]
    psum x0 -> x1, blocking collectives: none -> 18.3 us  [local(): counts = lax.psum(jnp.where(seats == device, live_counts, 0), 'seq')]
    all_to_all x1, waiting for transfers between devices: 11 us -> 0.01 us  [local(): lax.all_to_all(packed, 'seq', 0, 0, axis_index_groups=branches, tiled=True)]
    ppermute x1 -> x0, starting transfers between devices: 4.13 us -> none  [local(): lax.ppermute(live_counts, 'seq', [(i, (i + half) % groups) for i in range...]
    unnamed x4 -> x6, local copies, waits for them, and re-layouts: 1.52 us -> 0.02 us
    all_to_all x1, starting transfers between devices: 4.14 us -> 5.43 us  [local(): lax.all_to_all(packed, 'seq', 0, 0, axis_index_groups=branches, tiled=True)]
    all_to_all x1, starting transfers between devices: 4.87 us -> 3.63 us  [local(): parts = lax.all_to_all(parts, 'seq', 0, 0, tiled=True)]
    pallas_call x1, Pallas kernels: 3.92 us -> 2.93 us  [local(): pl.pallas_call(functools.partial(attend_kernel, score_scale=1.0 / math.sq...]
  transfers between devices with their start and end apart: 3 -> 2, of which waited for: 3 -> 1; matrix products, arithmetic and copies ran while one was open for 1% -> 0% of each run, Pallas kernels for 0% -> 0%
where the time goes in v2:
time: 65.5 us; the launch traced here: 65.1 us
  Pallas kernels  29 us (44%)
  blocking collectives  18.3 us (28%)
  starting transfers between devices  9.06 us (14%)
  waiting for transfers between devices  6.03 us (9%)
  between operations  2.66 us (4%)
    pallas_call x1, Pallas kernels, local(): pl.pallas_call(pack_kernel, out_shape=jax.ShapeDtypeStruct((half, 3 * row...  25.1 us
    psum x1, blocking collectives, local(): counts = lax.psum(jnp.where(seats == device, live_counts, 0), 'seq')  18.3 us
    all_to_all x1, waiting for transfers between devices, local(): parts = lax.all_to_all(parts, 'seq', 0, 0, tiled=True)  6.03 us
    all_to_all x1, starting transfers between devices, local(): lax.all_to_all(packed, 'seq', 0, 0, axis_index_groups=branches, tiled=True)  5.43 us
    all_to_all x1, starting transfers between devices, local(): parts = lax.all_to_all(parts, 'seq', 0, 0, tiled=True)  3.63 us
    pallas_call x1, Pallas kernels, local(): pl.pallas_call(functools.partial(attend_kernel, score_scale=1.0 / math.sq...  2.93 us
  transfers between devices with their start and end apart: 2, of which 1 were waited for; matrix products, arithmetic and copies ran while one was open for 0% of the time, Pallas kernels for 0%

profile of v2, /device:TPU:0, one launch (start us, length us, event | category | flops | bytes accessed | tf_op | source)
XLA Modules:
  0.0 65.1 jit_solution(960317949413935001)
XLA Ops:
  0.6 25.1 %pack.1 = bf16[8,96,512]{2,1,0:T(8,128)(2,1)} custom-call(bf16[32,4096]{1,0:T(8,128)(2,1)} %query_ref.1, bf16[32,4096]{1,0:T(8,128)(2,1)} %key_ref.1, bf16[32,4096]{1,0:T(8,128)(2,1)} %value_ref.1), custom_call_target="tpu_custom_call" | custom-call | tf_op jit(solution)/shard_map/pack/pallas_call | solution.py:164
  25.8 0.0 copy-start
  25.8 5.4 %all-to-all-start = ((bf16[8,96,512]{2,1,0:T(8,128)(2,1)}), bf16[8,96,512]{2,1,0:T(8,128)(2,1)S(1)}, u32[]{:S(2)}, u32[]{:S(2)}) async-start(bf16[8,96,512]{2,1,0:T(8,128)(2,1)} %pack.1), calls=%async_computation | async-start | bytes 1572864 | tf_op jit(solution)/shard_map/all_to_all | solution.py:174
  31.9 18.3 %psum.7.counts_ref = s32[1,16]{1,0:T(1,128)S(1)} all-reduce(s32[1,16]{1,0:T(1,128)S(1)} %compare_select_fusion), channel_id=1, replica_groups=mesh['jobs'=2,'seq'=16] {'seq'}, use_global_device_ids=true, to_apply=%region_0.1 | all-reduce | flops 16 | bytes 128 | tf_op jit(solution)/shard_map/psum | solution.py:176
  50.9 0.0 all-to-all-done.packed_ref
  50.9 0.0 copy-done
  50.9 2.9 %attend.1 = f32[2,8,1,8,128]{4,3,2,1,0:T(8,128)} custom-call(s32[1]{0:T(128)} %bitcast.device_ref, f32[1]{0:T(128)S(6)} %copy.12.guidance_ref, s32[1,16]{1,0:T(1,128)S(1)} %psum.7.counts_ref, bf16[8,96,512]{2,1,0:T(8,128)(2,1)S(1)} %all-to-all-done.packed_ref, bf16[64,4096]{1,0:T(8,128)(2,1)S(1)} %bitcast.5), custom_call_target="tpu_custom_call" | custom-call | tf_op jit(solution)/shard_map/attend/pallas_call | solution.py:177
  53.8 0.0 copy-start.1
  53.8 3.6 %all-to-all-start.1 = ((f32[16,1,8,128]{3,2,1,0:T(8,128)}), f32[16,1,8,128]{3,2,1,0:T(8,128)S(1)}, u32[]{:S(2)}, u32[]{:S(2)}) async-start(f32[16,1,8,128]{3,2,1,0:T(8,128)} %bitcast.3), calls=%async_computation.1 | async-start | bytes 131072 | tf_op jit(solution)/shard_map/all_to_all | solution.py:186
  57.4 0.0 copy-start.2
  58.1 0.0 copy-done.1
  58.1 0.0 copy-done.2
  58.1 0.1 prepare.1
  58.3 6.0 %all-to-all-done.1.parts_ref = f32[16,1,8,128]{3,2,1,0:T(8,128)S(1)} async-done(((f32[16,1,8,128]{3,2,1,0:T(8,128)}), f32[16,1,8,128]{3,2,1,0:T(8,128)S(1)}, u32[]{:S(2)}, u32[]{:S(2)}) %all-to-all-start.1) | async-done | bytes 65568 | tf_op jit(solution)/shard_map/all_to_all | solution.py:186
  64.3 0.8 %finish.1 = (f32[1,64,64]{2,1,0:T(8,128)}, f32[1,16,64]{2,1,0:T(8,128)}) custom-call(f32[16,1,8,128]{3,2,1,0:T(8,128)S(1)} %all-to-all-done.1.parts_ref, bf16[1,64,48]{2,1,0:T(8,128)(2,1)S(1)} %get-tuple-element.6.spread_ref, f32[1,16,64]{2,1,0:T(8,128)S(1)} %get-tuple-element.7.means_ref, f32[1,16,64]{2,1,0:T(8,128)S(1)} %get-tuple-element.8.gains_ref, ...), custom_call_target="tpu_custom_call" | custom-call | tf_op jit(solution)/shard_map/finish/pallas_call | solution.py:200
  (1 shorter events, 0.0 us)
Async XLA Ops:
  25.8 25.1 %copy-start = (bf16[4096,64]{0,1:T(8,128)(2,1)S(1)}, bf16[4096,64]{0,1:T(8,128)(2,1)}, u32[]{:S(2)}) copy-start(bf16[4096,64]{0,1:T(8,128)(2,1)} %param.17) | copy-start | bytes 1572868
  25.8 25.1 %all-to-all-start = ((bf16[8,96,512]{2,1,0:T(8,128)(2,1)}), bf16[8,96,512]{2,1,0:T(8,128)(2,1)S(1)}, u32[]{:S(2)}, u32[]{:S(2)}) async-start(bf16[8,96,512]{2,1,0:T(8,128)(2,1)} %pack.1), calls=%async_computation | async-start | bytes 1572864 | tf_op jit(solution)/shard_map/all_to_all | solution.py:174
  53.8 4.3 %copy-start.1 = (f32[1,64,64]{2,1,0:T(8,128)S(1)}, f32[1,64,64]{2,1,0:T(8,128)}, u32[]{:S(2)}) copy-start(f32[1,64,64]{2,1,0:T(8,128)} %latents_ref.3) | copy-start | bytes 49156
  53.8 10.5 %all-to-all-start.1 = ((f32[16,1,8,128]{3,2,1,0:T(8,128)}), f32[16,1,8,128]{3,2,1,0:T(8,128)S(1)}, u32[]{:S(2)}, u32[]{:S(2)}) async-start(f32[16,1,8,128]{3,2,1,0:T(8,128)} %bitcast.3), calls=%async_computation.1 | async-start | bytes 131072 | tf_op jit(solution)/shard_map/all_to_all | solution.py:186
  57.4 0.7 %copy-start.2 = (s32[1,64]{1,0:T(1,128)S(1)}, s32[1,64]{1,0:T(1,128)}, u32[]{:S(2)}) copy-start(s32[1,64]{1,0:T(1,128)} %dest_ref.1) | copy-start | bytes 772

commit v3 on v2

v3 whole, which is shorter than its diff:
```python
import functools
import math

import jax
import jax.numpy as jnp
from jax import lax
from jax.experimental import pallas as pl
from jax.experimental.pallas import tpu as pltpu
from jax.sharding import PartitionSpec as P


HD = 128
NOTE_ROWS = 8
TIMESTEPS = 1000
STRIDE = 20

neg_big = -1e30
shift_value = 5.0
small = pltpu.CompilerParams(vmem_limit_bytes=16 * 2**20)
large = pltpu.CompilerParams(vmem_limit_bytes=32 * 2**20)


def sigma_of(step_value):
    frac = 1.0 - step_value / TIMESTEPS
    return shift_value * frac / (1.0 + (shift_value - 1.0) * frac)


def pack_kernel(device_ref, query_ref, key_ref, value_ref, *refs, steps):
    *out_refs, sems = refs
    count = len(steps)
    rows, columns = query_ref.shape
    per_pair = columns // count
    seat = lax.rem(device_ref[0], 2 * count)
    copies = []
    for place, step in enumerate(steps):
        start = pl.multiple_of((seat ^ step) // 2 * per_pair, HD)
        targets = (
            (key_ref, out_refs[place].at[pl.ds(0, rows), :]),
            (value_ref, out_refs[place].at[pl.ds(rows, rows), :]),
            (query_ref, out_refs[count + place].at[pl.ds(0, rows), :]),
        )
        for part, (source, target) in enumerate(targets):
            copy = pltpu.make_async_copy(
                source.at[:, pl.ds(start, per_pair)], target, sems.at[part, place]
            )
            copy.start()
            copies.append(copy)
    for copy in copies:
        copy.wait()


def note_kernel(device_ref, own_ref, other_ref, mate_own_ref, mate_other_ref, *refs, steps, width):
    count = len(steps)
    query_refs, out_refs, home_ref = refs[: count - 1], refs[count - 1 : -1], refs[-1]
    per_pair = query_refs[0].shape[1]
    first = query_refs[0].shape[0] - NOTE_ROWS
    device = device_ref[0]
    seat = lax.rem(device, 2 * count)
    front = device < 2 * count
    row = lax.broadcasted_iota(jnp.int32, (NOTE_ROWS, HD), 0)
    note = None
    for place, step in enumerate(steps):
        if note is None or own_ref.shape[0] > 1:
            video = (seat ^ step) // 2 * per_pair // width
            note = jnp.zeros((NOTE_ROWS, HD), jnp.int32)
            for line, (own, other) in enumerate(
                ((own_ref, other_ref), (mate_own_ref, mate_other_ref))
            ):
                low = jnp.where(front, own[video, 0], other[video, 0])
                high = jnp.where(front, other[video, 0], own[video, 0])
                note = jnp.where(row == 2 * line, low, jnp.where(row == 2 * line + 1, high, note))
            note = note.astype(jnp.float32).astype(jnp.bfloat16)
        if place == 0:
            home_ref[...] = note
        else:
            for column in range(0, per_pair, HD):
                out_refs[place - 1][first : first + NOTE_ROWS, column : column + HD] = note


def attend_kernel(device_ref, guidance_ref, weight_ref, home_ref, *refs, score_scale, steps):
    *pack_refs, out_ref = refs
    count = len(steps)
    own_refs, mate_refs = pack_refs[:count], pack_refs[count : 2 * count]
    query_refs = pack_refs[2 * count :]
    rows, per_pair = own_refs[0].shape[0] // 2, own_refs[0].shape[1]
    cap_half = rows // 2
    channels, width = weight_ref.shape
    device = device_ref[0]
    seat = lax.rem(device, 2 * count)
    start = seat // 2 * per_pair
    video = start // width
    scale = guidance_ref[video]
    factor = jnp.where(device < 2 * count, scale, 1.0 - scale)
    weight = weight_ref[:, pl.ds(pl.multiple_of(lax.rem(start, width), HD), per_pair)]
    if out_ref.shape[2] > 1:
        out_ref[...] = jnp.zeros_like(out_ref)

    slot = lax.broadcasted_iota(jnp.int32, (cap_half, HD), 0).astype(jnp.float32)
    masks = []
    for line in range(2):
        for place in range(count):
            if place:
                note = query_refs[place][rows : rows + NOTE_ROWS, :HD]
            else:
                note = home_ref[...]
            note = note.astype(jnp.float32)
            for group in range(2):
                live = note[2 * line + group : 2 * line + group + 1, :]
                masks.append(jnp.where(slot < live, 0.0, neg_big))
    mask = jnp.concatenate(masks)
    sources = (*own_refs, *mate_refs)
    block = max(1, HD // rows)
    for first in range(0, count, block):
        places = range(first, min(count, first + block))
        attended = []
        for column in range(0, per_pair, HD):
            span = slice(column, column + HD)
            query = jnp.concatenate([query_refs[place][:rows, span] for place in places])
            key = jnp.concatenate([ref[:rows, span] for ref in sources])
            value = jnp.concatenate([ref[rows:, span] for ref in sources])
            scores = lax.dot_general(
                key, query, (((1,), (1,)), ((), ())), preferred_element_type=jnp.float32
            )
            scores = scores + mask[:, : query.shape[0]]
            top = jnp.max(scores, axis=0, keepdims=True)
            weights = jnp.exp2((scores - top) * (score_scale * math.log2(math.e)))
            share = 1.0 / jnp.sum(weights, axis=0, keepdims=True)
            probabilities = (weights * share).astype(jnp.bfloat16)
            attended.append(
                lax.dot_general(
                    value,
                    probabilities,
                    (((0,), (0,)), ((), ())),
                    preferred_element_type=jnp.float32,
                ).astype(jnp.bfloat16)
            )
        total = jnp.dot(
            weight, jnp.concatenate(attended, axis=0), preferred_element_type=jnp.float32
        )
        part = (total * factor).T.reshape(len(places), 2, 2, cap_half // 2, channels)
        part = jnp.concatenate([part[:, :, 0], part[:, :, 1]], axis=-1)
        for place in places:
            for group in range(2):
                out_ref[group, (seat ^ steps[place]) // 2, video] = part[place - first, group]


def prepare_kernel(
    step_ref, dest_ref, latents_ref, spread_ref, means_ref, gains_ref, sigma_ref
):
    videos, tokens = dest_ref.shape
    channels = latents_ref.shape[2]
    cap_half = means_ref.shape[1]
    for video in range(videos):
        slot = lax.broadcasted_iota(jnp.int32, (cap_half, tokens), 0)
        onehot = (dest_ref[video : video + 1, :] == slot).astype(jnp.float32)
        tally = jnp.sum(onehot, axis=1, keepdims=True)
        count = jnp.maximum(tally, 1.0)
        latent_sums = jnp.dot(
            onehot,
            latents_ref[video],
            precision=lax.Precision.HIGHEST,
            preferred_element_type=jnp.float32,
        )
        step_value = jnp.full((1, channels), step_ref[video], jnp.int32).astype(jnp.float32)
        sigma_now = sigma_of(step_value)
        sigma_next = sigma_of(step_value + float(STRIDE))
        spread_ref[video] = jnp.concatenate([onehot] * 3, axis=0).T.astype(jnp.bfloat16)
        means_ref[video] = latent_sums / count
        gains_ref[video] = (sigma_next - sigma_now) * (tally / count)
        sigma_ref[video] = jnp.broadcast_to(sigma_now, sigma_ref.shape[1:])


def finish_kernel(
    parts_ref, spread_ref, means_ref, gains_ref, sigma_ref, latents_ref, denoised_ref, merged_ref
):
    videos, _, channels = latents_ref.shape
    for video in range(videos):
        lanes = jnp.sum(parts_ref[:, video], axis=0)
        merged = jnp.concatenate([lanes[:, :channels], lanes[:, channels:]], axis=0)
        merged_ref[video] = means_ref[video] + gains_ref[video] * merged
        top = merged.astype(jnp.bfloat16)
        rest = merged - top.astype(jnp.float32)
        middle = rest.astype(jnp.bfloat16)
        bottom = (rest - middle.astype(jnp.float32)).astype(jnp.bfloat16)
        velocity = jnp.dot(
            spread_ref[video],
            jnp.concatenate([top, middle, bottom], axis=0),
            preferred_element_type=jnp.float32,
        )
        denoised_ref[video] = latents_ref[video] - sigma_ref[video, :1] * velocity


def steps_of(half):
    first = [step for step in (0, 6, 2, 4) if step < half]
    return (*first, *range(8, half, 2))


def run(
    queries, keys, values, live_counts, merge_dest, latents, guidance, step_index, out_weight
):
    groups = lax.axis_size("seq")
    device = lax.axis_index("seq")
    half = groups // 2
    count = half // 2
    rows, columns = queries.shape
    videos = guidance.shape[0]
    width, channels = out_weight.shape
    per_pair = columns // count
    cap_half = rows // 2
    tokens = merge_dest.shape[1]
    smem = pl.BlockSpec(memory_space=pltpu.SMEM)
    vmem = pl.BlockSpec(memory_space=pltpu.VMEM)
    hbm = pl.BlockSpec(memory_space=pl.ANY)
    f32 = jnp.float32
    bf16 = queries.dtype

    def swap(part, step):
        return lax.ppermute(part, "seq", [(i, i ^ step) for i in range(groups)])

    steps = steps_of(half)
    seat = device.reshape(1)
    other_counts = swap(live_counts, half)
    kv_shape = jax.ShapeDtypeStruct((2 * rows, per_pair), bf16)
    note_shape = jax.ShapeDtypeStruct((rows + NOTE_ROWS, per_pair), bf16)
    query_shapes = [jax.ShapeDtypeStruct((rows, per_pair), bf16)] + [note_shape] * (count - 1)
    packed = pl.pallas_call(
        functools.partial(pack_kernel, steps=steps),
        out_shape=[kv_shape] * count + query_shapes,
        in_specs=[smem, hbm, hbm, hbm],
        out_specs=[vmem] * (2 * count),
        scratch_shapes=[pltpu.SemaphoreType.DMA((3, count))],
        compiler_params=small,
        name="pack",
    )(seat, *(pltpu.with_memory_space_constraint(part, pltpu.HBM) for part in (queries, keys, values)))
    own, asked = packed[:count], packed[count:]
    held = [own[0]] + [swap(own[place], steps[place]) for place in range(1, count)]
    mate_own = swap(live_counts, 1)
    mate_other = swap(other_counts, 1)
    *noted, home = pl.pallas_call(
        functools.partial(note_kernel, steps=steps, width=width),
        out_shape=[note_shape] * (count - 1) + [jax.ShapeDtypeStruct((NOTE_ROWS, HD), bf16)],
        in_specs=[smem] * 5 + [vmem] * (count - 1),
        out_specs=[vmem] * count,
        input_output_aliases={5 + place: place for place in range(count - 1)},
        compiler_params=small,
        name="note",
    )(seat, live_counts, other_counts, mate_own, mate_other, *asked[1:])
    asked = [asked[0]] + [swap(noted[place - 1], steps[place]) for place in range(1, count)]
    lent = [swap(held[0], 1)] + [swap(held[place], 1) for place in range(1, count)]
    parts = pl.pallas_call(
        functools.partial(attend_kernel, score_scale=1.0 / math.sqrt(HD), steps=steps),
        out_shape=jax.ShapeDtypeStruct((2, count, videos, cap_half // 2, 2 * channels), f32),
        in_specs=[smem, smem] + [vmem] * (2 + 3 * count),
        out_specs=vmem,
        compiler_params=large,
        name="attend",
    )(seat, guidance, out_weight.T, home, *held, *lent, *asked)
    parts = parts.reshape(half, videos, cap_half // 2, 2 * channels)
    parities = [list(range(parity, groups, 2)) for parity in range(2)]
    parts = lax.all_to_all(parts, "seq", 0, 0, axis_index_groups=parities, tiled=True)
    prepared = pl.pallas_call(
        prepare_kernel,
        out_shape=(
            jax.ShapeDtypeStruct((videos, tokens, 3 * cap_half), jnp.bfloat16),
            jax.ShapeDtypeStruct((videos, cap_half, channels), f32),
            jax.ShapeDtypeStruct((videos, cap_half, channels), f32),
            jax.ShapeDtypeStruct((videos, 8, channels), f32),
        ),
        in_specs=[smem, vmem, vmem],
        out_specs=(vmem, vmem, vmem, vmem),
        compiler_params=small,
        name="prepare",
    )(step_index, merge_dest, latents)
    return pl.pallas_call(
        finish_kernel,
        out_shape=(
            jax.ShapeDtypeStruct((videos, tokens, channels), f32),
            jax.ShapeDtypeStruct((videos, cap_half, channels), f32),
        ),
        in_specs=[vmem] * 6,
        out_specs=(vmem, vmem),
        compiler_params=small,
        name="finish",
    )(parts, *prepared, latents)


def solution(mesh):
    placed = (
        P(("jobs", "seq"), None),
        P(("jobs", "seq"), None),
        P(("jobs", "seq"), None),
        P("jobs", "seq"),
        P("jobs", "seq"),
        P("jobs", "seq", None),
        P("jobs"),
        P("jobs"),
        P(),
    )
    return jax.shard_map(
        run,
        mesh=mesh,
        in_specs=placed,
        out_specs=(P("jobs", "seq", None), P("jobs", "seq", None)),
        check_vma=False,
    )
```

time: 65.5 us -> 42.3 us (0.65)
  Pallas kernels: 29 us -> 6 us
  blocking collectives: 18.3 us -> 0 us
  starting transfers between devices: 9.06 us -> 20.6 us
  waiting for transfers between devices: 6.03 us -> 12.7 us
    pallas_call x4 -> x5, Pallas kernels: 29 us -> 6 us  [the longest x1 1.87 us: run(): pl.pallas_call(functools.partial(attend_kernel, score_scale=1.0 / math.sq...]
    psum x1 -> x0, blocking collectives: 18.3 us -> none  [local(): counts = lax.psum(jnp.where(seats == device, live_counts, 0), 'seq')]
    ppermute x0 -> x13, starting transfers between devices: none -> 15.8 us  [swap(): return lax.ppermute(part, 'seq', [(i, i ^ step) for i in range(groups)])]
    ppermute x0 -> x13, waiting for transfers between devices: none -> 6.83 us  [swap(): return lax.ppermute(part, 'seq', [(i, i ^ step) for i in range(groups)])]
    all_to_all x2 -> x1, starting transfers between devices: 9.06 us -> 4.84 us  [run(): lax.all_to_all(parts, 'seq', 0, 0, axis_index_groups=parities, tiled=True)]
    all_to_all x2 -> x1, waiting for transfers between devices: 6.03 us -> 5.86 us  [run(): lax.all_to_all(parts, 'seq', 0, 0, axis_index_groups=parities, tiled=True)]
  transfers between devices with their start and end apart: 2 -> 14, of which waited for: 1 -> 6; matrix products, arithmetic and copies ran while one was open for 0% -> 0% of each run, Pallas kernels for 0% -> 5%
where the time goes in v3:
time: 42.3 us; the launch traced here: 42 us
  starting transfers between devices  20.6 us (49%)
  waiting for transfers between devices  12.7 us (30%)
  Pallas kernels  6 us (14%)
  between operations  2.71 us (6%)
    ppermute x13, starting transfers between devices, swap(): return lax.ppermute(part, 'seq', [(i, i ^ step) for i in range(groups)])  15.8 us
    ppermute x13, waiting for transfers between devices, swap(): return lax.ppermute(part, 'seq', [(i, i ^ step) for i in range(groups)])  6.83 us
    all_to_all x1, waiting for transfers between devices, run(): lax.all_to_all(parts, 'seq', 0, 0, axis_index_groups=parities, tiled=True)  5.86 us
    all_to_all x1, starting transfers between devices, run(): lax.all_to_all(parts, 'seq', 0, 0, axis_index_groups=parities, tiled=True)  4.84 us
    pallas_call x1, Pallas kernels, run(): pl.pallas_call(functools.partial(attend_kernel, score_scale=1.0 / math.sq...  1.87 us
    pallas_call x1, Pallas kernels, run(): pl.pallas_call(functools.partial(note_kernel, steps=steps, width=width),...  1.84 us
    pallas_call x1, Pallas kernels, run(): pl.pallas_call(functools.partial(pack_kernel, steps=steps), out_shape=[kv...  1.33 us
  transfers between devices with their start and end apart: 14, of which 6 were waited for; matrix products, arithmetic and copies ran while one was open for 0% of the time, Pallas kernels for 5%

profile of v3, /device:TPU:0, one launch (start us, length us, event | category | flops | bytes accessed | tf_op | source)
XLA Modules:
  0.0 42.0 jit_solution(652878729600994324)
XLA Ops:
  0.6 1.3 %pack.1 = (bf16[64,1024]{1,0:T(8,128)(2,1)S(1)}, bf16[64,1024]{1,0:T(8,128)(2,1)S(1)}, bf16[64,1024]{1,0:T(8,128)(2,1)S(1)}, bf16[64,1024]{1,0:T(8,128)(2,1)S(1)...) custom-call(s32[1]{0:T(128)} %bitcast.device_ref, ...), custom_call_target="tpu_custom_call" | custom-call | tf_op jit(solution)/shard_map/pack/pallas_call | solution.py:226
  2.0 4.1 %collective-permute-start.3 = (bf16[64,1024]{1,0:T(8,128)(2,1)S(1)}, bf16[64,1024]{1,0:T(8,128)(2,1)S(1)}, u32[]{:S(2)}, u32[]{:S(2)}) collective-permute-start(bf16[64,1024]{1,0:T(8,128)(2,1)S(1)} %get-tuple-element.23), channel_id=1, source_target_pairs={{0,6},{1,7},{2,4},{3,5},{4,2},{5,3},{6,0},{7,1},{8,14},{9,15},{10,... | collective-permute-start | bytes 393224 | tf_op jit(solution)/shard_map/ppermute | solution.py:218
  6.1 0.5 %collective-permute-start.4 = (bf16[64,1024]{1,0:T(8,128)(2,1)S(1)}, bf16[64,1024]{1,0:T(8,128)(2,1)S(1)}, u32[]{:S(2)}, u32[]{:S(2)}) collective-permute-start(bf16[64,1024]{1,0:T(8,128)(2,1)S(1)} %get-tuple-element.24), channel_id=1, source_target_pairs={{0,2},{1,3},{2,0},{3,1},{4,6},{5,7},{6,4},{7,5},{8,10},{9,11},{10,... | collective-permute-start | bytes 393224 | tf_op jit(solution)/shard_map/ppermute | solution.py:218
  6.6 0.1 collective-permute-start.5
  6.7 2.9 %collective-permute-start = (s32[1,1]{1,0:T(1,128)}, s32[1,1]{1,0:T(1,128)}, u32[]{:S(2)}, u32[]{:S(2)}) collective-permute-start(s32[1,1]{1,0:T(1,128)} %param.12), channel_id=1, source_target_pairs={{0,8},{1,9},{2,10},{3,11},{4,12},{5,13},{6,14},{7,15},{8,0},{9,1},... | collective-permute-start | bytes 20 | tf_op jit(solution)/shard_map/ppermute | solution.py:218
  9.6 0.0 collective-permute-start.1
  10.3 1.4 %collective-permute-done.other_ref = s32[1,1]{1,0:T(1,128)} collective-permute-done((s32[1,1]{1,0:T(1,128)}, s32[1,1]{1,0:T(1,128)}, u32[]{:S(2)}, u32[]{:S(2)}) %collective-permute-start) | collective-permute-done | bytes 36 | tf_op jit(solution)/shard_map/ppermute | solution.py:218
  11.7 0.0 collective-permute-start.2
  11.7 0.0 collective-permute-done.1.mate_own_ref
  11.7 1.3 %collective-permute-done.2.mate_other_ref = s32[1,1]{1,0:T(1,128)} collective-permute-done((s32[1,1]{1,0:T(1,128)}, s32[1,1]{1,0:T(1,128)}, u32[]{:S(2)}, u32[]{:S(2)}) %collective-permute-start.2) | collective-permute-done | bytes 36 | tf_op jit(solution)/shard_map/ppermute | solution.py:218
  13.1 1.8 %note.1 = (bf16[40,1024]{1,0:T(8,128)(2,1)S(1)}, bf16[40,1024]{1,0:T(8,128)(2,1)S(1)}, bf16[40,1024]{1,0:T(8,128)(2,1)S(1)}, bf16[8,128]{1,0:T(8,128)(2,1)S(1)}) custom-call(s32[1]{0:T(128)} %bitcast.device_ref, s32[1,1]{1,0:T(1,128)S(6)} %copy.17.own_ref, ...), custom_call_target="tpu_custom_call", output_to_operand_aliasing={{0}: (5, {}), {1}: (6, {}), {2}: (7, {})} | custom-call | tf_op jit(solution)/shard_map/note/pallas_call | solution.py:239
  14.9 3.5 %collective-permute-start.10 = (bf16[40,1024]{1,0:T(8,128)(2,1)S(1)}, bf16[40,1024]{1,0:T(8,128)(2,1)S(1)}, u32[]{:S(2)}, u32[]{:S(2)}) collective-permute-start(bf16[40,1024]{1,0:T(8,128)(2,1)S(1)} %get-tuple-element.27), channel_id=1, source_target_pairs={{0,6},{1,7},{2,4},{3,5},{4,2},{5,3},{6,0},{7,1},{8,14},{9,15},{10,... | collective-permute-start | bytes 245768 | tf_op jit(solution)/shard_map/ppermute | solution.py:218
  18.4 1.5 %collective-permute-start.11 = (bf16[40,1024]{1,0:T(8,128)(2,1)S(1)}, bf16[40,1024]{1,0:T(8,128)(2,1)S(1)}, u32[]{:S(2)}, u32[]{:S(2)}) collective-permute-start(bf16[40,1024]{1,0:T(8,128)(2,1)S(1)} %get-tuple-element.28), channel_id=1, source_target_pairs={{0,2},{1,3},{2,0},{3,1},{4,6},{5,7},{6,4},{7,5},{8,10},{9,11},{10,... | collective-permute-start | bytes 245768 | tf_op jit(solution)/shard_map/ppermute | solution.py:218
  20.0 1.3 %collective-permute-done.10.refs_9_ = bf16[40,1024]{1,0:T(8,128)(2,1)S(1)} collective-permute-done((bf16[40,1024]{1,0:T(8,128)(2,1)S(1)}, bf16[40,1024]{1,0:T(8,128)(2,1)S(1)}, u32[]{:S(2)}, u32[]{:S(2)}) %collective-permute-start.10) | collective-permute-done | bytes 81952 | tf_op jit(solution)/shard_map/ppermute | solution.py:218
  21.3 0.0 collective-permute-start.6
  21.3 0.0 collective-permute-done.3.refs_1_
  21.3 0.5 %collective-permute-start.7 = (bf16[64,1024]{1,0:T(8,128)(2,1)S(1)}, bf16[64,1024]{1,0:T(8,128)(2,1)S(1)}, u32[]{:S(2)}, u32[]{:S(2)}) collective-permute-start(bf16[64,1024]{1,0:T(8,128)(2,1)S(1)} %collective-permute-done.3.refs_1_), channel_id=1, source_target_pairs={{0,1},{1,0},{2,3},{3,2},{4,5},{5,4},{6,7},{7,6},{8,9},{9,8},{10,11... | collective-permute-start | bytes 393224 | tf_op jit(solution)/shard_map/ppermute | solution.py:218
  21.8 0.0 collective-permute-done.4.refs_2_
  21.8 0.1 collective-permute-start.8
  21.9 0.0 collective-permute-done.5.refs_3_
  21.9 0.4 %collective-permute-start.9 = (bf16[64,1024]{1,0:T(8,128)(2,1)S(1)}, bf16[64,1024]{1,0:T(8,128)(2,1)S(1)}, u32[]{:S(2)}, u32[]{:S(2)}) collective-permute-start(bf16[64,1024]{1,0:T(8,128)(2,1)S(1)} %collective-permute-done.5.refs_3_), channel_id=1, source_target_pairs={{0,1},{1,0},{2,3},{3,2},{4,5},{5,4},{6,7},{7,6},{8,9},{9,8},{10,11... | collective-permute-start | bytes 393224 | tf_op jit(solution)/shard_map/ppermute | solution.py:218
  22.3 0.7 %collective-permute-done.11.refs_10_ = bf16[40,1024]{1,0:T(8,128)(2,1)S(1)} collective-permute-done((bf16[40,1024]{1,0:T(8,128)(2,1)S(1)}, bf16[40,1024]{1,0:T(8,128)(2,1)S(1)}, u32[]{:S(2)}, u32[]{:S(2)}) %collective-permute-start.11) | collective-permute-done | bytes 81952 | tf_op jit(solution)/shard_map/ppermute | solution.py:218
  23.0 2.1 %collective-permute-start.12 = (bf16[40,1024]{1,0:T(8,128)(2,1)S(1)}, bf16[40,1024]{1,0:T(8,128)(2,1)S(1)}, u32[]{:S(2)}, u32[]{:S(2)}) collective-permute-start(bf16[40,1024]{1,0:T(8,128)(2,1)S(1)} %get-tuple-element.29), channel_id=1, source_target_pairs={{0,4},{1,5},{2,6},{3,7},{4,0},{5,1},{6,2},{7,3},{8,12},{9,13},{10,... | collective-permute-start | bytes 245768 | tf_op jit(solution)/shard_map/ppermute | solution.py:218
  25.7 2.0 %collective-permute-done.12.refs_11_ = bf16[40,1024]{1,0:T(8,128)(2,1)S(1)} collective-permute-done((bf16[40,1024]{1,0:T(8,128)(2,1)S(1)}, bf16[40,1024]{1,0:T(8,128)(2,1)S(1)}, u32[]{:S(2)}, u32[]{:S(2)}) %collective-permute-start.12) | collective-permute-done | bytes 81952 | tf_op jit(solution)/shard_map/ppermute | solution.py:218
  27.7 0.0 collective-permute-done.6.refs_4_
  27.7 0.0 collective-permute-done.7.refs_5_
  27.8 0.0 collective-permute-done.8.refs_6_
  27.8 1.9 %attend.1 = f32[2,4,1,8,128]{4,3,2,1,0:T(8,128)} custom-call(s32[1]{0:T(128)} %bitcast.device_ref, f32[1]{0:T(128)S(6)} %copy.18.guidance_ref, bf16[64,4096]{1,0:T(8,128)(2,1)S(1)} %bitcast.3, bf16[8,128]{1,0:T(8,128)(2,1)S(1)} %get-tuple-element.21.home_ref, bf16[64,1024]{1,0:T(8,128)(2,1)S(1)} %get-tuple-element.22.refs_0_, ...), custom_call_target="tpu_custom_call" | custom-call | tf_op jit(solution)/shard_map/attend/pallas_call | solution.py:250
  29.7 4.8 %all-to-all-start = ((f32[8,1,8,128]{3,2,1,0:T(8,128)}), f32[8,1,8,128]{3,2,1,0:T(8,128)S(1)}, u32[]{:S(2)}, u32[]{:S(2)}) async-start(f32[8,1,8,128]{3,2,1,0:T(8,128)} %bitcast.2), calls=%async_computation | async-start | bytes 65536 | tf_op jit(solution)/shard_map/all_to_all | solution.py:260
  35.2 0.1 prepare.1
  35.3 5.9 %all-to-all-done.parts_ref = f32[8,1,8,128]{3,2,1,0:T(8,128)S(1)} async-done(((f32[8,1,8,128]{3,2,1,0:T(8,128)}), f32[8,1,8,128]{3,2,1,0:T(8,128)S(1)}, u32[]{:S(2)}, u32[]{:S(2)}) %all-to-all-start) | async-done | bytes 32800 | tf_op jit(solution)/shard_map/all_to_all | solution.py:260
  41.2 0.8 %finish.1 = (f32[1,64,64]{2,1,0:T(8,128)}, f32[1,16,64]{2,1,0:T(8,128)}) custom-call(f32[8,1,8,128]{3,2,1,0:T(8,128)S(1)} %all-to-all-done.parts_ref, bf16[1,64,48]{2,1,0:T(8,128)(2,1)S(1)} %get-tuple-element.30.spread_ref, f32[1,16,64]{2,1,0:T(8,128)S(1)} %get-tuple-element.31.means_ref, f32[1,16,64]{2,1,0:T(8,128)S(1)} %get-tuple-element.32.gains_ref, ...), custom_call_target="tpu_custom_call" | custom-call | tf_op jit(solution)/shard_map/finish/pallas_call | solution.py:274
  (7 shorter events, 0.0 us)
Async XLA Ops:
  0.6 27.1 %copy-start = (bf16[4096,64]{0,1:T(8,128)(2,1)S(1)}, bf16[4096,64]{0,1:T(8,128)(2,1)}, u32[]{:S(2)}) copy-start(bf16[4096,64]{0,1:T(8,128)(2,1)} %param.17) | copy-start | bytes 1572868
  2.0 19.3 %collective-permute-start.3 = (bf16[64,1024]{1,0:T(8,128)(2,1)S(1)}, bf16[64,1024]{1,0:T(8,128)(2,1)S(1)}, u32[]{:S(2)}, u32[]{:S(2)}) collective-permute-start(bf16[64,1024]{1,0:T(8,128)(2,1)S(1)} %get-tuple-element.23), channel_id=1, source_target_pairs={{0,6},{1,7},{2,4},{3,5},{4,2},{5,3},{6,0},{7,1},{8,14},{9,15},{10,... | collective-permute-start | bytes 393224 | tf_op jit(solution)/shard_map/ppermute | solution.py:218
  6.1 15.7 %collective-permute-start.4 = (bf16[64,1024]{1,0:T(8,128)(2,1)S(1)}, bf16[64,1024]{1,0:T(8,128)(2,1)S(1)}, u32[]{:S(2)}, u32[]{:S(2)}) collective-permute-start(bf16[64,1024]{1,0:T(8,128)(2,1)S(1)} %get-tuple-element.24), channel_id=1, source_target_pairs={{0,2},{1,3},{2,0},{3,1},{4,6},{5,7},{6,4},{7,5},{8,10},{9,11},{10,... | collective-permute-start | bytes 393224 | tf_op jit(solution)/shard_map/ppermute | solution.py:218
  6.6 15.3 %collective-permute-start.5 = (bf16[64,1024]{1,0:T(8,128)(2,1)S(1)}, bf16[64,1024]{1,0:T(8,128)(2,1)S(1)}, u32[]{:S(2)}, u32[]{:S(2)}) collective-permute-start(bf16[64,1024]{1,0:T(8,128)(2,1)S(1)} %get-tuple-element.25), channel_id=1, source_target_pairs={{0,4},{1,5},{2,6},{3,7},{4,0},{5,1},{6,2},{7,3},{8,12},{9,13},{10,... | collective-permute-start | bytes 393224 | tf_op jit(solution)/shard_map/ppermute | solution.py:218
  6.7 5.0 %collective-permute-start = (s32[1,1]{1,0:T(1,128)}, s32[1,1]{1,0:T(1,128)}, u32[]{:S(2)}, u32[]{:S(2)}) collective-permute-start(s32[1,1]{1,0:T(1,128)} %param.12), channel_id=1, source_target_pairs={{0,8},{1,9},{2,10},{3,11},{4,12},{5,13},{6,14},{7,15},{8,0},{9,1},... | collective-permute-start | bytes 20 | tf_op jit(solution)/shard_map/ppermute | solution.py:218
  9.6 2.1 %collective-permute-start.1 = (s32[1,1]{1,0:T(1,128)}, s32[1,1]{1,0:T(1,128)}, u32[]{:S(2)}, u32[]{:S(2)}) collective-permute-start(s32[1,1]{1,0:T(1,128)} %param.12), channel_id=1, source_target_pairs={{0,1},{1,0},{2,3},{3,2},{4,5},{5,4},{6,7},{7,6},{8,9},{9,8},{10,11... | collective-permute-start | bytes 20 | tf_op jit(solution)/shard_map/ppermute | solution.py:218
  11.7 1.4 %collective-permute-start.2 = (s32[1,1]{1,0:T(1,128)}, s32[1,1]{1,0:T(1,128)}, u32[]{:S(2)}, u32[]{:S(2)}) collective-permute-start(s32[1,1]{1,0:T(1,128)} %collective-permute-done.other_ref), channel_id=1, source_target_pairs={{0,1},{1,0},{2,3},{3,2},{4,5},{5,4},{6,7},{7,6},{8,9},{9,8},{10,11... | collective-permute-start | bytes 20 | tf_op jit(solution)/shard_map/ppermute | solution.py:218
  14.9 6.4 %collective-permute-start.10 = (bf16[40,1024]{1,0:T(8,128)(2,1)S(1)}, bf16[40,1024]{1,0:T(8,128)(2,1)S(1)}, u32[]{:S(2)}, u32[]{:S(2)}) collective-permute-start(bf16[40,1024]{1,0:T(8,128)(2,1)S(1)} %get-tuple-element.27), channel_id=1, source_target_pairs={{0,6},{1,7},{2,4},{3,5},{4,2},{5,3},{6,0},{7,1},{8,14},{9,15},{10,... | collective-permute-start | bytes 245768 | tf_op jit(solution)/shard_map/ppermute | solution.py:218
  18.4 4.6 %collective-permute-start.11 = (bf16[40,1024]{1,0:T(8,128)(2,1)S(1)}, bf16[40,1024]{1,0:T(8,128)(2,1)S(1)}, u32[]{:S(2)}, u32[]{:S(2)}) collective-permute-start(bf16[40,1024]{1,0:T(8,128)(2,1)S(1)} %get-tuple-element.28), channel_id=1, source_target_pairs={{0,2},{1,3},{2,0},{3,1},{4,6},{5,7},{6,4},{7,5},{8,10},{9,11},{10,... | collective-permute-start | bytes 245768 | tf_op jit(solution)/shard_map/ppermute | solution.py:218
  21.3 6.5 %collective-permute-start.6 = (bf16[64,1024]{1,0:T(8,128)(2,1)S(1)}, bf16[64,1024]{1,0:T(8,128)(2,1)S(1)}, u32[]{:S(2)}, u32[]{:S(2)}) collective-permute-start(bf16[64,1024]{1,0:T(8,128)(2,1)S(1)} %get-tuple-element.22.refs_0_), channel_id=1, source_target_pairs={{0,1},{1,0},{2,3},{3,2},{4,5},{5,4},{6,7},{7,6},{8,9},{9,8},{10,11... | collective-permute-start | bytes 393224 | tf_op jit(solution)/shard_map/ppermute | solution.py:218
  21.3 6.5 %collective-permute-start.7 = (bf16[64,1024]{1,0:T(8,128)(2,1)S(1)}, bf16[64,1024]{1,0:T(8,128)(2,1)S(1)}, u32[]{:S(2)}, u32[]{:S(2)}) collective-permute-start(bf16[64,1024]{1,0:T(8,128)(2,1)S(1)} %collective-permute-done.3.refs_1_), channel_id=1, source_target_pairs={{0,1},{1,0},{2,3},{3,2},{4,5},{5,4},{6,7},{7,6},{8,9},{9,8},{10,11... | collective-permute-start | bytes 393224 | tf_op jit(solution)/shard_map/ppermute | solution.py:218
  21.8 6.0 %collective-permute-start.8 = (bf16[64,1024]{1,0:T(8,128)(2,1)S(1)}, bf16[64,1024]{1,0:T(8,128)(2,1)S(1)}, u32[]{:S(2)}, u32[]{:S(2)}) collective-permute-start(bf16[64,1024]{1,0:T(8,128)(2,1)S(1)} %collective-permute-done.4.refs_2_), channel_id=1, source_target_pairs={{0,1},{1,0},{2,3},{3,2},{4,5},{5,4},{6,7},{7,6},{8,9},{9,8},{10,11... | collective-permute-start | bytes 393224 | tf_op jit(solution)/shard_map/ppermute | solution.py:218
  21.9 5.9 %collective-permute-start.9 = (bf16[64,1024]{1,0:T(8,128)(2,1)S(1)}, bf16[64,1024]{1,0:T(8,128)(2,1)S(1)}, u32[]{:S(2)}, u32[]{:S(2)}) collective-permute-start(bf16[64,1024]{1,0:T(8,128)(2,1)S(1)} %collective-permute-done.5.refs_3_), channel_id=1, source_target_pairs={{0,1},{1,0},{2,3},{3,2},{4,5},{5,4},{6,7},{7,6},{8,9},{9,8},{10,11... | collective-permute-start | bytes 393224 | tf_op jit(solution)/shard_map/ppermute | solution.py:218
  23.0 4.7 %collective-permute-start.12 = (bf16[40,1024]{1,0:T(8,128)(2,1)S(1)}, bf16[40,1024]{1,0:T(8,128)(2,1)S(1)}, u32[]{:S(2)}, u32[]{:S(2)}) collective-permute-start(bf16[40,1024]{1,0:T(8,128)(2,1)S(1)} %get-tuple-element.29), channel_id=1, source_target_pairs={{0,4},{1,5},{2,6},{3,7},{4,0},{5,1},{6,2},{7,3},{8,12},{9,13},{10,... | collective-permute-start | bytes 245768 | tf_op jit(solution)/shard_map/ppermute | solution.py:218
  29.6 5.5 %copy-start.1 = (f32[1,64,64]{2,1,0:T(8,128)S(1)}, f32[1,64,64]{2,1,0:T(8,128)}, u32[]{:S(2)}) copy-start(f32[1,64,64]{2,1,0:T(8,128)} %latents_ref.3) | copy-start | bytes 49156
  29.7 11.5 %all-to-all-start = ((f32[8,1,8,128]{3,2,1,0:T(8,128)}), f32[8,1,8,128]{3,2,1,0:T(8,128)S(1)}, u32[]{:S(2)}, u32[]{:S(2)}) async-start(f32[8,1,8,128]{3,2,1,0:T(8,128)} %bitcast.2), calls=%async_computation | async-start | bytes 65536 | tf_op jit(solution)/shard_map/all_to_all | solution.py:260
  34.5 0.7 %copy-start.2 = (s32[1,64]{1,0:T(1,128)S(1)}, s32[1,64]{1,0:T(1,128)}, u32[]{:S(2)}) copy-start(s32[1,64]{1,0:T(1,128)} %dest_ref.1) | copy-start | bytes 772

commit v4 on v3

--- a/solution.py
+++ b/solution.py
@@ -49,7 +49,11 @@
         copy.wait()
 
 
-def note_kernel(device_ref, own_ref, other_ref, mate_own_ref, mate_other_ref, *refs, steps, width):
+def live_count(dest_ref, video):
+    return jnp.max(dest_ref[pl.ds(video, 1), :], axis=1, keepdims=True) + 1
+
+
+def note_kernel(device_ref, own_ref, other_ref, mate_dest_ref, mate_other_ref, *refs, steps, width):
     count = len(steps)
     query_refs, out_refs, home_ref = refs[: count - 1], refs[count - 1 : -1], refs[-1]
     per_pair = query_refs[0].shape[1]
@@ -61,13 +65,13 @@
     note = None
     for place, step in enumerate(steps):
         if note is None or own_ref.shape[0] > 1:
-            video = (seat ^ step) // 2 * per_pair // width
+            video = (seat ^ step) // 2 * per_pair // width if own_ref.shape[0] > 1 else 0
             note = jnp.zeros((NOTE_ROWS, HD), jnp.int32)
             for line, (own, other) in enumerate(
-                ((own_ref, other_ref), (mate_own_ref, mate_other_ref))
+                ((own_ref, other_ref), (mate_dest_ref, mate_other_ref))
             ):
-                low = jnp.where(front, own[video, 0], other[video, 0])
-                high = jnp.where(front, other[video, 0], own[video, 0])
+                own, other = live_count(own, video), live_count(other, video)
+                low, high = jnp.where(front, own, other), jnp.where(front, other, own)
                 note = jnp.where(row == 2 * line, low, jnp.where(row == 2 * line + 1, high, note))
             note = note.astype(jnp.float32).astype(jnp.bfloat16)
         if place == 0:
@@ -219,7 +223,7 @@
 
     steps = steps_of(half)
     seat = device.reshape(1)
-    other_counts = swap(live_counts, half)
+    other_dest = swap(merge_dest, half)
     kv_shape = jax.ShapeDtypeStruct((2 * rows, per_pair), bf16)
     note_shape = jax.ShapeDtypeStruct((rows + NOTE_ROWS, per_pair), bf16)
     query_shapes = [jax.ShapeDtypeStruct((rows, per_pair), bf16)] + [note_shape] * (count - 1)
@@ -234,17 +238,24 @@
     )(seat, *(pltpu.with_memory_space_constraint(part, pltpu.HBM) for part in (queries, keys, values)))
     own, asked = packed[:count], packed[count:]
     held = [own[0]] + [swap(own[place], steps[place]) for place in range(1, count)]
-    mate_own = swap(live_counts, 1)
-    mate_other = swap(other_counts, 1)
+    mate_dest = swap(merge_dest, 1)
+    mate_other = swap(other_dest, 1)
     *noted, home = pl.pallas_call(
         functools.partial(note_kernel, steps=steps, width=width),
         out_shape=[note_shape] * (count - 1) + [jax.ShapeDtypeStruct((NOTE_ROWS, HD), bf16)],
-        in_specs=[smem] * 5 + [vmem] * (count - 1),
+        in_specs=[smem] + [vmem] * (count + 3),
         out_specs=[vmem] * count,
         input_output_aliases={5 + place: place for place in range(count - 1)},
         compiler_params=small,
         name="note",
-    )(seat, live_counts, other_counts, mate_own, mate_other, *asked[1:])
+    )(
+        seat,
+        *(
+            pltpu.with_memory_space_constraint(part, pltpu.VMEM)
+            for part in (merge_dest, other_dest, mate_dest, mate_other)
+        ),
+        *asked[1:],
+    )
     asked = [asked[0]] + [swap(noted[place - 1], steps[place]) for place in range(1, count)]
     lent = [swap(held[0], 1)] + [swap(held[place], 1) for place in range(1, count)]
     parts = pl.pallas_call(

time: 42.3 us -> 40.2 us (0.950)
  Pallas kernels: 6 us -> 4.33 us
  between operations: 2.71 us -> 2 us
  waiting for transfers between devices: 12.7 us -> 13.2 us
    pallas_call x1, Pallas kernels: 1.84 us -> 0.17 us  [run(): pl.pallas_call(functools.partial(note_kernel, steps=steps, width=width),...]
    ppermute x13, waiting for transfers between devices: 6.83 us -> 7.3 us  [swap(): return lax.ppermute(part, 'seq', [(i, i ^ step) for i in range(groups)])]
  transfers between devices with their start and end apart: 14 -> 14, of which waited for: 6 -> 6; matrix products, arithmetic and copies ran while one was open for 0% -> 0% of each run, Pallas kernels for 5% -> 1%
where the time goes in v4:
time: 40.2 us; the launch traced here: 39.9 us
  starting transfers between devices  20.4 us (51%)
  waiting for transfers between devices  13.2 us (33%)
  Pallas kernels  4.33 us (11%)
  between operations  2 us (5%)
    ppermute x13, starting transfers between devices, swap(): return lax.ppermute(part, 'seq', [(i, i ^ step) for i in range(groups)])  15.6 us
    ppermute x13, waiting for transfers between devices, swap(): return lax.ppermute(part, 'seq', [(i, i ^ step) for i in range(groups)])  7.3 us
    all_to_all x1, waiting for transfers between devices, run(): lax.all_to_all(parts, 'seq', 0, 0, axis_index_groups=parities, tiled=True)  5.88 us
    all_to_all x1, starting transfers between devices, run(): lax.all_to_all(parts, 'seq', 0, 0, axis_index_groups=parities, tiled=True)  4.71 us
    pallas_call x1, Pallas kernels, run(): pl.pallas_call(functools.partial(attend_kernel, score_scale=1.0 / math.sq...  1.87 us
    pallas_call x1, Pallas kernels, run(): pl.pallas_call(functools.partial(pack_kernel, steps=steps), out_shape=[kv...  1.33 us
    pallas_call x1, Pallas kernels, run(): pl.pallas_call(finish_kernel, out_shape=(jax.ShapeDtypeStruct((videos, to...  0.82 us
  transfers between devices with their start and end apart: 14, of which 6 were waited for; matrix products, arithmetic and copies ran while one was open for 0% of the time, Pallas kernels for 1%

profile of v4, /device:TPU:0, one launch (start us, length us, event | category | flops | bytes accessed | tf_op | source)
XLA Modules:
  0.0 39.9 jit_solution(2165771840465309949)
XLA Ops:
  0.6 1.3 %pack.1 = (bf16[64,1024]{1,0:T(8,128)(2,1)S(1)}, bf16[64,1024]{1,0:T(8,128)(2,1)S(1)}, bf16[64,1024]{1,0:T(8,128)(2,1)S(1)}, bf16[64,1024]{1,0:T(8,128)(2,1)S(1)...) custom-call(s32[1]{0:T(128)} %bitcast.device_ref, ...), custom_call_target="tpu_custom_call" | custom-call | tf_op jit(solution)/shard_map/pack/pallas_call | solution.py:230
  2.0 4.1 %collective-permute-start.3 = (bf16[64,1024]{1,0:T(8,128)(2,1)S(1)}, bf16[64,1024]{1,0:T(8,128)(2,1)S(1)}, u32[]{:S(2)}, u32[]{:S(2)}) collective-permute-start(bf16[64,1024]{1,0:T(8,128)(2,1)S(1)} %get-tuple-element.23), channel_id=1, source_target_pairs={{0,6},{1,7},{2,4},{3,5},{4,2},{5,3},{6,0},{7,1},{8,14},{9,15},{10,... | collective-permute-start | bytes 393224 | tf_op jit(solution)/shard_map/ppermute | solution.py:222
  6.1 0.5 %collective-permute-start.4 = (bf16[64,1024]{1,0:T(8,128)(2,1)S(1)}, bf16[64,1024]{1,0:T(8,128)(2,1)S(1)}, u32[]{:S(2)}, u32[]{:S(2)}) collective-permute-start(bf16[64,1024]{1,0:T(8,128)(2,1)S(1)} %get-tuple-element.24), channel_id=1, source_target_pairs={{0,2},{1,3},{2,0},{3,1},{4,6},{5,7},{6,4},{7,5},{8,10},{9,11},{10,... | collective-permute-start | bytes 393224 | tf_op jit(solution)/shard_map/ppermute | solution.py:222
  6.6 0.1 collective-permute-start.5
  6.7 2.9 %collective-permute-start = (s32[1,64]{1,0:T(1,128)S(1)}, s32[1,64]{1,0:T(1,128)S(1)}, u32[]{:S(2)}, u32[]{:S(2)}) collective-permute-start(s32[1,64]{1,0:T(1,128)S(1)} %copy-done.2), channel_id=1, source_target_pairs={{0,8},{1,9},{2,10},{3,11},{4,12},{5,13},{6,14},{7,15},{8,0},{9,1},... | collective-permute-start | bytes 776 | tf_op jit(solution)/shard_map/ppermute | solution.py:222
  9.6 0.0 collective-permute-start.1
  9.6 2.1 %collective-permute-done.other_ref = s32[1,64]{1,0:T(1,128)S(1)} collective-permute-done((s32[1,64]{1,0:T(1,128)S(1)}, s32[1,64]{1,0:T(1,128)S(1)}, u32[]{:S(2)}, u32[]{:S(2)}) %collective-permute-start) | collective-permute-done | bytes 288 | tf_op jit(solution)/shard_map/ppermute | solution.py:222
  11.7 0.0 collective-permute-start.2
  11.7 0.0 collective-permute-done.1.mate_dest_ref
  11.7 1.2 %collective-permute-done.2.mate_other_ref = s32[1,64]{1,0:T(1,128)S(1)} collective-permute-done((s32[1,64]{1,0:T(1,128)S(1)}, s32[1,64]{1,0:T(1,128)S(1)}, u32[]{:S(2)}, u32[]{:S(2)}) %collective-permute-start.2) | collective-permute-done | bytes 288 | tf_op jit(solution)/shard_map/ppermute | solution.py:222
  12.9 0.2 note.1
  13.0 3.4 %collective-permute-start.10 = (bf16[40,1024]{1,0:T(8,128)(2,1)S(1)}, bf16[40,1024]{1,0:T(8,128)(2,1)S(1)}, u32[]{:S(2)}, u32[]{:S(2)}) collective-permute-start(bf16[40,1024]{1,0:T(8,128)(2,1)S(1)} %get-tuple-element.27), channel_id=1, source_target_pairs={{0,6},{1,7},{2,4},{3,5},{4,2},{5,3},{6,0},{7,1},{8,14},{9,15},{10,... | collective-permute-start | bytes 245768 | tf_op jit(solution)/shard_map/ppermute | solution.py:222
  16.5 1.5 %collective-permute-start.11 = (bf16[40,1024]{1,0:T(8,128)(2,1)S(1)}, bf16[40,1024]{1,0:T(8,128)(2,1)S(1)}, u32[]{:S(2)}, u32[]{:S(2)}) collective-permute-start(bf16[40,1024]{1,0:T(8,128)(2,1)S(1)} %get-tuple-element.28), channel_id=1, source_target_pairs={{0,2},{1,3},{2,0},{3,1},{4,6},{5,7},{6,4},{7,5},{8,10},{9,11},{10,... | collective-permute-start | bytes 245768 | tf_op jit(solution)/shard_map/ppermute | solution.py:222
  18.0 1.3 %collective-permute-done.10.refs_9_ = bf16[40,1024]{1,0:T(8,128)(2,1)S(1)} collective-permute-done((bf16[40,1024]{1,0:T(8,128)(2,1)S(1)}, bf16[40,1024]{1,0:T(8,128)(2,1)S(1)}, u32[]{:S(2)}, u32[]{:S(2)}) %collective-permute-start.10) | collective-permute-done | bytes 81952 | tf_op jit(solution)/shard_map/ppermute | solution.py:222
  19.3 0.0 collective-permute-start.6
  19.3 0.0 collective-permute-done.3.refs_1_
  19.3 0.5 %collective-permute-start.7 = (bf16[64,1024]{1,0:T(8,128)(2,1)S(1)}, bf16[64,1024]{1,0:T(8,128)(2,1)S(1)}, u32[]{:S(2)}, u32[]{:S(2)}) collective-permute-start(bf16[64,1024]{1,0:T(8,128)(2,1)S(1)} %collective-permute-done.3.refs_1_), channel_id=1, source_target_pairs={{0,1},{1,0},{2,3},{3,2},{4,5},{5,4},{6,7},{7,6},{8,9},{9,8},{10,11... | collective-permute-start | bytes 393224 | tf_op jit(solution)/shard_map/ppermute | solution.py:222
  19.8 0.0 collective-permute-done.4.refs_2_
  19.8 0.1 collective-permute-start.8
  19.9 0.0 collective-permute-done.5.refs_3_
  19.9 0.4 %collective-permute-start.9 = (bf16[64,1024]{1,0:T(8,128)(2,1)S(1)}, bf16[64,1024]{1,0:T(8,128)(2,1)S(1)}, u32[]{:S(2)}, u32[]{:S(2)}) collective-permute-start(bf16[64,1024]{1,0:T(8,128)(2,1)S(1)} %collective-permute-done.5.refs_3_), channel_id=1, source_target_pairs={{0,1},{1,0},{2,3},{3,2},{4,5},{5,4},{6,7},{7,6},{8,9},{9,8},{10,11... | collective-permute-start | bytes 393224 | tf_op jit(solution)/shard_map/ppermute | solution.py:222
  20.3 0.7 %collective-permute-done.11.refs_10_ = bf16[40,1024]{1,0:T(8,128)(2,1)S(1)} collective-permute-done((bf16[40,1024]{1,0:T(8,128)(2,1)S(1)}, bf16[40,1024]{1,0:T(8,128)(2,1)S(1)}, u32[]{:S(2)}, u32[]{:S(2)}) %collective-permute-start.11) | collective-permute-done | bytes 81952 | tf_op jit(solution)/shard_map/ppermute | solution.py:222
  21.0 2.1 %collective-permute-start.12 = (bf16[40,1024]{1,0:T(8,128)(2,1)S(1)}, bf16[40,1024]{1,0:T(8,128)(2,1)S(1)}, u32[]{:S(2)}, u32[]{:S(2)}) collective-permute-start(bf16[40,1024]{1,0:T(8,128)(2,1)S(1)} %get-tuple-element.29), channel_id=1, source_target_pairs={{0,4},{1,5},{2,6},{3,7},{4,0},{5,1},{6,2},{7,3},{8,12},{9,13},{10,... | collective-permute-start | bytes 245768 | tf_op jit(solution)/shard_map/ppermute | solution.py:222
  23.7 2.0 %collective-permute-done.12.refs_11_ = bf16[40,1024]{1,0:T(8,128)(2,1)S(1)} collective-permute-done((bf16[40,1024]{1,0:T(8,128)(2,1)S(1)}, bf16[40,1024]{1,0:T(8,128)(2,1)S(1)}, u32[]{:S(2)}, u32[]{:S(2)}) %collective-permute-start.12) | collective-permute-done | bytes 81952 | tf_op jit(solution)/shard_map/ppermute | solution.py:222
  25.8 0.0 collective-permute-done.6.refs_4_
  25.8 0.0 collective-permute-done.7.refs_5_
  25.8 0.0 collective-permute-done.8.refs_6_
  25.8 1.9 %attend.1 = f32[2,4,1,8,128]{4,3,2,1,0:T(8,128)} custom-call(s32[1]{0:T(128)} %bitcast.device_ref, f32[1]{0:T(128)S(6)} %copy.16.guidance_ref, bf16[64,4096]{1,0:T(8,128)(2,1)S(1)} %bitcast.3, bf16[8,128]{1,0:T(8,128)(2,1)S(1)} %get-tuple-element.21.home_ref, bf16[64,1024]{1,0:T(8,128)(2,1)S(1)} %get-tuple-element.22.refs_0_, ...), custom_call_target="tpu_custom_call" | custom-call | tf_op jit(solution)/shard_map/attend/pallas_call | solution.py:261
  27.7 4.7 %all-to-all-start = ((f32[8,1,8,128]{3,2,1,0:T(8,128)}), f32[8,1,8,128]{3,2,1,0:T(8,128)S(1)}, u32[]{:S(2)}, u32[]{:S(2)}) async-start(f32[8,1,8,128]{3,2,1,0:T(8,128)} %bitcast.2), calls=%async_computation | async-start | bytes 65536 | tf_op jit(solution)/shard_map/all_to_all | solution.py:271
  33.0 0.1 prepare.1
  33.2 5.9 %all-to-all-done.parts_ref = f32[8,1,8,128]{3,2,1,0:T(8,128)S(1)} async-done(((f32[8,1,8,128]{3,2,1,0:T(8,128)}), f32[8,1,8,128]{3,2,1,0:T(8,128)S(1)}, u32[]{:S(2)}, u32[]{:S(2)}) %all-to-all-start) | async-done | bytes 32800 | tf_op jit(solution)/shard_map/all_to_all | solution.py:271
  39.1 0.8 %finish.1 = (f32[1,64,64]{2,1,0:T(8,128)}, f32[1,16,64]{2,1,0:T(8,128)}) custom-call(f32[8,1,8,128]{3,2,1,0:T(8,128)S(1)} %all-to-all-done.parts_ref, bf16[1,64,48]{2,1,0:T(8,128)(2,1)S(1)} %get-tuple-element.30.spread_ref, f32[1,16,64]{2,1,0:T(8,128)S(1)} %get-tuple-element.31.means_ref, f32[1,16,64]{2,1,0:T(8,128)S(1)} %get-tuple-element.32.gains_ref, ...), custom_call_target="tpu_custom_call" | custom-call | tf_op jit(solution)/shard_map/finish/pallas_call | solution.py:285
  (7 shorter events, 0.0 us)
Async XLA Ops:
  0.6 25.1 %copy-start = (bf16[4096,64]{0,1:T(8,128)(2,1)S(1)}, bf16[4096,64]{0,1:T(8,128)(2,1)}, u32[]{:S(2)}) copy-start(bf16[4096,64]{0,1:T(8,128)(2,1)} %param.16) | copy-start | bytes 1572868
  2.0 17.3 %collective-permute-start.3 = (bf16[64,1024]{1,0:T(8,128)(2,1)S(1)}, bf16[64,1024]{1,0:T(8,128)(2,1)S(1)}, u32[]{:S(2)}, u32[]{:S(2)}) collective-permute-start(bf16[64,1024]{1,0:T(8,128)(2,1)S(1)} %get-tuple-element.23), channel_id=1, source_target_pairs={{0,6},{1,7},{2,4},{3,5},{4,2},{5,3},{6,0},{7,1},{8,14},{9,15},{10,... | collective-permute-start | bytes 393224 | tf_op jit(solution)/shard_map/ppermute | solution.py:222
  6.1 0.7 %copy-start.2 = (s32[1,64]{1,0:T(1,128)S(1)}, s32[1,64]{1,0:T(1,128)}, u32[]{:S(2)}) copy-start(s32[1,64]{1,0:T(1,128)} %dest_ref.1) | copy-start | bytes 772
  6.1 13.7 %collective-permute-start.4 = (bf16[64,1024]{1,0:T(8,128)(2,1)S(1)}, bf16[64,1024]{1,0:T(8,128)(2,1)S(1)}, u32[]{:S(2)}, u32[]{:S(2)}) collective-permute-start(bf16[64,1024]{1,0:T(8,128)(2,1)S(1)} %get-tuple-element.24), channel_id=1, source_target_pairs={{0,2},{1,3},{2,0},{3,1},{4,6},{5,7},{6,4},{7,5},{8,10},{9,11},{10,... | collective-permute-start | bytes 393224 | tf_op jit(solution)/shard_map/ppermute | solution.py:222
  6.6 13.3 %collective-permute-start.5 = (bf16[64,1024]{1,0:T(8,128)(2,1)S(1)}, bf16[64,1024]{1,0:T(8,128)(2,1)S(1)}, u32[]{:S(2)}, u32[]{:S(2)}) collective-permute-start(bf16[64,1024]{1,0:T(8,128)(2,1)S(1)} %get-tuple-element.25), channel_id=1, source_target_pairs={{0,4},{1,5},{2,6},{3,7},{4,0},{5,1},{6,2},{7,3},{8,12},{9,13},{10,... | collective-permute-start | bytes 393224 | tf_op jit(solution)/shard_map/ppermute | solution.py:222
  6.7 5.0 %collective-permute-start = (s32[1,64]{1,0:T(1,128)S(1)}, s32[1,64]{1,0:T(1,128)S(1)}, u32[]{:S(2)}, u32[]{:S(2)}) collective-permute-start(s32[1,64]{1,0:T(1,128)S(1)} %copy-done.2), channel_id=1, source_target_pairs={{0,8},{1,9},{2,10},{3,11},{4,12},{5,13},{6,14},{7,15},{8,0},{9,1},... | collective-permute-start | bytes 776 | tf_op jit(solution)/shard_map/ppermute | solution.py:222
  9.6 2.1 %collective-permute-start.1 = (s32[1,64]{1,0:T(1,128)S(1)}, s32[1,64]{1,0:T(1,128)S(1)}, u32[]{:S(2)}, u32[]{:S(2)}) collective-permute-start(s32[1,64]{1,0:T(1,128)S(1)} %copy-done.2), channel_id=1, source_target_pairs={{0,1},{1,0},{2,3},{3,2},{4,5},{5,4},{6,7},{7,6},{8,9},{9,8},{10,11... | collective-permute-start | bytes 776 | tf_op jit(solution)/shard_map/ppermute | solution.py:222
  11.7 1.2 %collective-permute-start.2 = (s32[1,64]{1,0:T(1,128)S(1)}, s32[1,64]{1,0:T(1,128)S(1)}, u32[]{:S(2)}, u32[]{:S(2)}) collective-permute-start(s32[1,64]{1,0:T(1,128)S(1)} %collective-permute-done.other_ref), channel_id=1, source_target_pairs={{0,1},{1,0},{2,3},{3,2},{4,5},{5,4},{6,7},{7,6},{8,9},{9,8},{10,11... | collective-permute-start | bytes 776 | tf_op jit(solution)/shard_map/ppermute | solution.py:222
  13.0 6.2 %collective-permute-start.10 = (bf16[40,1024]{1,0:T(8,128)(2,1)S(1)}, bf16[40,1024]{1,0:T(8,128)(2,1)S(1)}, u32[]{:S(2)}, u32[]{:S(2)}) collective-permute-start(bf16[40,1024]{1,0:T(8,128)(2,1)S(1)} %get-tuple-element.27), channel_id=1, source_target_pairs={{0,6},{1,7},{2,4},{3,5},{4,2},{5,3},{6,0},{7,1},{8,14},{9,15},{10,... | collective-permute-start | bytes 245768 | tf_op jit(solution)/shard_map/ppermute | solution.py:222
  16.5 4.5 %collective-permute-start.11 = (bf16[40,1024]{1,0:T(8,128)(2,1)S(1)}, bf16[40,1024]{1,0:T(8,128)(2,1)S(1)}, u32[]{:S(2)}, u32[]{:S(2)}) collective-permute-start(bf16[40,1024]{1,0:T(8,128)(2,1)S(1)} %get-tuple-element.28), channel_id=1, source_target_pairs={{0,2},{1,3},{2,0},{3,1},{4,6},{5,7},{6,4},{7,5},{8,10},{9,11},{10,... | collective-permute-start | bytes 245768 | tf_op jit(solution)/shard_map/ppermute | solution.py:222
  19.3 6.5 %collective-permute-start.6 = (bf16[64,1024]{1,0:T(8,128)(2,1)S(1)}, bf16[64,1024]{1,0:T(8,128)(2,1)S(1)}, u32[]{:S(2)}, u32[]{:S(2)}) collective-permute-start(bf16[64,1024]{1,0:T(8,128)(2,1)S(1)} %get-tuple-element.22.refs_0_), channel_id=1, source_target_pairs={{0,1},{1,0},{2,3},{3,2},{4,5},{5,4},{6,7},{7,6},{8,9},{9,8},{10,11... | collective-permute-start | bytes 393224 | tf_op jit(solution)/shard_map/ppermute | solution.py:222
  19.3 6.5 %collective-permute-start.7 = (bf16[64,1024]{1,0:T(8,128)(2,1)S(1)}, bf16[64,1024]{1,0:T(8,128)(2,1)S(1)}, u32[]{:S(2)}, u32[]{:S(2)}) collective-permute-start(bf16[64,1024]{1,0:T(8,128)(2,1)S(1)} %collective-permute-done.3.refs_1_), channel_id=1, source_target_pairs={{0,1},{1,0},{2,3},{3,2},{4,5},{5,4},{6,7},{7,6},{8,9},{9,8},{10,11... | collective-permute-start | bytes 393224 | tf_op jit(solution)/shard_map/ppermute | solution.py:222
  19.8 6.0 %collective-permute-start.8 = (bf16[64,1024]{1,0:T(8,128)(2,1)S(1)}, bf16[64,1024]{1,0:T(8,128)(2,1)S(1)}, u32[]{:S(2)}, u32[]{:S(2)}) collective-permute-start(bf16[64,1024]{1,0:T(8,128)(2,1)S(1)} %collective-permute-done.4.refs_2_), channel_id=1, source_target_pairs={{0,1},{1,0},{2,3},{3,2},{4,5},{5,4},{6,7},{7,6},{8,9},{9,8},{10,11... | collective-permute-start | bytes 393224 | tf_op jit(solution)/shard_map/ppermute | solution.py:222
  19.9 5.9 %collective-permute-start.9 = (bf16[64,1024]{1,0:T(8,128)(2,1)S(1)}, bf16[64,1024]{1,0:T(8,128)(2,1)S(1)}, u32[]{:S(2)}, u32[]{:S(2)}) collective-permute-start(bf16[64,1024]{1,0:T(8,128)(2,1)S(1)} %collective-permute-done.5.refs_3_), channel_id=1, source_target_pairs={{0,1},{1,0},{2,3},{3,2},{4,5},{5,4},{6,7},{7,6},{8,9},{9,8},{10,11... | collective-permute-start | bytes 393224 | tf_op jit(solution)/shard_map/ppermute | solution.py:222
  21.0 4.7 %collective-permute-start.12 = (bf16[40,1024]{1,0:T(8,128)(2,1)S(1)}, bf16[40,1024]{1,0:T(8,128)(2,1)S(1)}, u32[]{:S(2)}, u32[]{:S(2)}) collective-permute-start(bf16[40,1024]{1,0:T(8,128)(2,1)S(1)} %get-tuple-element.29), channel_id=1, source_target_pairs={{0,4},{1,5},{2,6},{3,7},{4,0},{5,1},{6,2},{7,3},{8,12},{9,13},{10,... | collective-permute-start | bytes 245768 | tf_op jit(solution)/shard_map/ppermute | solution.py:222
  27.7 5.4 %copy-start.1 = (f32[1,64,64]{2,1,0:T(8,128)S(1)}, f32[1,64,64]{2,1,0:T(8,128)}, u32[]{:S(2)}) copy-start(f32[1,64,64]{2,1,0:T(8,128)} %latents_ref.3) | copy-start | bytes 49156
  27.7 11.4 %all-to-all-start = ((f32[8,1,8,128]{3,2,1,0:T(8,128)}), f32[8,1,8,128]{3,2,1,0:T(8,128)S(1)}, u32[]{:S(2)}, u32[]{:S(2)}) async-start(f32[8,1,8,128]{3,2,1,0:T(8,128)} %bitcast.2), calls=%async_computation | async-start | bytes 65536 | tf_op jit(solution)/shard_map/all_to_all | solution.py:271

commit v5 on v4

--- a/solution.py
+++ b/solution.py
@@ -11,6 +11,7 @@
 
 HD = 128
 NOTE_ROWS = 8
+FOLD = 2
 TIMESTEPS = 1000
 STRIDE = 20
 
@@ -23,6 +24,15 @@
 def sigma_of(step_value):
     frac = 1.0 - step_value / TIMESTEPS
     return shift_value * frac / (1.0 + (shift_value - 1.0) * frac)
+
+
+def fetch(pieces, sems):
+    copies = []
+    for number, (source, target) in enumerate(pieces):
+        copies.append(pltpu.make_async_copy(source, target, sems.at[number]))
+        copies[-1].start()
+    for copy in copies:
+        copy.wait()
 
 
 def pack_kernel(device_ref, query_ref, key_ref, value_ref, *refs, steps):
@@ -31,32 +41,27 @@
     rows, columns = query_ref.shape
     per_pair = columns // count
     seat = lax.rem(device_ref[0], 2 * count)
-    copies = []
+    pieces = []
     for place, step in enumerate(steps):
-        start = pl.multiple_of((seat ^ step) // 2 * per_pair, HD)
-        targets = (
-            (key_ref, out_refs[place].at[pl.ds(0, rows), :]),
-            (value_ref, out_refs[place].at[pl.ds(rows, rows), :]),
-            (query_ref, out_refs[count + place].at[pl.ds(0, rows), :]),
-        )
-        for part, (source, target) in enumerate(targets):
-            copy = pltpu.make_async_copy(
-                source.at[:, pl.ds(start, per_pair)], target, sems.at[part, place]
-            )
-            copy.start()
-            copies.append(copy)
-    for copy in copies:
-        copy.wait()
+        start = (seat ^ step) // 2 * per_pair
+        span = pl.ds(pl.multiple_of(start, HD), per_pair)
+        pieces.append((key_ref.at[:, span], out_refs[place].at[pl.ds(0, rows), :]))
+        pieces.append((value_ref.at[:, span], out_refs[place].at[pl.ds(rows, rows), :]))
+        folded = per_pair // FOLD
+        for fold in range(FOLD):
+            span = pl.ds(pl.multiple_of(start + fold * folded, HD), folded)
+            target = out_refs[count + place].at[pl.ds(fold * rows, rows), :]
+            pieces.append((query_ref.at[:, span], target))
+    fetch(pieces, sems)
 
 
 def live_count(dest_ref, video):
     return jnp.max(dest_ref[pl.ds(video, 1), :], axis=1, keepdims=True) + 1
 
 
-def note_kernel(device_ref, own_ref, other_ref, mate_dest_ref, mate_other_ref, *refs, steps, width):
+def note_kernel(device_ref, own_ref, other_ref, mate_dest_ref, mate_other_ref, *refs, steps):
     count = len(steps)
     query_refs, out_refs, home_ref = refs[: count - 1], refs[count - 1 : -1], refs[-1]
-    per_pair = query_refs[0].shape[1]
     first = query_refs[0].shape[0] - NOTE_ROWS
     device = device_ref[0]
     seat = lax.rem(device, 2 * count)
@@ -65,7 +70,7 @@
     note = None
     for place, step in enumerate(steps):
         if note is None or own_ref.shape[0] > 1:
-            video = (seat ^ step) // 2 * per_pair // width if own_ref.shape[0] > 1 else 0
+            video = (seat ^ step) // 2 * own_ref.shape[0] // count if own_ref.shape[0] > 1 else 0
             note = jnp.zeros((NOTE_ROWS, HD), jnp.int32)
             for line, (own, other) in enumerate(
                 ((own_ref, other_ref), (mate_dest_ref, mate_other_ref))
@@ -77,13 +82,12 @@
         if place == 0:
             home_ref[...] = note
         else:
-            for column in range(0, per_pair, HD):
-                out_refs[place - 1][first : first + NOTE_ROWS, column : column + HD] = note
+            out_refs[place - 1][first : first + NOTE_ROWS, :HD] = note
 
 
 def attend_kernel(device_ref, guidance_ref, weight_ref, home_ref, *refs, score_scale, steps):
-    *pack_refs, out_ref = refs
     count = len(steps)
+    pack_refs, out_refs = refs[:-count], refs[-count:]
     own_refs, mate_refs = pack_refs[:count], pack_refs[count : 2 * count]
     query_refs = pack_refs[2 * count :]
     rows, per_pair = own_refs[0].shape[0] // 2, own_refs[0].shape[1]
@@ -94,17 +98,19 @@
     start = seat // 2 * per_pair
     video = start // width
     scale = guidance_ref[video]
-    factor = jnp.where(device < 2 * count, scale, 1.0 - scale)
+    front = device < 2 * count
+    factor = jnp.where(front, scale, 1.0 - scale)
     weight = weight_ref[:, pl.ds(pl.multiple_of(lax.rem(start, width), HD), per_pair)]
-    if out_ref.shape[2] > 1:
-        out_ref[...] = jnp.zeros_like(out_ref)
+    if out_refs[0].shape[1] > 1:
+        for out_ref in out_refs:
+            out_ref[...] = jnp.zeros_like(out_ref)
 
     slot = lax.broadcasted_iota(jnp.int32, (cap_half, HD), 0).astype(jnp.float32)
     masks = []
     for line in range(2):
         for place in range(count):
             if place:
-                note = query_refs[place][rows : rows + NOTE_ROWS, :HD]
+                note = query_refs[place][FOLD * rows :, :HD]
             else:
                 note = home_ref[...]
             note = note.astype(jnp.float32)
@@ -119,7 +125,13 @@
         attended = []
         for column in range(0, per_pair, HD):
             span = slice(column, column + HD)
-            query = jnp.concatenate([query_refs[place][:rows, span] for place in places])
+            fold, lane = divmod(column, per_pair // FOLD)
+            query = jnp.concatenate(
+                [
+                    query_refs[place][fold * rows : (fold + 1) * rows, lane : lane + HD]
+                    for place in places
+                ]
+            )
             key = jnp.concatenate([ref[:rows, span] for ref in sources])
             value = jnp.concatenate([ref[rows:, span] for ref in sources])
             scores = lax.dot_general(
@@ -144,8 +156,20 @@
         part = (total * factor).T.reshape(len(places), 2, 2, cap_half // 2, channels)
         part = jnp.concatenate([part[:, :, 0], part[:, :, 1]], axis=-1)
         for place in places:
-            for group in range(2):
-                out_ref[group, (seat ^ steps[place]) // 2, video] = part[place - first, group]
+            near, far = part[place - first, 0], part[place - first, 1]
+            near, far = jnp.where(front, near, far), jnp.where(front, far, near)
+            quad, line = steps[place] // 4, steps[place] // 2 % 2
+            out_refs[quad][line, video] = near
+            out_refs[count // 2 + quad][line, video] = far
+
+
+def gather_kernel(*refs):
+    *part_refs, kept_ref, sent_ref = refs
+    for line, out_ref in enumerate((kept_ref, sent_ref)):
+        terms = [ref[line] for ref in part_refs]
+        while len(terms) > 1:
+            terms = [sum(terms[i : i + 2]) for i in range(0, len(terms), 2)]
+        out_ref[...] = terms[0]
 
 
 def prepare_kernel(
@@ -175,11 +199,19 @@
 
 
 def finish_kernel(
-    parts_ref, spread_ref, means_ref, gains_ref, sigma_ref, latents_ref, denoised_ref, merged_ref
+    kept_ref,
+    came_ref,
+    spread_ref,
+    means_ref,
+    gains_ref,
+    sigma_ref,
+    latents_ref,
+    denoised_ref,
+    merged_ref,
 ):
     videos, _, channels = latents_ref.shape
     for video in range(videos):
-        lanes = jnp.sum(parts_ref[:, video], axis=0)
+        lanes = kept_ref[video] + came_ref[video]
         merged = jnp.concatenate([lanes[:, :channels], lanes[:, channels:]], axis=0)
         merged_ref[video] = means_ref[video] + gains_ref[video] * merged
         top = merged.astype(jnp.bfloat16)
@@ -208,7 +240,7 @@
     count = half // 2
     rows, columns = queries.shape
     videos = guidance.shape[0]
-    width, channels = out_weight.shape
+    _, channels = out_weight.shape
     per_pair = columns // count
     cap_half = rows // 2
     tokens = merge_dest.shape[1]
@@ -225,23 +257,25 @@
     seat = device.reshape(1)
     other_dest = swap(merge_dest, half)
     kv_shape = jax.ShapeDtypeStruct((2 * rows, per_pair), bf16)
-    note_shape = jax.ShapeDtypeStruct((rows + NOTE_ROWS, per_pair), bf16)
-    query_shapes = [jax.ShapeDtypeStruct((rows, per_pair), bf16)] + [note_shape] * (count - 1)
+    note_shape = jax.ShapeDtypeStruct((FOLD * rows + NOTE_ROWS, per_pair // FOLD), bf16)
+    query_shape = jax.ShapeDtypeStruct((FOLD * rows, per_pair // FOLD), bf16)
+    query_shapes = [query_shape] + [note_shape] * (count - 1)
+    sources = [pltpu.with_memory_space_constraint(part, pltpu.HBM) for part in (queries, keys, values)]
     packed = pl.pallas_call(
         functools.partial(pack_kernel, steps=steps),
         out_shape=[kv_shape] * count + query_shapes,
         in_specs=[smem, hbm, hbm, hbm],
         out_specs=[vmem] * (2 * count),
-        scratch_shapes=[pltpu.SemaphoreType.DMA((3, count))],
+        scratch_shapes=[pltpu.SemaphoreType.DMA((count * (2 + FOLD),))],
         compiler_params=small,
         name="pack",
-    )(seat, *(pltpu.with_memory_space_constraint(part, pltpu.HBM) for part in (queries, keys, values)))
+    )(seat, *sources)
     own, asked = packed[:count], packed[count:]
     held = [own[0]] + [swap(own[place], steps[place]) for place in range(1, count)]
     mate_dest = swap(merge_dest, 1)
     mate_other = swap(other_dest, 1)
     *noted, home = pl.pallas_call(
-        functools.partial(note_kernel, steps=steps, width=width),
+        functools.partial(note_kernel, steps=steps),
         out_shape=[note_shape] * (count - 1) + [jax.ShapeDtypeStruct((NOTE_ROWS, HD), bf16)],
         in_specs=[smem] + [vmem] * (count + 3),
         out_specs=[vmem] * count,
@@ -258,17 +292,25 @@
     )
     asked = [asked[0]] + [swap(noted[place - 1], steps[place]) for place in range(1, count)]
     lent = [swap(held[0], 1)] + [swap(held[place], 1) for place in range(1, count)]
+    part_shape = (videos, cap_half // 2, 2 * channels)
     parts = pl.pallas_call(
         functools.partial(attend_kernel, score_scale=1.0 / math.sqrt(HD), steps=steps),
-        out_shape=jax.ShapeDtypeStruct((2, count, videos, cap_half // 2, 2 * channels), f32),
-        in_specs=[smem, smem] + [vmem] * (2 + 3 * count),
-        out_specs=vmem,
+        out_shape=[jax.ShapeDtypeStruct((2, *part_shape), f32)] * count,
+        in_specs=[smem, smem] + [vmem] * (1 + 1 + 3 * count),
+        out_specs=[vmem] * count,
         compiler_params=large,
         name="attend",
     )(seat, guidance, out_weight.T, home, *held, *lent, *asked)
-    parts = parts.reshape(half, videos, cap_half // 2, 2 * channels)
-    parities = [list(range(parity, groups, 2)) for parity in range(2)]
-    parts = lax.all_to_all(parts, "seq", 0, 0, axis_index_groups=parities, tiled=True)
+    parts = [parts[0]] + [swap(parts[quad], 4 * quad) for quad in range(1, count)]
+    kept, sent = pl.pallas_call(
+        gather_kernel,
+        out_shape=[jax.ShapeDtypeStruct(part_shape, f32)] * 2,
+        in_specs=[vmem] * count,
+        out_specs=[vmem] * 2,
+        compiler_params=small,
+        name="gather",
+    )(*parts)
+    came = swap(sent, 2)
     prepared = pl.pallas_call(
         prepare_kernel,
         out_shape=(
@@ -288,11 +330,11 @@
             jax.ShapeDtypeStruct((videos, tokens, channels), f32),
             jax.ShapeDtypeStruct((videos, cap_half, channels), f32),
         ),
-        in_specs=[vmem] * 6,
+        in_specs=[vmem] * 7,
         out_specs=(vmem, vmem),
         compiler_params=small,
         name="finish",
-    )(parts, *prepared, latents)
+    )(kept, came, *prepared, latents)
 
 
 def solution(mesh):

time: 40.2 us -> 39.6 us (0.985)
  starting transfers between devices: 20.4 us -> 21.6 us
  waiting for transfers between devices: 13.2 us -> 12.1 us
  Pallas kernels: 4.33 us -> 3.71 us
    ppermute x13 -> x17, starting transfers between devices: 15.6 us -> 21.6 us  [swap(): return lax.ppermute(part, 'seq', [(i, i ^ step) for i in range(groups)])]
    all_to_all x1 -> x0, waiting for transfers between devices: 5.88 us -> none  [run(): lax.all_to_all(parts, 'seq', 0, 0, axis_index_groups=parities, tiled=True)]
    ppermute x13 -> x17, waiting for transfers between devices: 7.3 us -> 12.1 us  [swap(): return lax.ppermute(part, 'seq', [(i, i ^ step) for i in range(groups)])]
    all_to_all x1 -> x0, starting transfers between devices: 4.71 us -> none  [run(): lax.all_to_all(parts, 'seq', 0, 0, axis_index_groups=parities, tiled=True)]
    pallas_call x1, Pallas kernels: 1.87 us -> 1.24 us  [run(): pl.pallas_call(functools.partial(attend_kernel, score_scale=1.0 / math.sq...]
  transfers between devices with their start and end apart: 14 -> 17, of which waited for: 6 -> 8; matrix products, arithmetic and copies ran while one was open for 0% -> 0% of each run, Pallas kernels for 1% -> 1%
where the time goes in v5:
time: 39.6 us; the launch traced here: 39.5 us
  starting transfers between devices  21.6 us (55%)
  waiting for transfers between devices  12.1 us (31%)
  Pallas kernels  3.71 us (9%)
  between operations  2.02 us (5%)
    ppermute x17, starting transfers between devices, swap(): return lax.ppermute(part, 'seq', [(i, i ^ step) for i in range(groups)])  21.6 us
    ppermute x17, waiting for transfers between devices, swap(): return lax.ppermute(part, 'seq', [(i, i ^ step) for i in range(groups)])  12.1 us
    pallas_call x1, Pallas kernels, run(): pl.pallas_call(functools.partial(pack_kernel, steps=steps), out_shape=[kv...  1.34 us
    pallas_call x1, Pallas kernels, run(): pl.pallas_call(functools.partial(attend_kernel, score_scale=1.0 / math.sq...  1.24 us
    pallas_call x1, Pallas kernels, run(): pl.pallas_call(finish_kernel, out_shape=(jax.ShapeDtypeStruct((videos, to...  0.81 us
  transfers between devices with their start and end apart: 17, of which 8 were waited for; matrix products, arithmetic and copies ran while one was open for 0% of the time, Pallas kernels for 1%

profile of v5, /device:TPU:0, one launch (start us, length us, event | category | flops | bytes accessed | tf_op | source)
XLA Modules:
  0.0 39.5 jit_solution(18272175033694178260)
XLA Ops:
  0.6 1.3 %pack.1 = (bf16[64,1024]{1,0:T(8,128)(2,1)S(1)}, bf16[64,1024]{1,0:T(8,128)(2,1)S(1)}, bf16[64,1024]{1,0:T(8,128)(2,1)S(1)}, bf16[64,1024]{1,0:T(8,128)(2,1)S(1)...) custom-call(s32[1]{0:T(128)} %bitcast.device_ref, ...), custom_call_target="tpu_custom_call" | custom-call | tf_op jit(solution)/shard_map/pack/pallas_call | solution.py:264
  2.0 4.1 %collective-permute-start.3 = (bf16[64,1024]{1,0:T(8,128)(2,1)S(1)}, bf16[64,1024]{1,0:T(8,128)(2,1)S(1)}, u32[]{:S(2)}, u32[]{:S(2)}) collective-permute-start(bf16[64,1024]{1,0:T(8,128)(2,1)S(1)} %get-tuple-element.29), channel_id=1, source_target_pairs={{0,6},{1,7},{2,4},{3,5},{4,2},{5,3},{6,0},{7,1},{8,14},{9,15},{10,... | collective-permute-start | bytes 393224 | tf_op jit(solution)/shard_map/ppermute | solution.py:254
  6.1 0.5 %collective-permute-start.4 = (bf16[64,1024]{1,0:T(8,128)(2,1)S(1)}, bf16[64,1024]{1,0:T(8,128)(2,1)S(1)}, u32[]{:S(2)}, u32[]{:S(2)}) collective-permute-start(bf16[64,1024]{1,0:T(8,128)(2,1)S(1)} %get-tuple-element.30), channel_id=1, source_target_pairs={{0,2},{1,3},{2,0},{3,1},{4,6},{5,7},{6,4},{7,5},{8,10},{9,11},{10,... | collective-permute-start | bytes 393224 | tf_op jit(solution)/shard_map/ppermute | solution.py:254
  6.6 0.1 collective-permute-start.5
  6.7 2.9 %collective-permute-start = (s32[1,64]{1,0:T(1,128)S(1)}, s32[1,64]{1,0:T(1,128)S(1)}, u32[]{:S(2)}, u32[]{:S(2)}) collective-permute-start(s32[1,64]{1,0:T(1,128)S(1)} %copy-done.2), channel_id=1, source_target_pairs={{0,8},{1,9},{2,10},{3,11},{4,12},{5,13},{6,14},{7,15},{8,0},{9,1},... | collective-permute-start | bytes 776 | tf_op jit(solution)/shard_map/ppermute | solution.py:254
  9.6 0.0 collective-permute-start.1
  9.6 2.1 %collective-permute-done.other_ref = s32[1,64]{1,0:T(1,128)S(1)} collective-permute-done((s32[1,64]{1,0:T(1,128)S(1)}, s32[1,64]{1,0:T(1,128)S(1)}, u32[]{:S(2)}, u32[]{:S(2)}) %collective-permute-start) | collective-permute-done | bytes 288 | tf_op jit(solution)/shard_map/ppermute | solution.py:254
  11.7 0.0 collective-permute-done.1.mate_dest_ref
  11.7 1.2 %collective-permute-done.2.mate_other_ref = s32[1,64]{1,0:T(1,128)S(1)} collective-permute-done((s32[1,64]{1,0:T(1,128)S(1)}, s32[1,64]{1,0:T(1,128)S(1)}, u32[]{:S(2)}, u32[]{:S(2)}) %collective-permute-start.2) | collective-permute-done | bytes 288 | tf_op jit(solution)/shard_map/ppermute | solution.py:254
  12.9 0.2 note.1
  13.1 3.4 %collective-permute-start.10 = (bf16[72,512]{1,0:T(8,128)(2,1)S(1)}, bf16[72,512]{1,0:T(8,128)(2,1)S(1)}, u32[]{:S(2)}, u32[]{:S(2)}) collective-permute-start(bf16[72,512]{1,0:T(8,128)(2,1)S(1)} %get-tuple-element.33), channel_id=1, source_target_pairs={{0,6},{1,7},{2,4},{3,5},{4,2},{5,3},{6,0},{7,1},{8,14},{9,15},{10,... | collective-permute-start | bytes 221192 | tf_op jit(solution)/shard_map/ppermute | solution.py:254
  16.5 1.5 %collective-permute-start.11 = (bf16[72,512]{1,0:T(8,128)(2,1)S(1)}, bf16[72,512]{1,0:T(8,128)(2,1)S(1)}, u32[]{:S(2)}, u32[]{:S(2)}) collective-permute-start(bf16[72,512]{1,0:T(8,128)(2,1)S(1)} %get-tuple-element.34), channel_id=1, source_target_pairs={{0,2},{1,3},{2,0},{3,1},{4,6},{5,7},{6,4},{7,5},{8,10},{9,11},{10,... | collective-permute-start | bytes 221192 | tf_op jit(solution)/shard_map/ppermute | solution.py:254
  18.0 1.1 %collective-permute-done.10.refs_9_ = bf16[72,512]{1,0:T(8,128)(2,1)S(1)} collective-permute-done((bf16[72,512]{1,0:T(8,128)(2,1)S(1)}, bf16[72,512]{1,0:T(8,128)(2,1)S(1)}, u32[]{:S(2)}, u32[]{:S(2)}) %collective-permute-start.10) | collective-permute-done | bytes 73760 | tf_op jit(solution)/shard_map/ppermute | solution.py:254
  19.1 0.5 %collective-permute-start.7 = (bf16[64,1024]{1,0:T(8,128)(2,1)S(1)}, bf16[64,1024]{1,0:T(8,128)(2,1)S(1)}, u32[]{:S(2)}, u32[]{:S(2)}) collective-permute-start(bf16[64,1024]{1,0:T(8,128)(2,1)S(1)} %collective-permute-done.3.refs_1_), channel_id=1, source_target_pairs={{0,1},{1,0},{2,3},{3,2},{4,5},{5,4},{6,7},{7,6},{8,9},{9,8},{10,11... | collective-permute-start | bytes 393224 | tf_op jit(solution)/shard_map/ppermute | solution.py:254
  19.6 0.0 collective-permute-done.4.refs_2_
  19.6 0.1 collective-permute-start.8
  19.7 0.4 %collective-permute-start.9 = (bf16[64,1024]{1,0:T(8,128)(2,1)S(1)}, bf16[64,1024]{1,0:T(8,128)(2,1)S(1)}, u32[]{:S(2)}, u32[]{:S(2)}) collective-permute-start(bf16[64,1024]{1,0:T(8,128)(2,1)S(1)} %collective-permute-done.5.refs_3_), channel_id=1, source_target_pairs={{0,1},{1,0},{2,3},{3,2},{4,5},{5,4},{6,7},{7,6},{8,9},{9,8},{10,11... | collective-permute-start | bytes 393224 | tf_op jit(solution)/shard_map/ppermute | solution.py:254
  20.1 0.7 %collective-permute-done.11.refs_10_ = bf16[72,512]{1,0:T(8,128)(2,1)S(1)} collective-permute-done((bf16[72,512]{1,0:T(8,128)(2,1)S(1)}, bf16[72,512]{1,0:T(8,128)(2,1)S(1)}, u32[]{:S(2)}, u32[]{:S(2)}) %collective-permute-start.11) | collective-permute-done | bytes 73760 | tf_op jit(solution)/shard_map/ppermute | solution.py:254
  20.8 2.1 %collective-permute-start.12 = (bf16[72,512]{1,0:T(8,128)(2,1)S(1)}, bf16[72,512]{1,0:T(8,128)(2,1)S(1)}, u32[]{:S(2)}, u32[]{:S(2)}) collective-permute-start(bf16[72,512]{1,0:T(8,128)(2,1)S(1)} %get-tuple-element.35), channel_id=1, source_target_pairs={{0,4},{1,5},{2,6},{3,7},{4,0},{5,1},{6,2},{7,3},{8,12},{9,13},{10,... | collective-permute-start | bytes 221192 | tf_op jit(solution)/shard_map/ppermute | solution.py:254
  23.6 1.9 %collective-permute-done.12.refs_11_ = bf16[72,512]{1,0:T(8,128)(2,1)S(1)} collective-permute-done((bf16[72,512]{1,0:T(8,128)(2,1)S(1)}, bf16[72,512]{1,0:T(8,128)(2,1)S(1)}, u32[]{:S(2)}, u32[]{:S(2)}) %collective-permute-start.12) | collective-permute-done | bytes 73760 | tf_op jit(solution)/shard_map/ppermute | solution.py:254
  25.4 0.0 collective-permute-done.7.refs_5_
  25.5 1.2 %attend.1 = (f32[2,1,8,128]{3,2,1,0:T(8,128)S(1)}, f32[2,1,8,128]{3,2,1,0:T(8,128)S(1)}, f32[2,1,8,128]{3,2,1,0:T(8,128)S(1)}, f32[2,1,8,128]{3,2,1,0:T(8,128)S(1)}) custom-call(s32[1]{0:T(128)} %bitcast.device_ref, f32[1]{0:T(128)S(6)} %copy.16.guidance_ref, bf16[64,4096]{1,0:T(8,128)(2,1)S(1)} %bitcast.2, bf16[8,128]{1,0:T(8,128)(2,1)S(1)} %get-tuple-element.27.home_ref, ...), custom_call_target="tpu_custom_call" | custom-call | tf_op jit(solution)/shard_map/attend/pallas_call | solution.py:296
  26.7 0.0 copy-start.1
  26.7 1.9 %collective-permute-start.13 = (f32[2,1,8,128]{3,2,1,0:T(8,128)S(1)}, f32[2,1,8,128]{3,2,1,0:T(8,128)S(1)}, u32[]{:S(2)}, u32[]{:S(2)}) collective-permute-start(f32[2,1,8,128]{3,2,1,0:T(8,128)S(1)} %get-tuple-element.37), channel_id=1, source_target_pairs={{0,4},{1,5},{2,6},{3,7},{4,0},{5,1},{6,2},{7,3},{8,12},{9,13},{10,... | collective-permute-start | bytes 24584 | tf_op jit(solution)/shard_map/ppermute | solution.py:254
  28.6 1.0 %collective-permute-start.14 = (f32[2,1,8,128]{3,2,1,0:T(8,128)S(1)}, f32[2,1,8,128]{3,2,1,0:T(8,128)S(1)}, u32[]{:S(2)}, u32[]{:S(2)}) collective-permute-start(f32[2,1,8,128]{3,2,1,0:T(8,128)S(1)} %get-tuple-element.38), channel_id=1, source_target_pairs={{0,8},{1,9},{2,10},{3,11},{4,12},{5,13},{6,14},{7,15},{8,0},{9,1},... | collective-permute-start | bytes 24584 | tf_op jit(solution)/shard_map/ppermute | solution.py:254
  29.6 1.6 %collective-permute-start.15 = (f32[2,1,8,128]{3,2,1,0:T(8,128)S(1)}, f32[2,1,8,128]{3,2,1,0:T(8,128)S(1)}, u32[]{:S(2)}, u32[]{:S(2)}) collective-permute-start(f32[2,1,8,128]{3,2,1,0:T(8,128)S(1)} %get-tuple-element.39), channel_id=1, source_target_pairs={{0,12},{1,13},{2,14},{3,15},{4,8},{5,9},{6,10},{7,11},{8,4},{9,5},... | collective-permute-start | bytes 24584 | tf_op jit(solution)/shard_map/ppermute | solution.py:254
  31.2 2.0 %collective-permute-done.14.refs_2_ = f32[2,1,8,128]{3,2,1,0:T(8,128)S(1)} collective-permute-done((f32[2,1,8,128]{3,2,1,0:T(8,128)S(1)}, f32[2,1,8,128]{3,2,1,0:T(8,128)S(1)}, u32[]{:S(2)}, u32[]{:S(2)}) %collective-permute-start.14) | collective-permute-done | bytes 8224 | tf_op jit(solution)/shard_map/ppermute | solution.py:254
  33.2 1.9 %collective-permute-done.15.refs_3_ = f32[2,1,8,128]{3,2,1,0:T(8,128)S(1)} collective-permute-done((f32[2,1,8,128]{3,2,1,0:T(8,128)S(1)}, f32[2,1,8,128]{3,2,1,0:T(8,128)S(1)}, u32[]{:S(2)}, u32[]{:S(2)}) %collective-permute-start.15) | collective-permute-done | bytes 8224 | tf_op jit(solution)/shard_map/ppermute | solution.py:254
  35.1 1.5 %collective-permute-start.16 = (f32[1,8,128]{2,1,0:T(8,128)S(1)}, f32[1,8,128]{2,1,0:T(8,128)S(1)}, u32[]{:S(2)}, u32[]{:S(2)}) collective-permute-start(f32[1,8,128]{2,1,0:T(8,128)S(1)} %get-tuple-element.41), channel_id=1, source_target_pairs={{0,2},{1,3},{2,0},{3,1},{4,6},{5,7},{6,4},{7,5},{8,10},{9,11},{10,... | collective-permute-start | bytes 12296 | tf_op jit(solution)/shard_map/ppermute | solution.py:254
  37.2 0.1 prepare.1
  37.4 1.3 %collective-permute-done.16.came_ref = f32[1,8,128]{2,1,0:T(8,128)S(1)} collective-permute-done((f32[1,8,128]{2,1,0:T(8,128)S(1)}, f32[1,8,128]{2,1,0:T(8,128)S(1)}, u32[]{:S(2)}, u32[]{:S(2)}) %collective-permute-start.16) | collective-permute-done | bytes 4128 | tf_op jit(solution)/shard_map/ppermute | solution.py:254
  38.7 0.8 %finish.1 = (f32[1,64,64]{2,1,0:T(8,128)}, f32[1,16,64]{2,1,0:T(8,128)}) custom-call(f32[1,8,128]{2,1,0:T(8,128)S(1)} %get-tuple-element.40.kept_ref, f32[1,8,128]{2,1,0:T(8,128)S(1)} %collective-permute-done.16.came_ref, bf16[1,64,48]{2,1,0:T(8,128)(2,1)S(1)} %get-tuple-element.42.spread_ref, f32[1,16,64]{2,1,0:T(8,128)S(1)} %get-tuple-element.43.means_ref, ...), custom_call_target="tpu_custom_call" | custom-call | tf_op jit(solution)/shard_map/finish/pallas_call | solution.py:327
  (14 shorter events, 0.0 us)
Async XLA Ops:
  0.6 24.8 %copy-start = (bf16[4096,64]{0,1:T(8,128)(2,1)S(1)}, bf16[4096,64]{0,1:T(8,128)(2,1)}, u32[]{:S(2)}) copy-start(bf16[4096,64]{0,1:T(8,128)(2,1)} %param.16) | copy-start | bytes 1572868
  2.0 17.1 %collective-permute-start.3 = (bf16[64,1024]{1,0:T(8,128)(2,1)S(1)}, bf16[64,1024]{1,0:T(8,128)(2,1)S(1)}, u32[]{:S(2)}, u32[]{:S(2)}) collective-permute-start(bf16[64,1024]{1,0:T(8,128)(2,1)S(1)} %get-tuple-element.29), channel_id=1, source_target_pairs={{0,6},{1,7},{2,4},{3,5},{4,2},{5,3},{6,0},{7,1},{8,14},{9,15},{10,... | collective-permute-start | bytes 393224 | tf_op jit(solution)/shard_map/ppermute | solution.py:254
  6.1 0.7 %copy-start.2 = (s32[1,64]{1,0:T(1,128)S(1)}, s32[1,64]{1,0:T(1,128)}, u32[]{:S(2)}) copy-start(s32[1,64]{1,0:T(1,128)} %dest_ref.1) | copy-start | bytes 772
  6.1 13.6 %collective-permute-start.4 = (bf16[64,1024]{1,0:T(8,128)(2,1)S(1)}, bf16[64,1024]{1,0:T(8,128)(2,1)S(1)}, u32[]{:S(2)}, u32[]{:S(2)}) collective-permute-start(bf16[64,1024]{1,0:T(8,128)(2,1)S(1)} %get-tuple-element.30), channel_id=1, source_target_pairs={{0,2},{1,3},{2,0},{3,1},{4,6},{5,7},{6,4},{7,5},{8,10},{9,11},{10,... | collective-permute-start | bytes 393224 | tf_op jit(solution)/shard_map/ppermute | solution.py:254
  6.6 13.1 %collective-permute-start.5 = (bf16[64,1024]{1,0:T(8,128)(2,1)S(1)}, bf16[64,1024]{1,0:T(8,128)(2,1)S(1)}, u32[]{:S(2)}, u32[]{:S(2)}) collective-permute-start(bf16[64,1024]{1,0:T(8,128)(2,1)S(1)} %get-tuple-element.31), channel_id=1, source_target_pairs={{0,4},{1,5},{2,6},{3,7},{4,0},{5,1},{6,2},{7,3},{8,12},{9,13},{10,... | collective-permute-start | bytes 393224 | tf_op jit(solution)/shard_map/ppermute | solution.py:254
  6.7 5.0 %collective-permute-start = (s32[1,64]{1,0:T(1,128)S(1)}, s32[1,64]{1,0:T(1,128)S(1)}, u32[]{:S(2)}, u32[]{:S(2)}) collective-permute-start(s32[1,64]{1,0:T(1,128)S(1)} %copy-done.2), channel_id=1, source_target_pairs={{0,8},{1,9},{2,10},{3,11},{4,12},{5,13},{6,14},{7,15},{8,0},{9,1},... | collective-permute-start | bytes 776 | tf_op jit(solution)/shard_map/ppermute | solution.py:254
  9.6 2.1 %collective-permute-start.1 = (s32[1,64]{1,0:T(1,128)S(1)}, s32[1,64]{1,0:T(1,128)S(1)}, u32[]{:S(2)}, u32[]{:S(2)}) collective-permute-start(s32[1,64]{1,0:T(1,128)S(1)} %copy-done.2), channel_id=1, source_target_pairs={{0,1},{1,0},{2,3},{3,2},{4,5},{5,4},{6,7},{7,6},{8,9},{9,8},{10,11... | collective-permute-start | bytes 776 | tf_op jit(solution)/shard_map/ppermute | solution.py:254
  11.7 1.2 %collective-permute-start.2 = (s32[1,64]{1,0:T(1,128)S(1)}, s32[1,64]{1,0:T(1,128)S(1)}, u32[]{:S(2)}, u32[]{:S(2)}) collective-permute-start(s32[1,64]{1,0:T(1,128)S(1)} %collective-permute-done.other_ref), channel_id=1, source_target_pairs={{0,1},{1,0},{2,3},{3,2},{4,5},{5,4},{6,7},{7,6},{8,9},{9,8},{10,11... | collective-permute-start | bytes 776 | tf_op jit(solution)/shard_map/ppermute | solution.py:254
  13.1 6.0 %collective-permute-start.10 = (bf16[72,512]{1,0:T(8,128)(2,1)S(1)}, bf16[72,512]{1,0:T(8,128)(2,1)S(1)}, u32[]{:S(2)}, u32[]{:S(2)}) collective-permute-start(bf16[72,512]{1,0:T(8,128)(2,1)S(1)} %get-tuple-element.33), channel_id=1, source_target_pairs={{0,6},{1,7},{2,4},{3,5},{4,2},{5,3},{6,0},{7,1},{8,14},{9,15},{10,... | collective-permute-start | bytes 221192 | tf_op jit(solution)/shard_map/ppermute | solution.py:254
  16.5 4.4 %collective-permute-start.11 = (bf16[72,512]{1,0:T(8,128)(2,1)S(1)}, bf16[72,512]{1,0:T(8,128)(2,1)S(1)}, u32[]{:S(2)}, u32[]{:S(2)}) collective-permute-start(bf16[72,512]{1,0:T(8,128)(2,1)S(1)} %get-tuple-element.34), channel_id=1, source_target_pairs={{0,2},{1,3},{2,0},{3,1},{4,6},{5,7},{6,4},{7,5},{8,10},{9,11},{10,... | collective-permute-start | bytes 221192 | tf_op jit(solution)/shard_map/ppermute | solution.py:254
  19.1 6.3 %collective-permute-start.6 = (bf16[64,1024]{1,0:T(8,128)(2,1)S(1)}, bf16[64,1024]{1,0:T(8,128)(2,1)S(1)}, u32[]{:S(2)}, u32[]{:S(2)}) collective-permute-start(bf16[64,1024]{1,0:T(8,128)(2,1)S(1)} %get-tuple-element.28.refs_0_), channel_id=1, source_target_pairs={{0,1},{1,0},{2,3},{3,2},{4,5},{5,4},{6,7},{7,6},{8,9},{9,8},{10,11... | collective-permute-start | bytes 393224 | tf_op jit(solution)/shard_map/ppermute | solution.py:254
  19.1 6.3 %collective-permute-start.7 = (bf16[64,1024]{1,0:T(8,128)(2,1)S(1)}, bf16[64,1024]{1,0:T(8,128)(2,1)S(1)}, u32[]{:S(2)}, u32[]{:S(2)}) collective-permute-start(bf16[64,1024]{1,0:T(8,128)(2,1)S(1)} %collective-permute-done.3.refs_1_), channel_id=1, source_target_pairs={{0,1},{1,0},{2,3},{3,2},{4,5},{5,4},{6,7},{7,6},{8,9},{9,8},{10,11... | collective-permute-start | bytes 393224 | tf_op jit(solution)/shard_map/ppermute | solution.py:254
  19.6 5.8 %collective-permute-start.8 = (bf16[64,1024]{1,0:T(8,128)(2,1)S(1)}, bf16[64,1024]{1,0:T(8,128)(2,1)S(1)}, u32[]{:S(2)}, u32[]{:S(2)}) collective-permute-start(bf16[64,1024]{1,0:T(8,128)(2,1)S(1)} %collective-permute-done.4.refs_2_), channel_id=1, source_target_pairs={{0,1},{1,0},{2,3},{3,2},{4,5},{5,4},{6,7},{7,6},{8,9},{9,8},{10,11... | collective-permute-start | bytes 393224 | tf_op jit(solution)/shard_map/ppermute | solution.py:254
  19.7 5.7 %collective-permute-start.9 = (bf16[64,1024]{1,0:T(8,128)(2,1)S(1)}, bf16[64,1024]{1,0:T(8,128)(2,1)S(1)}, u32[]{:S(2)}, u32[]{:S(2)}) collective-permute-start(bf16[64,1024]{1,0:T(8,128)(2,1)S(1)} %collective-permute-done.5.refs_3_), channel_id=1, source_target_pairs={{0,1},{1,0},{2,3},{3,2},{4,5},{5,4},{6,7},{7,6},{8,9},{9,8},{10,11... | collective-permute-start | bytes 393224 | tf_op jit(solution)/shard_map/ppermute | solution.py:254
  20.8 4.6 %collective-permute-start.12 = (bf16[72,512]{1,0:T(8,128)(2,1)S(1)}, bf16[72,512]{1,0:T(8,128)(2,1)S(1)}, u32[]{:S(2)}, u32[]{:S(2)}) collective-permute-start(bf16[72,512]{1,0:T(8,128)(2,1)S(1)} %get-tuple-element.35), channel_id=1, source_target_pairs={{0,4},{1,5},{2,6},{3,7},{4,0},{5,1},{6,2},{7,3},{8,12},{9,13},{10,... | collective-permute-start | bytes 221192 | tf_op jit(solution)/shard_map/ppermute | solution.py:254
  26.7 10.5 %copy-start.1 = (f32[1,64,64]{2,1,0:T(8,128)S(1)}, f32[1,64,64]{2,1,0:T(8,128)}, u32[]{:S(2)}) copy-start(f32[1,64,64]{2,1,0:T(8,128)} %latents_ref.3) | copy-start | bytes 49156
  26.7 4.5 %collective-permute-start.13 = (f32[2,1,8,128]{3,2,1,0:T(8,128)S(1)}, f32[2,1,8,128]{3,2,1,0:T(8,128)S(1)}, u32[]{:S(2)}, u32[]{:S(2)}) collective-permute-start(f32[2,1,8,128]{3,2,1,0:T(8,128)S(1)} %get-tuple-element.37), channel_id=1, source_target_pairs={{0,4},{1,5},{2,6},{3,7},{4,0},{5,1},{6,2},{7,3},{8,12},{9,13},{10,... | collective-permute-start | bytes 24584 | tf_op jit(solution)/shard_map/ppermute | solution.py:254
  28.6 4.5 %collective-permute-start.14 = (f32[2,1,8,128]{3,2,1,0:T(8,128)S(1)}, f32[2,1,8,128]{3,2,1,0:T(8,128)S(1)}, u32[]{:S(2)}, u32[]{:S(2)}) collective-permute-start(f32[2,1,8,128]{3,2,1,0:T(8,128)S(1)} %get-tuple-element.38), channel_id=1, source_target_pairs={{0,8},{1,9},{2,10},{3,11},{4,12},{5,13},{6,14},{7,15},{8,0},{9,1},... | collective-permute-start | bytes 24584 | tf_op jit(solution)/shard_map/ppermute | solution.py:254
  29.6 5.4 %collective-permute-start.15 = (f32[2,1,8,128]{3,2,1,0:T(8,128)S(1)}, f32[2,1,8,128]{3,2,1,0:T(8,128)S(1)}, u32[]{:S(2)}, u32[]{:S(2)}) collective-permute-start(f32[2,1,8,128]{3,2,1,0:T(8,128)S(1)} %get-tuple-element.39), channel_id=1, source_target_pairs={{0,12},{1,13},{2,14},{3,15},{4,8},{5,9},{6,10},{7,11},{8,4},{9,5},... | collective-permute-start | bytes 24584 | tf_op jit(solution)/shard_map/ppermute | solution.py:254
  35.1 3.6 %collective-permute-start.16 = (f32[1,8,128]{2,1,0:T(8,128)S(1)}, f32[1,8,128]{2,1,0:T(8,128)S(1)}, u32[]{:S(2)}, u32[]{:S(2)}) collective-permute-start(f32[1,8,128]{2,1,0:T(8,128)S(1)} %get-tuple-element.41), channel_id=1, source_target_pairs={{0,2},{1,3},{2,0},{3,1},{4,6},{5,7},{6,4},{7,5},{8,10},{9,11},{10,... | collective-permute-start | bytes 12296 | tf_op jit(solution)/shard_map/ppermute | solution.py:254

commit v6 on v5

--- a/solution.py
+++ b/solution.py
@@ -107,15 +107,13 @@
 
     slot = lax.broadcasted_iota(jnp.int32, (cap_half, HD), 0).astype(jnp.float32)
     masks = []
-    for line in range(2):
+    for mate in range(2):
         for place in range(count):
-            if place:
-                note = query_refs[place][FOLD * rows :, :HD]
-            else:
-                note = home_ref[...]
+            note = query_refs[place][FOLD * rows :, :HD] if place else home_ref[...]
             note = note.astype(jnp.float32)
+            line = 2 * (mate if place == 0 else 1 - mate)
             for group in range(2):
-                live = note[2 * line + group : 2 * line + group + 1, :]
+                live = note[line + group : line + group + 1, :]
                 masks.append(jnp.where(slot < live, 0.0, neg_big))
     mask = jnp.concatenate(masks)
     sources = (*own_refs, *mate_refs)
@@ -290,7 +288,7 @@
         ),
         *asked[1:],
     )
-    asked = [asked[0]] + [swap(noted[place - 1], steps[place]) for place in range(1, count)]
+    asked = [swap(part, steps[place] ^ 1) for place, part in enumerate((asked[0], *noted))]
     lent = [swap(held[0], 1)] + [swap(held[place], 1) for place in range(1, count)]
     part_shape = (videos, cap_half // 2, 2 * channels)
     parts = pl.pallas_call(
@@ -301,7 +299,7 @@
         compiler_params=large,
         name="attend",
     )(seat, guidance, out_weight.T, home, *held, *lent, *asked)
-    parts = [parts[0]] + [swap(parts[quad], 4 * quad) for quad in range(1, count)]
+    parts = [swap(parts[quad], 4 * quad + 1) for quad in range(count)]
     kept, sent = pl.pallas_call(
         gather_kernel,
         out_shape=[jax.ShapeDtypeStruct(part_shape, f32)] * 2,

time: 39.6 us -> 40.3 us (1.018)
  waiting for transfers between devices: 12.1 us -> 15.3 us
  starting transfers between devices: 21.6 us -> 18.6 us
  local copies, waits for them, and re-layouts: 0.01 us -> 0.53 us
    ppermute x17 -> x19, waiting for transfers between devices: 12.1 us -> 15.3 us  [swap(): return lax.ppermute(part, 'seq', [(i, i ^ step) for i in range(groups)])]
    ppermute x17 -> x19, starting transfers between devices: 21.6 us -> 18.6 us  [swap(): return lax.ppermute(part, 'seq', [(i, i ^ step) for i in range(groups)])]
    unnamed x6, local copies, waits for them, and re-layouts: 0.01 us -> 0.53 us
  transfers between devices with their start and end apart: 17 -> 19, of which waited for: 8 -> 9; matrix products, arithmetic and copies ran while one was open for 0% -> 0% of each run, Pallas kernels for 1% -> 1%
where the time goes in v6:
time: 40.3 us; the launch traced here: 40.2 us
  starting transfers between devices  18.6 us (46%)
  waiting for transfers between devices  15.3 us (38%)
  Pallas kernels  3.71 us (9%)
  between operations  2.02 us (5%)
  local copies, waits for them, and re-layouts  0.53 us (1%)
    ppermute x19, starting transfers between devices, swap(): return lax.ppermute(part, 'seq', [(i, i ^ step) for i in range(groups)])  18.6 us
    ppermute x19, waiting for transfers between devices, swap(): return lax.ppermute(part, 'seq', [(i, i ^ step) for i in range(groups)])  15.3 us
    pallas_call x1, Pallas kernels, run(): pl.pallas_call(functools.partial(pack_kernel, steps=steps), out_shape=[kv...  1.34 us
    pallas_call x1, Pallas kernels, run(): pl.pallas_call(functools.partial(attend_kernel, score_scale=1.0 / math.sq...  1.24 us
    pallas_call x1, Pallas kernels, run(): pl.pallas_call(finish_kernel, out_shape=(jax.ShapeDtypeStruct((videos, to...  0.81 us
  transfers between devices with their start and end apart: 19, of which 9 were waited for; matrix products, arithmetic and copies ran while one was open for 0% of the time, Pallas kernels for 1%

profile of v6, /device:TPU:0, one launch (start us, length us, event | category | flops | bytes accessed | tf_op | source)
XLA Modules:
  0.0 40.2 jit_solution(15165133890903031847)
XLA Ops:
  0.6 1.3 %pack.1 = (bf16[64,1024]{1,0:T(8,128)(2,1)S(1)}, bf16[64,1024]{1,0:T(8,128)(2,1)S(1)}, bf16[64,1024]{1,0:T(8,128)(2,1)S(1)}, bf16[64,1024]{1,0:T(8,128)(2,1)S(1)...) custom-call(s32[1]{0:T(128)} %bitcast.device_ref, ...), custom_call_target="tpu_custom_call" | custom-call | tf_op jit(solution)/shard_map/pack/pallas_call | solution.py:262
  2.0 4.1 %collective-permute-start.3 = (bf16[64,1024]{1,0:T(8,128)(2,1)S(1)}, bf16[64,1024]{1,0:T(8,128)(2,1)S(1)}, u32[]{:S(2)}, u32[]{:S(2)}) collective-permute-start(bf16[64,1024]{1,0:T(8,128)(2,1)S(1)} %get-tuple-element.29), channel_id=1, source_target_pairs={{0,6},{1,7},{2,4},{3,5},{4,2},{5,3},{6,0},{7,1},{8,14},{9,15},{10,... | collective-permute-start | bytes 393224 | tf_op jit(solution)/shard_map/ppermute | solution.py:252
  6.1 0.5 %collective-permute-start.4 = (bf16[64,1024]{1,0:T(8,128)(2,1)S(1)}, bf16[64,1024]{1,0:T(8,128)(2,1)S(1)}, u32[]{:S(2)}, u32[]{:S(2)}) collective-permute-start(bf16[64,1024]{1,0:T(8,128)(2,1)S(1)} %get-tuple-element.30), channel_id=1, source_target_pairs={{0,2},{1,3},{2,0},{3,1},{4,6},{5,7},{6,4},{7,5},{8,10},{9,11},{10,... | collective-permute-start | bytes 393224 | tf_op jit(solution)/shard_map/ppermute | solution.py:252
  6.6 0.1 collective-permute-start.5
  6.7 0.5 %copy-done.2 = s32[1,64]{1,0:T(1,128)S(1)} copy-done((s32[1,64]{1,0:T(1,128)S(1)}, s32[1,64]{1,0:T(1,128)}, u32[]{:S(2)}) %copy-start.2) | copy-done | bytes 280
  7.2 0.0 collective-permute-start.1
  7.2 1.2 %collective-permute-done.1.mate_dest_ref = s32[1,64]{1,0:T(1,128)S(1)} collective-permute-done((s32[1,64]{1,0:T(1,128)S(1)}, s32[1,64]{1,0:T(1,128)S(1)}, u32[]{:S(2)}, u32[]{:S(2)}) %collective-permute-start.1) | collective-permute-done | bytes 288 | tf_op jit(solution)/shard_map/ppermute | solution.py:252
  8.4 2.6 %collective-permute-start = (s32[1,64]{1,0:T(1,128)S(1)}, s32[1,64]{1,0:T(1,128)S(1)}, u32[]{:S(2)}, u32[]{:S(2)}) collective-permute-start(s32[1,64]{1,0:T(1,128)S(1)} %copy-done.2), channel_id=1, source_target_pairs={{0,8},{1,9},{2,10},{3,11},{4,12},{5,13},{6,14},{7,15},{8,0},{9,1},... | collective-permute-start | bytes 776 | tf_op jit(solution)/shard_map/ppermute | solution.py:252
  11.0 1.9 %collective-permute-done.other_ref = s32[1,64]{1,0:T(1,128)S(1)} collective-permute-done((s32[1,64]{1,0:T(1,128)S(1)}, s32[1,64]{1,0:T(1,128)S(1)}, u32[]{:S(2)}, u32[]{:S(2)}) %collective-permute-start) | collective-permute-done | bytes 288 | tf_op jit(solution)/shard_map/ppermute | solution.py:252
  12.9 1.2 %collective-permute-done.2.mate_other_ref = s32[1,64]{1,0:T(1,128)S(1)} collective-permute-done((s32[1,64]{1,0:T(1,128)S(1)}, s32[1,64]{1,0:T(1,128)S(1)}, u32[]{:S(2)}, u32[]{:S(2)}) %collective-permute-start.2) | collective-permute-done | bytes 288 | tf_op jit(solution)/shard_map/ppermute | solution.py:252
  14.0 0.2 note.1
  14.2 2.3 %collective-permute-start.11 = (bf16[72,512]{1,0:T(8,128)(2,1)S(1)}, bf16[72,512]{1,0:T(8,128)(2,1)S(1)}, u32[]{:S(2)}, u32[]{:S(2)}) collective-permute-start(bf16[72,512]{1,0:T(8,128)(2,1)S(1)} %get-tuple-element.33), channel_id=1, source_target_pairs={{0,7},{1,6},{2,5},{3,4},{4,3},{5,2},{6,1},{7,0},{8,15},{9,14},{10,... | collective-permute-start | bytes 221192 | tf_op jit(solution)/shard_map/ppermute | solution.py:252
  16.5 1.2 %collective-permute-start.12 = (bf16[72,512]{1,0:T(8,128)(2,1)S(1)}, bf16[72,512]{1,0:T(8,128)(2,1)S(1)}, u32[]{:S(2)}, u32[]{:S(2)}) collective-permute-start(bf16[72,512]{1,0:T(8,128)(2,1)S(1)} %get-tuple-element.34), channel_id=1, source_target_pairs={{0,3},{1,2},{2,1},{3,0},{4,7},{5,6},{6,5},{7,4},{8,11},{9,10},{10,... | collective-permute-start | bytes 221192 | tf_op jit(solution)/shard_map/ppermute | solution.py:252
  17.7 1.7 %collective-permute-done.11.refs_9_ = bf16[72,512]{1,0:T(8,128)(2,1)S(1)} collective-permute-done((bf16[72,512]{1,0:T(8,128)(2,1)S(1)}, bf16[72,512]{1,0:T(8,128)(2,1)S(1)}, u32[]{:S(2)}, u32[]{:S(2)}) %collective-permute-start.11) | collective-permute-done | bytes 73760 | tf_op jit(solution)/shard_map/ppermute | solution.py:252
  19.4 0.2 collective-permute-start.6
  19.6 0.3 collective-permute-start.7
  19.9 0.2 collective-permute-start.8
  20.1 0.3 collective-permute-start.9
  20.4 0.6 %collective-permute-done.12.refs_10_ = bf16[72,512]{1,0:T(8,128)(2,1)S(1)} collective-permute-done((bf16[72,512]{1,0:T(8,128)(2,1)S(1)}, bf16[72,512]{1,0:T(8,128)(2,1)S(1)}, u32[]{:S(2)}, u32[]{:S(2)}) %collective-permute-start.12) | collective-permute-done | bytes 73760 | tf_op jit(solution)/shard_map/ppermute | solution.py:252
  21.0 1.6 %collective-permute-start.13 = (bf16[72,512]{1,0:T(8,128)(2,1)S(1)}, bf16[72,512]{1,0:T(8,128)(2,1)S(1)}, u32[]{:S(2)}, u32[]{:S(2)}) collective-permute-start(bf16[72,512]{1,0:T(8,128)(2,1)S(1)} %get-tuple-element.35), channel_id=1, source_target_pairs={{0,5},{1,4},{2,7},{3,6},{4,1},{5,0},{6,3},{7,2},{8,13},{9,12},{10,... | collective-permute-start | bytes 221192 | tf_op jit(solution)/shard_map/ppermute | solution.py:252
  23.2 1.9 %collective-permute-done.13.refs_11_ = bf16[72,512]{1,0:T(8,128)(2,1)S(1)} collective-permute-done((bf16[72,512]{1,0:T(8,128)(2,1)S(1)}, bf16[72,512]{1,0:T(8,128)(2,1)S(1)}, u32[]{:S(2)}, u32[]{:S(2)}) %collective-permute-start.13) | collective-permute-done | bytes 73760 | tf_op jit(solution)/shard_map/ppermute | solution.py:252
  25.2 1.2 %attend.1 = (f32[2,1,8,128]{3,2,1,0:T(8,128)S(1)}, f32[2,1,8,128]{3,2,1,0:T(8,128)S(1)}, f32[2,1,8,128]{3,2,1,0:T(8,128)S(1)}, f32[2,1,8,128]{3,2,1,0:T(8,128)S(1)}) custom-call(s32[1]{0:T(128)} %bitcast.device_ref, f32[1]{0:T(128)S(6)} %copy.16.guidance_ref, bf16[64,4096]{1,0:T(8,128)(2,1)S(1)} %bitcast.2, bf16[8,128]{1,0:T(8,128)(2,1)S(1)} %get-tuple-element.27.home_ref, ...), custom_call_target="tpu_custom_call" | custom-call | tf_op jit(solution)/shard_map/attend/pallas_call | solution.py:294
  26.5 0.0 copy-start.1
  26.5 0.2 collective-permute-start.14
  26.7 1.7 %collective-permute-start.15 = (f32[2,1,8,128]{3,2,1,0:T(8,128)S(1)}, f32[2,1,8,128]{3,2,1,0:T(8,128)S(1)}, u32[]{:S(2)}, u32[]{:S(2)}) collective-permute-start(f32[2,1,8,128]{3,2,1,0:T(8,128)S(1)} %get-tuple-element.37), channel_id=1, source_target_pairs={{0,5},{1,4},{2,7},{3,6},{4,1},{5,0},{6,3},{7,2},{8,13},{9,12},{10,... | collective-permute-start | bytes 24584 | tf_op jit(solution)/shard_map/ppermute | solution.py:252
  28.5 2.4 %collective-permute-start.16 = (f32[2,1,8,128]{3,2,1,0:T(8,128)S(1)}, f32[2,1,8,128]{3,2,1,0:T(8,128)S(1)}, u32[]{:S(2)}, u32[]{:S(2)}) collective-permute-start(f32[2,1,8,128]{3,2,1,0:T(8,128)S(1)} %get-tuple-element.38), channel_id=1, source_target_pairs={{0,9},{1,8},{2,11},{3,10},{4,13},{5,12},{6,15},{7,14},{8,1},{9,0},... | collective-permute-start | bytes 24584 | tf_op jit(solution)/shard_map/ppermute | solution.py:252
  30.9 1.6 %collective-permute-done.16.refs_2_ = f32[2,1,8,128]{3,2,1,0:T(8,128)S(1)} collective-permute-done((f32[2,1,8,128]{3,2,1,0:T(8,128)S(1)}, f32[2,1,8,128]{3,2,1,0:T(8,128)S(1)}, u32[]{:S(2)}, u32[]{:S(2)}) %collective-permute-start.16) | collective-permute-done | bytes 8224 | tf_op jit(solution)/shard_map/ppermute | solution.py:252
  32.4 3.3 %collective-permute-done.17.refs_3_ = f32[2,1,8,128]{3,2,1,0:T(8,128)S(1)} collective-permute-done((f32[2,1,8,128]{3,2,1,0:T(8,128)S(1)}, f32[2,1,8,128]{3,2,1,0:T(8,128)S(1)}, u32[]{:S(2)}, u32[]{:S(2)}) %collective-permute-start.17) | collective-permute-done | bytes 8224 | tf_op jit(solution)/shard_map/ppermute | solution.py:252
  35.7 0.8 %collective-permute-start.18 = (f32[1,8,128]{2,1,0:T(8,128)S(1)}, f32[1,8,128]{2,1,0:T(8,128)S(1)}, u32[]{:S(2)}, u32[]{:S(2)}) collective-permute-start(f32[1,8,128]{2,1,0:T(8,128)S(1)} %get-tuple-element.41), channel_id=1, source_target_pairs={{0,2},{1,3},{2,0},{3,1},{4,6},{5,7},{6,4},{7,5},{8,10},{9,11},{10,... | collective-permute-start | bytes 12296 | tf_op jit(solution)/shard_map/ppermute | solution.py:252
  37.2 0.1 prepare.1
  37.3 2.0 %collective-permute-done.18.came_ref = f32[1,8,128]{2,1,0:T(8,128)S(1)} collective-permute-done((f32[1,8,128]{2,1,0:T(8,128)S(1)}, f32[1,8,128]{2,1,0:T(8,128)S(1)}, u32[]{:S(2)}, u32[]{:S(2)}) %collective-permute-start.18) | collective-permute-done | bytes 4128 | tf_op jit(solution)/shard_map/ppermute | solution.py:252
  39.4 0.8 %finish.1 = (f32[1,64,64]{2,1,0:T(8,128)}, f32[1,16,64]{2,1,0:T(8,128)}) custom-call(f32[1,8,128]{2,1,0:T(8,128)S(1)} %get-tuple-element.40.kept_ref, f32[1,8,128]{2,1,0:T(8,128)S(1)} %collective-permute-done.18.came_ref, bf16[1,64,48]{2,1,0:T(8,128)(2,1)S(1)} %get-tuple-element.42.spread_ref, f32[1,16,64]{2,1,0:T(8,128)S(1)} %get-tuple-element.43.means_ref, ...), custom_call_target="tpu_custom_call" | custom-call | tf_op jit(solution)/shard_map/finish/pallas_call | solution.py:325
  (18 shorter events, 0.0 us)
Async XLA Ops:
  0.6 24.6 %copy-start = (bf16[4096,64]{0,1:T(8,128)(2,1)S(1)}, bf16[4096,64]{0,1:T(8,128)(2,1)}, u32[]{:S(2)}) copy-start(bf16[4096,64]{0,1:T(8,128)(2,1)} %param.16) | copy-start | bytes 1572868
  2.0 17.6 %collective-permute-start.3 = (bf16[64,1024]{1,0:T(8,128)(2,1)S(1)}, bf16[64,1024]{1,0:T(8,128)(2,1)S(1)}, u32[]{:S(2)}, u32[]{:S(2)}) collective-permute-start(bf16[64,1024]{1,0:T(8,128)(2,1)S(1)} %get-tuple-element.29), channel_id=1, source_target_pairs={{0,6},{1,7},{2,4},{3,5},{4,2},{5,3},{6,0},{7,1},{8,14},{9,15},{10,... | collective-permute-start | bytes 393224 | tf_op jit(solution)/shard_map/ppermute | solution.py:252
  6.1 13.8 %collective-permute-start.4 = (bf16[64,1024]{1,0:T(8,128)(2,1)S(1)}, bf16[64,1024]{1,0:T(8,128)(2,1)S(1)}, u32[]{:S(2)}, u32[]{:S(2)}) collective-permute-start(bf16[64,1024]{1,0:T(8,128)(2,1)S(1)} %get-tuple-element.30), channel_id=1, source_target_pairs={{0,2},{1,3},{2,0},{3,1},{4,6},{5,7},{6,4},{7,5},{8,10},{9,11},{10,... | collective-permute-start | bytes 393224 | tf_op jit(solution)/shard_map/ppermute | solution.py:252
  6.6 0.7 %copy-start.2 = (s32[1,64]{1,0:T(1,128)S(1)}, s32[1,64]{1,0:T(1,128)}, u32[]{:S(2)}) copy-start(s32[1,64]{1,0:T(1,128)} %dest_ref.1) | copy-start | bytes 772
  6.6 13.5 %collective-permute-start.5 = (bf16[64,1024]{1,0:T(8,128)(2,1)S(1)}, bf16[64,1024]{1,0:T(8,128)(2,1)S(1)}, u32[]{:S(2)}, u32[]{:S(2)}) collective-permute-start(bf16[64,1024]{1,0:T(8,128)(2,1)S(1)} %get-tuple-element.31), channel_id=1, source_target_pairs={{0,4},{1,5},{2,6},{3,7},{4,0},{5,1},{6,2},{7,3},{8,12},{9,13},{10,... | collective-permute-start | bytes 393224 | tf_op jit(solution)/shard_map/ppermute | solution.py:252
  6.7 9.8 %collective-permute-start.10 = (bf16[64,512]{1,0:T(8,128)(2,1)S(1)}, bf16[64,512]{1,0:T(8,128)(2,1)S(1)}, u32[]{:S(2)}, u32[]{:S(2)}) collective-permute-start(bf16[64,512]{1,0:T(8,128)(2,1)S(1)} %get-tuple-element.32), channel_id=1, source_target_pairs={{0,1},{1,0},{2,3},{3,2},{4,5},{5,4},{6,7},{7,6},{8,9},{9,8},{10,11... | collective-permute-start | bytes 196616 | tf_op jit(solution)/shard_map/ppermute | solution.py:252
  7.2 1.2 %collective-permute-start.1 = (s32[1,64]{1,0:T(1,128)S(1)}, s32[1,64]{1,0:T(1,128)S(1)}, u32[]{:S(2)}, u32[]{:S(2)}) collective-permute-start(s32[1,64]{1,0:T(1,128)S(1)} %copy-done.2), channel_id=1, source_target_pairs={{0,1},{1,0},{2,3},{3,2},{4,5},{5,4},{6,7},{7,6},{8,9},{9,8},{10,11... | collective-permute-start | bytes 776 | tf_op jit(solution)/shard_map/ppermute | solution.py:252
  8.4 4.5 %collective-permute-start = (s32[1,64]{1,0:T(1,128)S(1)}, s32[1,64]{1,0:T(1,128)S(1)}, u32[]{:S(2)}, u32[]{:S(2)}) collective-permute-start(s32[1,64]{1,0:T(1,128)S(1)} %copy-done.2), channel_id=1, source_target_pairs={{0,8},{1,9},{2,10},{3,11},{4,12},{5,13},{6,14},{7,15},{8,0},{9,1},... | collective-permute-start | bytes 776 | tf_op jit(solution)/shard_map/ppermute | solution.py:252
  12.9 1.2 %collective-permute-start.2 = (s32[1,64]{1,0:T(1,128)S(1)}, s32[1,64]{1,0:T(1,128)S(1)}, u32[]{:S(2)}, u32[]{:S(2)}) collective-permute-start(s32[1,64]{1,0:T(1,128)S(1)} %collective-permute-done.other_ref), channel_id=1, source_target_pairs={{0,1},{1,0},{2,3},{3,2},{4,5},{5,4},{6,7},{7,6},{8,9},{9,8},{10,11... | collective-permute-start | bytes 776 | tf_op jit(solution)/shard_map/ppermute | solution.py:252
  14.2 5.2 %collective-permute-start.11 = (bf16[72,512]{1,0:T(8,128)(2,1)S(1)}, bf16[72,512]{1,0:T(8,128)(2,1)S(1)}, u32[]{:S(2)}, u32[]{:S(2)}) collective-permute-start(bf16[72,512]{1,0:T(8,128)(2,1)S(1)} %get-tuple-element.33), channel_id=1, source_target_pairs={{0,7},{1,6},{2,5},{3,4},{4,3},{5,2},{6,1},{7,0},{8,15},{9,14},{10,... | collective-permute-start | bytes 221192 | tf_op jit(solution)/shard_map/ppermute | solution.py:252
  16.5 4.4 %collective-permute-start.12 = (bf16[72,512]{1,0:T(8,128)(2,1)S(1)}, bf16[72,512]{1,0:T(8,128)(2,1)S(1)}, u32[]{:S(2)}, u32[]{:S(2)}) collective-permute-start(bf16[72,512]{1,0:T(8,128)(2,1)S(1)} %get-tuple-element.34), channel_id=1, source_target_pairs={{0,3},{1,2},{2,1},{3,0},{4,7},{5,6},{6,5},{7,4},{8,11},{9,10},{10,... | collective-permute-start | bytes 221192 | tf_op jit(solution)/shard_map/ppermute | solution.py:252
  19.4 5.8 %collective-permute-start.6 = (bf16[64,1024]{1,0:T(8,128)(2,1)S(1)}, bf16[64,1024]{1,0:T(8,128)(2,1)S(1)}, u32[]{:S(2)}, u32[]{:S(2)}) collective-permute-start(bf16[64,1024]{1,0:T(8,128)(2,1)S(1)} %get-tuple-element.28.refs_0_), channel_id=1, source_target_pairs={{0,1},{1,0},{2,3},{3,2},{4,5},{5,4},{6,7},{7,6},{8,9},{9,8},{10,11... | collective-permute-start | bytes 393224 | tf_op jit(solution)/shard_map/ppermute | solution.py:252
  19.6 5.6 %collective-permute-start.7 = (bf16[64,1024]{1,0:T(8,128)(2,1)S(1)}, bf16[64,1024]{1,0:T(8,128)(2,1)S(1)}, u32[]{:S(2)}, u32[]{:S(2)}) collective-permute-start(bf16[64,1024]{1,0:T(8,128)(2,1)S(1)} %collective-permute-done.3.refs_1_), channel_id=1, source_target_pairs={{0,1},{1,0},{2,3},{3,2},{4,5},{5,4},{6,7},{7,6},{8,9},{9,8},{10,11... | collective-permute-start | bytes 393224 | tf_op jit(solution)/shard_map/ppermute | solution.py:252
  19.9 5.3 %collective-permute-start.8 = (bf16[64,1024]{1,0:T(8,128)(2,1)S(1)}, bf16[64,1024]{1,0:T(8,128)(2,1)S(1)}, u32[]{:S(2)}, u32[]{:S(2)}) collective-permute-start(bf16[64,1024]{1,0:T(8,128)(2,1)S(1)} %collective-permute-done.4.refs_2_), channel_id=1, source_target_pairs={{0,1},{1,0},{2,3},{3,2},{4,5},{5,4},{6,7},{7,6},{8,9},{9,8},{10,11... | collective-permute-start | bytes 393224 | tf_op jit(solution)/shard_map/ppermute | solution.py:252
  20.1 5.1 %collective-permute-start.9 = (bf16[64,1024]{1,0:T(8,128)(2,1)S(1)}, bf16[64,1024]{1,0:T(8,128)(2,1)S(1)}, u32[]{:S(2)}, u32[]{:S(2)}) collective-permute-start(bf16[64,1024]{1,0:T(8,128)(2,1)S(1)} %collective-permute-done.5.refs_3_), channel_id=1, source_target_pairs={{0,1},{1,0},{2,3},{3,2},{4,5},{5,4},{6,7},{7,6},{8,9},{9,8},{10,11... | collective-permute-start | bytes 393224 | tf_op jit(solution)/shard_map/ppermute | solution.py:252
  21.0 4.2 %collective-permute-start.13 = (bf16[72,512]{1,0:T(8,128)(2,1)S(1)}, bf16[72,512]{1,0:T(8,128)(2,1)S(1)}, u32[]{:S(2)}, u32[]{:S(2)}) collective-permute-start(bf16[72,512]{1,0:T(8,128)(2,1)S(1)} %get-tuple-element.35), channel_id=1, source_target_pairs={{0,5},{1,4},{2,7},{3,6},{4,1},{5,0},{6,3},{7,2},{8,13},{9,12},{10,... | collective-permute-start | bytes 221192 | tf_op jit(solution)/shard_map/ppermute | solution.py:252
  26.5 10.7 %copy-start.1 = (f32[1,64,64]{2,1,0:T(8,128)S(1)}, f32[1,64,64]{2,1,0:T(8,128)}, u32[]{:S(2)}) copy-start(f32[1,64,64]{2,1,0:T(8,128)} %latents_ref.3) | copy-start | bytes 49156
  26.5 4.4 %collective-permute-start.14 = (f32[2,1,8,128]{3,2,1,0:T(8,128)S(1)}, f32[2,1,8,128]{3,2,1,0:T(8,128)S(1)}, u32[]{:S(2)}, u32[]{:S(2)}) collective-permute-start(f32[2,1,8,128]{3,2,1,0:T(8,128)S(1)} %get-tuple-element.36), channel_id=1, source_target_pairs={{0,1},{1,0},{2,3},{3,2},{4,5},{5,4},{6,7},{7,6},{8,9},{9,8},{10,11... | collective-permute-start | bytes 24584 | tf_op jit(solution)/shard_map/ppermute | solution.py:252
  26.7 4.1 %collective-permute-start.15 = (f32[2,1,8,128]{3,2,1,0:T(8,128)S(1)}, f32[2,1,8,128]{3,2,1,0:T(8,128)S(1)}, u32[]{:S(2)}, u32[]{:S(2)}) collective-permute-start(f32[2,1,8,128]{3,2,1,0:T(8,128)S(1)} %get-tuple-element.37), channel_id=1, source_target_pairs={{0,5},{1,4},{2,7},{3,6},{4,1},{5,0},{6,3},{7,2},{8,13},{9,12},{10,... | collective-permute-start | bytes 24584 | tf_op jit(solution)/shard_map/ppermute | solution.py:252
  28.5 4.0 %collective-permute-start.16 = (f32[2,1,8,128]{3,2,1,0:T(8,128)S(1)}, f32[2,1,8,128]{3,2,1,0:T(8,128)S(1)}, u32[]{:S(2)}, u32[]{:S(2)}) collective-permute-start(f32[2,1,8,128]{3,2,1,0:T(8,128)S(1)} %get-tuple-element.38), channel_id=1, source_target_pairs={{0,9},{1,8},{2,11},{3,10},{4,13},{5,12},{6,15},{7,14},{8,1},{9,0},... | collective-permute-start | bytes 24584 | tf_op jit(solution)/shard_map/ppermute | solution.py:252
  30.9 4.9 %collective-permute-start.17 = (f32[2,1,8,128]{3,2,1,0:T(8,128)S(1)}, f32[2,1,8,128]{3,2,1,0:T(8,128)S(1)}, u32[]{:S(2)}, u32[]{:S(2)}) collective-permute-start(f32[2,1,8,128]{3,2,1,0:T(8,128)S(1)} %get-tuple-element.39), channel_id=1, source_target_pairs={{0,13},{1,12},{2,15},{3,14},{4,9},{5,8},{6,11},{7,10},{8,5},{9,4},... | collective-permute-start | bytes 24584 | tf_op jit(solution)/shard_map/ppermute | solution.py:252
  35.7 3.6 %collective-permute-start.18 = (f32[1,8,128]{2,1,0:T(8,128)S(1)}, f32[1,8,128]{2,1,0:T(8,128)S(1)}, u32[]{:S(2)}, u32[]{:S(2)}) collective-permute-start(f32[1,8,128]{2,1,0:T(8,128)S(1)} %get-tuple-element.41), channel_id=1, source_target_pairs={{0,2},{1,3},{2,0},{3,1},{4,6},{5,7},{6,4},{7,5},{8,10},{9,11},{10,... | collective-permute-start | bytes 12296 | tf_op jit(solution)/shard_map/ppermute | solution.py:252

commit v7 on v6

--- a/solution.py
+++ b/solution.py
@@ -35,23 +35,30 @@
         copy.wait()
 
 
-def pack_kernel(device_ref, query_ref, key_ref, value_ref, *refs, steps):
+def pack_keys_kernel(device_ref, key_ref, value_ref, *refs, steps):
     *out_refs, sems = refs
-    count = len(steps)
-    rows, columns = query_ref.shape
-    per_pair = columns // count
-    seat = lax.rem(device_ref[0], 2 * count)
+    rows, columns = key_ref.shape
+    per_pair = columns // len(steps)
+    seat = lax.rem(device_ref[0], 2 * len(steps))
     pieces = []
     for place, step in enumerate(steps):
-        start = (seat ^ step) // 2 * per_pair
-        span = pl.ds(pl.multiple_of(start, HD), per_pair)
+        span = pl.ds(pl.multiple_of((seat ^ step) // 2 * per_pair, HD), per_pair)
         pieces.append((key_ref.at[:, span], out_refs[place].at[pl.ds(0, rows), :]))
         pieces.append((value_ref.at[:, span], out_refs[place].at[pl.ds(rows, rows), :]))
-        folded = per_pair // FOLD
+    fetch(pieces, sems)
+
+
+def pack_queries_kernel(device_ref, query_ref, *refs, steps):
+    *out_refs, sems = refs
+    rows, columns = query_ref.shape
+    folded = columns // len(steps) // FOLD
+    seat = lax.rem(device_ref[0], 2 * len(steps))
+    pieces = []
+    for place, step in enumerate(steps):
         for fold in range(FOLD):
-            span = pl.ds(pl.multiple_of(start + fold * folded, HD), folded)
-            target = out_refs[count + place].at[pl.ds(fold * rows, rows), :]
-            pieces.append((query_ref.at[:, span], target))
+            start = ((seat ^ step) // 2 * FOLD + fold) * folded
+            span = pl.ds(pl.multiple_of(start, HD), folded)
+            pieces.append((query_ref.at[:, span], out_refs[place].at[pl.ds(fold * rows, rows), :]))
     fetch(pieces, sems)
 
 
@@ -135,9 +142,9 @@
             scores = lax.dot_general(
                 key, query, (((1,), (1,)), ((), ())), preferred_element_type=jnp.float32
             )
-            scores = scores + mask[:, : query.shape[0]]
+            scores = scores * (score_scale * math.log2(math.e)) + mask[:, : query.shape[0]]
             top = jnp.max(scores, axis=0, keepdims=True)
-            weights = jnp.exp2((scores - top) * (score_scale * math.log2(math.e)))
+            weights = jnp.exp2(scores - top)
             share = 1.0 / jnp.sum(weights, axis=0, keepdims=True)
             probabilities = (weights * share).astype(jnp.bfloat16)
             attended.append(
@@ -259,16 +266,24 @@
     query_shape = jax.ShapeDtypeStruct((FOLD * rows, per_pair // FOLD), bf16)
     query_shapes = [query_shape] + [note_shape] * (count - 1)
     sources = [pltpu.with_memory_space_constraint(part, pltpu.HBM) for part in (queries, keys, values)]
-    packed = pl.pallas_call(
-        functools.partial(pack_kernel, steps=steps),
-        out_shape=[kv_shape] * count + query_shapes,
-        in_specs=[smem, hbm, hbm, hbm],
-        out_specs=[vmem] * (2 * count),
-        scratch_shapes=[pltpu.SemaphoreType.DMA((count * (2 + FOLD),))],
-        compiler_params=small,
-        name="pack",
-    )(seat, *sources)
-    own, asked = packed[:count], packed[count:]
+    own = pl.pallas_call(
+        functools.partial(pack_keys_kernel, steps=steps),
+        out_shape=[kv_shape] * count,
+        in_specs=[smem, hbm, hbm],
+        out_specs=[vmem] * count,
+        scratch_shapes=[pltpu.SemaphoreType.DMA((2 * count,))],
+        compiler_params=small,
+        name="pack_keys",
+    )(seat, *sources[1:])
+    asked = pl.pallas_call(
+        functools.partial(pack_queries_kernel, steps=steps),
+        out_shape=query_shapes,
+        in_specs=[smem, hbm],
+        out_specs=[vmem] * count,
+        scratch_shapes=[pltpu.SemaphoreType.DMA((FOLD * count,))],
+        compiler_params=small,
+        name="pack_queries",
+    )(seat, sources[0])
     held = [own[0]] + [swap(own[place], steps[place]) for place in range(1, count)]
     mate_dest = swap(merge_dest, 1)
     mate_other = swap(other_dest, 1)

time: 40.3 us -> 41.7 us (1.035)
  Pallas kernels: 3.71 us -> 4.49 us
  starting transfers between devices: 18.6 us -> 19.3 us
    pallas_call x1 -> x2, Pallas kernels: 1.34 us -> 2.14 us  [the longest x1 1.2 us: run(): pl.pallas_call(functools.partial(pack_keys_kernel, steps=steps), out_shap...]
    ppermute x19, starting transfers between devices: 18.6 us -> 19.3 us  [swap(): return lax.ppermute(part, 'seq', [(i, i ^ step) for i in range(groups)])]
  transfers between devices with their start and end apart: 19 -> 19, of which waited for: 9 -> 9; matrix products, arithmetic and copies ran while one was open for 0% -> 0% of each run, Pallas kernels for 1% -> 3%
where the time goes in v7:
time: 41.7 us; the launch traced here: 41.4 us
  starting transfers between devices  19.3 us (46%)
  waiting for transfers between devices  15.1 us (36%)
  Pallas kernels  4.49 us (11%)
  between operations  2.04 us (5%)
  local copies, waits for them, and re-layouts  0.58 us (1%)
    ppermute x19, starting transfers between devices, swap(): return lax.ppermute(part, 'seq', [(i, i ^ step) for i in range(groups)])  19.3 us
    ppermute x19, waiting for transfers between devices, swap(): return lax.ppermute(part, 'seq', [(i, i ^ step) for i in range(groups)])  15.1 us
    pallas_call x1, Pallas kernels, run(): pl.pallas_call(functools.partial(attend_kernel, score_scale=1.0 / math.sq...  1.23 us
    pallas_call x1, Pallas kernels, run(): pl.pallas_call(functools.partial(pack_keys_kernel, steps=steps), out_shap...  1.2 us
    pallas_call x1, Pallas kernels, run(): pl.pallas_call(functools.partial(pack_queries_kernel, steps=steps), out_s...  0.94 us
  transfers between devices with their start and end apart: 19, of which 9 were waited for; matrix products, arithmetic and copies ran while one was open for 0% of the time, Pallas kernels for 3%

profile of v7, /device:TPU:0, one launch (start us, length us, event | category | flops | bytes accessed | tf_op | source)
XLA Modules:
  0.0 41.4 jit_solution(7505888817915459693)
XLA Ops:
  0.6 1.2 %pack_keys.1 = (bf16[64,1024]{1,0:T(8,128)(2,1)S(1)}, bf16[64,1024]{1,0:T(8,128)(2,1)S(1)}, bf16[64,1024]{1,0:T(8,128)(2,1)S(1)}, bf16[64,1024]{1,0:T(8,128)(2,1)S(1)}) custom-call(s32[1]{0:T(128)} %bitcast.device_ref, bf16[32,4096]{1,0:T(8,128)(2,1)} %key_ref.1, bf16[32,4096]{1,0:T(8,128)(2,1)} %value_ref.1), custom_call_target="tpu_custom_call" | custom-call | tf_op jit(solution)/shard_map/pack_keys/pallas_call | solution.py:269
  1.9 4.1 %collective-permute-start.3 = (bf16[64,1024]{1,0:T(8,128)(2,1)S(1)}, bf16[64,1024]{1,0:T(8,128)(2,1)S(1)}, u32[]{:S(2)}, u32[]{:S(2)}) collective-permute-start(bf16[64,1024]{1,0:T(8,128)(2,1)S(1)} %get-tuple-element.29), channel_id=1, source_target_pairs={{0,6},{1,7},{2,4},{3,5},{4,2},{5,3},{6,0},{7,1},{8,14},{9,15},{10,... | collective-permute-start | bytes 393224 | tf_op jit(solution)/shard_map/ppermute | solution.py:259
  5.9 0.5 %collective-permute-start.4 = (bf16[64,1024]{1,0:T(8,128)(2,1)S(1)}, bf16[64,1024]{1,0:T(8,128)(2,1)S(1)}, u32[]{:S(2)}, u32[]{:S(2)}) collective-permute-start(bf16[64,1024]{1,0:T(8,128)(2,1)S(1)} %get-tuple-element.30), channel_id=1, source_target_pairs={{0,2},{1,3},{2,0},{3,1},{4,6},{5,7},{6,4},{7,5},{8,10},{9,11},{10,... | collective-permute-start | bytes 393224 | tf_op jit(solution)/shard_map/ppermute | solution.py:259
  6.4 0.1 collective-permute-start.5
  6.6 0.9 %pack_queries.1 = (bf16[64,512]{1,0:T(8,128)(2,1)S(1)}, bf16[72,512]{1,0:T(8,128)(2,1)S(1)}, bf16[72,512]{1,0:T(8,128)(2,1)S(1)}, bf16[72,512]{1,0:T(8,128)(2,1)S(1)}) custom-call(s32[1]{0:T(128)} %bitcast.device_ref, bf16[32,4096]{1,0:T(8,128)(2,1)} %query_ref.1), custom_call_target="tpu_custom_call" | custom-call | tf_op jit(solution)/shard_map/pack_queries/pallas_call | solution.py:278
  7.5 0.1 collective-permute-start.10
  7.6 0.6 %copy-done.2 = s32[1,64]{1,0:T(1,128)S(1)} copy-done((s32[1,64]{1,0:T(1,128)S(1)}, s32[1,64]{1,0:T(1,128)}, u32[]{:S(2)}) %copy-start.2) | copy-done | bytes 280
  8.2 1.2 %collective-permute-done.1.mate_dest_ref = s32[1,64]{1,0:T(1,128)S(1)} collective-permute-done((s32[1,64]{1,0:T(1,128)S(1)}, s32[1,64]{1,0:T(1,128)S(1)}, u32[]{:S(2)}, u32[]{:S(2)}) %collective-permute-start.1) | collective-permute-done | bytes 288 | tf_op jit(solution)/shard_map/ppermute | solution.py:259
  9.3 2.9 %collective-permute-start = (s32[1,64]{1,0:T(1,128)S(1)}, s32[1,64]{1,0:T(1,128)S(1)}, u32[]{:S(2)}, u32[]{:S(2)}) collective-permute-start(s32[1,64]{1,0:T(1,128)S(1)} %copy-done.2), channel_id=1, source_target_pairs={{0,8},{1,9},{2,10},{3,11},{4,12},{5,13},{6,14},{7,15},{8,0},{9,1},... | collective-permute-start | bytes 776 | tf_op jit(solution)/shard_map/ppermute | solution.py:259
  12.2 1.6 %collective-permute-done.other_ref = s32[1,64]{1,0:T(1,128)S(1)} collective-permute-done((s32[1,64]{1,0:T(1,128)S(1)}, s32[1,64]{1,0:T(1,128)S(1)}, u32[]{:S(2)}, u32[]{:S(2)}) %collective-permute-start) | collective-permute-done | bytes 288 | tf_op jit(solution)/shard_map/ppermute | solution.py:259
  13.8 1.2 %collective-permute-done.2.mate_other_ref = s32[1,64]{1,0:T(1,128)S(1)} collective-permute-done((s32[1,64]{1,0:T(1,128)S(1)}, s32[1,64]{1,0:T(1,128)S(1)}, u32[]{:S(2)}, u32[]{:S(2)}) %collective-permute-start.2) | collective-permute-done | bytes 288 | tf_op jit(solution)/shard_map/ppermute | solution.py:259
  15.0 0.2 note.1
  15.1 2.7 %collective-permute-start.11 = (bf16[72,512]{1,0:T(8,128)(2,1)S(1)}, bf16[72,512]{1,0:T(8,128)(2,1)S(1)}, u32[]{:S(2)}, u32[]{:S(2)}) collective-permute-start(bf16[72,512]{1,0:T(8,128)(2,1)S(1)} %get-tuple-element.33), channel_id=1, source_target_pairs={{0,7},{1,6},{2,5},{3,4},{4,3},{5,2},{6,1},{7,0},{8,15},{9,14},{10,... | collective-permute-start | bytes 221192 | tf_op jit(solution)/shard_map/ppermute | solution.py:259
  17.8 0.5 %collective-permute-start.12 = (bf16[72,512]{1,0:T(8,128)(2,1)S(1)}, bf16[72,512]{1,0:T(8,128)(2,1)S(1)}, u32[]{:S(2)}, u32[]{:S(2)}) collective-permute-start(bf16[72,512]{1,0:T(8,128)(2,1)S(1)} %get-tuple-element.34), channel_id=1, source_target_pairs={{0,3},{1,2},{2,1},{3,0},{4,7},{5,6},{6,5},{7,4},{8,11},{9,10},{10,... | collective-permute-start | bytes 221192 | tf_op jit(solution)/shard_map/ppermute | solution.py:259
  18.3 1.9 %collective-permute-done.11.refs_9_ = bf16[72,512]{1,0:T(8,128)(2,1)S(1)} collective-permute-done((bf16[72,512]{1,0:T(8,128)(2,1)S(1)}, bf16[72,512]{1,0:T(8,128)(2,1)S(1)}, u32[]{:S(2)}, u32[]{:S(2)}) %collective-permute-start.11) | collective-permute-done | bytes 73760 | tf_op jit(solution)/shard_map/ppermute | solution.py:259
  20.2 0.3 collective-permute-start.6
  20.5 0.2 collective-permute-start.7
  20.7 0.3 collective-permute-start.8
  21.0 0.2 collective-permute-start.9
  21.2 0.7 %collective-permute-done.12.refs_10_ = bf16[72,512]{1,0:T(8,128)(2,1)S(1)} collective-permute-done((bf16[72,512]{1,0:T(8,128)(2,1)S(1)}, bf16[72,512]{1,0:T(8,128)(2,1)S(1)}, u32[]{:S(2)}, u32[]{:S(2)}) %collective-permute-start.12) | collective-permute-done | bytes 73760 | tf_op jit(solution)/shard_map/ppermute | solution.py:259
  21.9 1.9 %collective-permute-start.13 = (bf16[72,512]{1,0:T(8,128)(2,1)S(1)}, bf16[72,512]{1,0:T(8,128)(2,1)S(1)}, u32[]{:S(2)}, u32[]{:S(2)}) collective-permute-start(bf16[72,512]{1,0:T(8,128)(2,1)S(1)} %get-tuple-element.35), channel_id=1, source_target_pairs={{0,5},{1,4},{2,7},{3,6},{4,1},{5,0},{6,3},{7,2},{8,13},{9,12},{10,... | collective-permute-start | bytes 221192 | tf_op jit(solution)/shard_map/ppermute | solution.py:259
  24.5 1.7 %collective-permute-done.13.refs_11_ = bf16[72,512]{1,0:T(8,128)(2,1)S(1)} collective-permute-done((bf16[72,512]{1,0:T(8,128)(2,1)S(1)}, bf16[72,512]{1,0:T(8,128)(2,1)S(1)}, u32[]{:S(2)}, u32[]{:S(2)}) %collective-permute-start.13) | collective-permute-done | bytes 73760 | tf_op jit(solution)/shard_map/ppermute | solution.py:259
  26.2 1.2 %attend.1 = (f32[2,1,8,128]{3,2,1,0:T(8,128)S(1)}, f32[2,1,8,128]{3,2,1,0:T(8,128)S(1)}, f32[2,1,8,128]{3,2,1,0:T(8,128)S(1)}, f32[2,1,8,128]{3,2,1,0:T(8,128)S(1)}) custom-call(s32[1]{0:T(128)} %bitcast.device_ref, f32[1]{0:T(128)S(6)} %copy.16.guidance_ref, bf16[64,4096]{1,0:T(8,128)(2,1)S(1)} %bitcast.2, bf16[8,128]{1,0:T(8,128)(2,1)S(1)} %get-tuple-element.27.home_ref, ...), custom_call_target="tpu_custom_call" | custom-call | tf_op jit(solution)/shard_map/attend/pallas_call | solution.py:309
  27.5 0.3 collective-permute-start.14
  27.8 2.0 %collective-permute-start.15 = (f32[2,1,8,128]{3,2,1,0:T(8,128)S(1)}, f32[2,1,8,128]{3,2,1,0:T(8,128)S(1)}, u32[]{:S(2)}, u32[]{:S(2)}) collective-permute-start(f32[2,1,8,128]{3,2,1,0:T(8,128)S(1)} %get-tuple-element.37), channel_id=1, source_target_pairs={{0,5},{1,4},{2,7},{3,6},{4,1},{5,0},{6,3},{7,2},{8,13},{9,12},{10,... | collective-permute-start | bytes 24584 | tf_op jit(solution)/shard_map/ppermute | solution.py:259
  29.8 2.3 %collective-permute-start.16 = (f32[2,1,8,128]{3,2,1,0:T(8,128)S(1)}, f32[2,1,8,128]{3,2,1,0:T(8,128)S(1)}, u32[]{:S(2)}, u32[]{:S(2)}) collective-permute-start(f32[2,1,8,128]{3,2,1,0:T(8,128)S(1)} %get-tuple-element.38), channel_id=1, source_target_pairs={{0,9},{1,8},{2,11},{3,10},{4,13},{5,12},{6,15},{7,14},{8,1},{9,0},... | collective-permute-start | bytes 24584 | tf_op jit(solution)/shard_map/ppermute | solution.py:259
  32.1 1.7 %collective-permute-done.16.refs_2_ = f32[2,1,8,128]{3,2,1,0:T(8,128)S(1)} collective-permute-done((f32[2,1,8,128]{3,2,1,0:T(8,128)S(1)}, f32[2,1,8,128]{3,2,1,0:T(8,128)S(1)}, u32[]{:S(2)}, u32[]{:S(2)}) %collective-permute-start.16) | collective-permute-done | bytes 8224 | tf_op jit(solution)/shard_map/ppermute | solution.py:259
  33.8 3.2 %collective-permute-done.17.refs_3_ = f32[2,1,8,128]{3,2,1,0:T(8,128)S(1)} collective-permute-done((f32[2,1,8,128]{3,2,1,0:T(8,128)S(1)}, f32[2,1,8,128]{3,2,1,0:T(8,128)S(1)}, u32[]{:S(2)}, u32[]{:S(2)}) %collective-permute-start.17) | collective-permute-done | bytes 8224 | tf_op jit(solution)/shard_map/ppermute | solution.py:259
  37.0 0.8 %collective-permute-start.18 = (f32[1,8,128]{2,1,0:T(8,128)S(1)}, f32[1,8,128]{2,1,0:T(8,128)S(1)}, u32[]{:S(2)}, u32[]{:S(2)}) collective-permute-start(f32[1,8,128]{2,1,0:T(8,128)S(1)} %get-tuple-element.41), channel_id=1, source_target_pairs={{0,2},{1,3},{2,0},{3,1},{4,6},{5,7},{6,4},{7,5},{8,10},{9,11},{10,... | collective-permute-start | bytes 12296 | tf_op jit(solution)/shard_map/ppermute | solution.py:259
  38.4 0.1 prepare.1
  38.6 2.0 %collective-permute-done.18.came_ref = f32[1,8,128]{2,1,0:T(8,128)S(1)} collective-permute-done((f32[1,8,128]{2,1,0:T(8,128)S(1)}, f32[1,8,128]{2,1,0:T(8,128)S(1)}, u32[]{:S(2)}, u32[]{:S(2)}) %collective-permute-start.18) | collective-permute-done | bytes 4128 | tf_op jit(solution)/shard_map/ppermute | solution.py:259
  40.6 0.8 %finish.1 = (f32[1,64,64]{2,1,0:T(8,128)}, f32[1,16,64]{2,1,0:T(8,128)}) custom-call(f32[1,8,128]{2,1,0:T(8,128)S(1)} %get-tuple-element.40.kept_ref, f32[1,8,128]{2,1,0:T(8,128)S(1)} %collective-permute-done.18.came_ref, bf16[1,64,48]{2,1,0:T(8,128)(2,1)S(1)} %get-tuple-element.42.spread_ref, f32[1,16,64]{2,1,0:T(8,128)S(1)} %get-tuple-element.43.means_ref, ...), custom_call_target="tpu_custom_call" | custom-call | tf_op jit(solution)/shard_map/finish/pallas_call | solution.py:340
  (19 shorter events, 0.1 us)
Async XLA Ops:
  0.6 25.6 %copy-start = (bf16[4096,64]{0,1:T(8,128)(2,1)S(1)}, bf16[4096,64]{0,1:T(8,128)(2,1)}, u32[]{:S(2)}) copy-start(bf16[4096,64]{0,1:T(8,128)(2,1)} %param.16) | copy-start | bytes 1572868
  1.9 18.6 %collective-permute-start.3 = (bf16[64,1024]{1,0:T(8,128)(2,1)S(1)}, bf16[64,1024]{1,0:T(8,128)(2,1)S(1)}, u32[]{:S(2)}, u32[]{:S(2)}) collective-permute-start(bf16[64,1024]{1,0:T(8,128)(2,1)S(1)} %get-tuple-element.29), channel_id=1, source_target_pairs={{0,6},{1,7},{2,4},{3,5},{4,2},{5,3},{6,0},{7,1},{8,14},{9,15},{10,... | collective-permute-start | bytes 393224 | tf_op jit(solution)/shard_map/ppermute | solution.py:259
  5.9 14.8 %collective-permute-start.4 = (bf16[64,1024]{1,0:T(8,128)(2,1)S(1)}, bf16[64,1024]{1,0:T(8,128)(2,1)S(1)}, u32[]{:S(2)}, u32[]{:S(2)}) collective-permute-start(bf16[64,1024]{1,0:T(8,128)(2,1)S(1)} %get-tuple-element.30), channel_id=1, source_target_pairs={{0,2},{1,3},{2,0},{3,1},{4,6},{5,7},{6,4},{7,5},{8,10},{9,11},{10,... | collective-permute-start | bytes 393224 | tf_op jit(solution)/shard_map/ppermute | solution.py:259
  6.4 14.6 %collective-permute-start.5 = (bf16[64,1024]{1,0:T(8,128)(2,1)S(1)}, bf16[64,1024]{1,0:T(8,128)(2,1)S(1)}, u32[]{:S(2)}, u32[]{:S(2)}) collective-permute-start(bf16[64,1024]{1,0:T(8,128)(2,1)S(1)} %get-tuple-element.31), channel_id=1, source_target_pairs={{0,4},{1,5},{2,6},{3,7},{4,0},{5,1},{6,2},{7,3},{8,12},{9,13},{10,... | collective-permute-start | bytes 393224 | tf_op jit(solution)/shard_map/ppermute | solution.py:259
  7.5 0.7 %copy-start.2 = (s32[1,64]{1,0:T(1,128)S(1)}, s32[1,64]{1,0:T(1,128)}, u32[]{:S(2)}) copy-start(s32[1,64]{1,0:T(1,128)} %dest_ref.1) | copy-start | bytes 772
  7.5 10.3 %collective-permute-start.10 = (bf16[64,512]{1,0:T(8,128)(2,1)S(1)}, bf16[64,512]{1,0:T(8,128)(2,1)S(1)}, u32[]{:S(2)}, u32[]{:S(2)}) collective-permute-start(bf16[64,512]{1,0:T(8,128)(2,1)S(1)} %get-tuple-element.32), channel_id=1, source_target_pairs={{0,1},{1,0},{2,3},{3,2},{4,5},{5,4},{6,7},{7,6},{8,9},{9,8},{10,11... | collective-permute-start | bytes 196616 | tf_op jit(solution)/shard_map/ppermute | solution.py:259
  8.2 1.2 %collective-permute-start.1 = (s32[1,64]{1,0:T(1,128)S(1)}, s32[1,64]{1,0:T(1,128)S(1)}, u32[]{:S(2)}, u32[]{:S(2)}) collective-permute-start(s32[1,64]{1,0:T(1,128)S(1)} %copy-done.2), channel_id=1, source_target_pairs={{0,1},{1,0},{2,3},{3,2},{4,5},{5,4},{6,7},{7,6},{8,9},{9,8},{10,11... | collective-permute-start | bytes 776 | tf_op jit(solution)/shard_map/ppermute | solution.py:259
  9.3 4.5 %collective-permute-start = (s32[1,64]{1,0:T(1,128)S(1)}, s32[1,64]{1,0:T(1,128)S(1)}, u32[]{:S(2)}, u32[]{:S(2)}) collective-permute-start(s32[1,64]{1,0:T(1,128)S(1)} %copy-done.2), channel_id=1, source_target_pairs={{0,8},{1,9},{2,10},{3,11},{4,12},{5,13},{6,14},{7,15},{8,0},{9,1},... | collective-permute-start | bytes 776 | tf_op jit(solution)/shard_map/ppermute | solution.py:259
  13.8 1.2 %collective-permute-start.2 = (s32[1,64]{1,0:T(1,128)S(1)}, s32[1,64]{1,0:T(1,128)S(1)}, u32[]{:S(2)}, u32[]{:S(2)}) collective-permute-start(s32[1,64]{1,0:T(1,128)S(1)} %collective-permute-done.other_ref), channel_id=1, source_target_pairs={{0,1},{1,0},{2,3},{3,2},{4,5},{5,4},{6,7},{7,6},{8,9},{9,8},{10,11... | collective-permute-start | bytes 776 | tf_op jit(solution)/shard_map/ppermute | solution.py:259
  15.1 5.0 %collective-permute-start.11 = (bf16[72,512]{1,0:T(8,128)(2,1)S(1)}, bf16[72,512]{1,0:T(8,128)(2,1)S(1)}, u32[]{:S(2)}, u32[]{:S(2)}) collective-permute-start(bf16[72,512]{1,0:T(8,128)(2,1)S(1)} %get-tuple-element.33), channel_id=1, source_target_pairs={{0,7},{1,6},{2,5},{3,4},{4,3},{5,2},{6,1},{7,0},{8,15},{9,14},{10,... | collective-permute-start | bytes 221192 | tf_op jit(solution)/shard_map/ppermute | solution.py:259
  17.8 4.0 %collective-permute-start.12 = (bf16[72,512]{1,0:T(8,128)(2,1)S(1)}, bf16[72,512]{1,0:T(8,128)(2,1)S(1)}, u32[]{:S(2)}, u32[]{:S(2)}) collective-permute-start(bf16[72,512]{1,0:T(8,128)(2,1)S(1)} %get-tuple-element.34), channel_id=1, source_target_pairs={{0,3},{1,2},{2,1},{3,0},{4,7},{5,6},{6,5},{7,4},{8,11},{9,10},{10,... | collective-permute-start | bytes 221192 | tf_op jit(solution)/shard_map/ppermute | solution.py:259
  20.2 6.0 %collective-permute-start.6 = (bf16[64,1024]{1,0:T(8,128)(2,1)S(1)}, bf16[64,1024]{1,0:T(8,128)(2,1)S(1)}, u32[]{:S(2)}, u32[]{:S(2)}) collective-permute-start(bf16[64,1024]{1,0:T(8,128)(2,1)S(1)} %get-tuple-element.28.refs_0_), channel_id=1, source_target_pairs={{0,1},{1,0},{2,3},{3,2},{4,5},{5,4},{6,7},{7,6},{8,9},{9,8},{10,11... | collective-permute-start | bytes 393224 | tf_op jit(solution)/shard_map/ppermute | solution.py:259
  20.5 5.7 %collective-permute-start.7 = (bf16[64,1024]{1,0:T(8,128)(2,1)S(1)}, bf16[64,1024]{1,0:T(8,128)(2,1)S(1)}, u32[]{:S(2)}, u32[]{:S(2)}) collective-permute-start(bf16[64,1024]{1,0:T(8,128)(2,1)S(1)} %collective-permute-done.3.refs_1_), channel_id=1, source_target_pairs={{0,1},{1,0},{2,3},{3,2},{4,5},{5,4},{6,7},{7,6},{8,9},{9,8},{10,11... | collective-permute-start | bytes 393224 | tf_op jit(solution)/shard_map/ppermute | solution.py:259
  20.7 5.5 %collective-permute-start.8 = (bf16[64,1024]{1,0:T(8,128)(2,1)S(1)}, bf16[64,1024]{1,0:T(8,128)(2,1)S(1)}, u32[]{:S(2)}, u32[]{:S(2)}) collective-permute-start(bf16[64,1024]{1,0:T(8,128)(2,1)S(1)} %collective-permute-done.4.refs_2_), channel_id=1, source_target_pairs={{0,1},{1,0},{2,3},{3,2},{4,5},{5,4},{6,7},{7,6},{8,9},{9,8},{10,11... | collective-permute-start | bytes 393224 | tf_op jit(solution)/shard_map/ppermute | solution.py:259
  21.0 5.2 %collective-permute-start.9 = (bf16[64,1024]{1,0:T(8,128)(2,1)S(1)}, bf16[64,1024]{1,0:T(8,128)(2,1)S(1)}, u32[]{:S(2)}, u32[]{:S(2)}) collective-permute-start(bf16[64,1024]{1,0:T(8,128)(2,1)S(1)} %collective-permute-done.5.refs_3_), channel_id=1, source_target_pairs={{0,1},{1,0},{2,3},{3,2},{4,5},{5,4},{6,7},{7,6},{8,9},{9,8},{10,11... | collective-permute-start | bytes 393224 | tf_op jit(solution)/shard_map/ppermute | solution.py:259
  21.9 4.3 %collective-permute-start.13 = (bf16[72,512]{1,0:T(8,128)(2,1)S(1)}, bf16[72,512]{1,0:T(8,128)(2,1)S(1)}, u32[]{:S(2)}, u32[]{:S(2)}) collective-permute-start(bf16[72,512]{1,0:T(8,128)(2,1)S(1)} %get-tuple-element.35), channel_id=1, source_target_pairs={{0,5},{1,4},{2,7},{3,6},{4,1},{5,0},{6,3},{7,2},{8,13},{9,12},{10,... | collective-permute-start | bytes 221192 | tf_op jit(solution)/shard_map/ppermute | solution.py:259
  27.4 11.0 %copy-start.1 = (f32[1,64,64]{2,1,0:T(8,128)S(1)}, f32[1,64,64]{2,1,0:T(8,128)}, u32[]{:S(2)}) copy-start(f32[1,64,64]{2,1,0:T(8,128)} %latents_ref.3) | copy-start | bytes 49156
  27.5 4.7 %collective-permute-start.14 = (f32[2,1,8,128]{3,2,1,0:T(8,128)S(1)}, f32[2,1,8,128]{3,2,1,0:T(8,128)S(1)}, u32[]{:S(2)}, u32[]{:S(2)}) collective-permute-start(f32[2,1,8,128]{3,2,1,0:T(8,128)S(1)} %get-tuple-element.36), channel_id=1, source_target_pairs={{0,1},{1,0},{2,3},{3,2},{4,5},{5,4},{6,7},{7,6},{8,9},{9,8},{10,11... | collective-permute-start | bytes 24584 | tf_op jit(solution)/shard_map/ppermute | solution.py:259
  27.8 4.3 %collective-permute-start.15 = (f32[2,1,8,128]{3,2,1,0:T(8,128)S(1)}, f32[2,1,8,128]{3,2,1,0:T(8,128)S(1)}, u32[]{:S(2)}, u32[]{:S(2)}) collective-permute-start(f32[2,1,8,128]{3,2,1,0:T(8,128)S(1)} %get-tuple-element.37), channel_id=1, source_target_pairs={{0,5},{1,4},{2,7},{3,6},{4,1},{5,0},{6,3},{7,2},{8,13},{9,12},{10,... | collective-permute-start | bytes 24584 | tf_op jit(solution)/shard_map/ppermute | solution.py:259
  29.8 4.0 %collective-permute-start.16 = (f32[2,1,8,128]{3,2,1,0:T(8,128)S(1)}, f32[2,1,8,128]{3,2,1,0:T(8,128)S(1)}, u32[]{:S(2)}, u32[]{:S(2)}) collective-permute-start(f32[2,1,8,128]{3,2,1,0:T(8,128)S(1)} %get-tuple-element.38), channel_id=1, source_target_pairs={{0,9},{1,8},{2,11},{3,10},{4,13},{5,12},{6,15},{7,14},{8,1},{9,0},... | collective-permute-start | bytes 24584 | tf_op jit(solution)/shard_map/ppermute | solution.py:259
  32.1 4.9 %collective-permute-start.17 = (f32[2,1,8,128]{3,2,1,0:T(8,128)S(1)}, f32[2,1,8,128]{3,2,1,0:T(8,128)S(1)}, u32[]{:S(2)}, u32[]{:S(2)}) collective-permute-start(f32[2,1,8,128]{3,2,1,0:T(8,128)S(1)} %get-tuple-element.39), channel_id=1, source_target_pairs={{0,13},{1,12},{2,15},{3,14},{4,9},{5,8},{6,11},{7,10},{8,5},{9,4},... | collective-permute-start | bytes 24584 | tf_op jit(solution)/shard_map/ppermute | solution.py:259
  37.0 3.6 %collective-permute-start.18 = (f32[1,8,128]{2,1,0:T(8,128)S(1)}, f32[1,8,128]{2,1,0:T(8,128)S(1)}, u32[]{:S(2)}, u32[]{:S(2)}) collective-permute-start(f32[1,8,128]{2,1,0:T(8,128)S(1)} %get-tuple-element.41), channel_id=1, source_target_pairs={{0,2},{1,3},{2,0},{3,1},{4,6},{5,7},{6,4},{7,5},{8,10},{9,11},{10,... | collective-permute-start | bytes 12296 | tf_op jit(solution)/shard_map/ppermute | solution.py:259

commit v8 on v7

--- a/solution.py
+++ b/solution.py
@@ -94,7 +94,7 @@
 
 def attend_kernel(device_ref, guidance_ref, weight_ref, home_ref, *refs, score_scale, steps):
     count = len(steps)
-    pack_refs, out_refs = refs[:-count], refs[-count:]
+    pack_refs, out_refs = refs[:-2], refs[-2:]
     own_refs, mate_refs = pack_refs[:count], pack_refs[count : 2 * count]
     query_refs = pack_refs[2 * count :]
     rows, per_pair = own_refs[0].shape[0] // 2, own_refs[0].shape[1]
@@ -164,17 +164,13 @@
             near, far = part[place - first, 0], part[place - first, 1]
             near, far = jnp.where(front, near, far), jnp.where(front, far, near)
             quad, line = steps[place] // 4, steps[place] // 2 % 2
-            out_refs[quad][line, video] = near
-            out_refs[count // 2 + quad][line, video] = far
-
-
-def gather_kernel(*refs):
-    *part_refs, kept_ref, sent_ref = refs
-    for line, out_ref in enumerate((kept_ref, sent_ref)):
-        terms = [ref[line] for ref in part_refs]
-        while len(terms) > 1:
-            terms = [sum(terms[i : i + 2]) for i in range(0, len(terms), 2)]
-        out_ref[...] = terms[0]
+            out_refs[line][quad, video] = near
+            out_refs[line][count // 2 + quad, video] = far
+
+
+def add_lines_kernel(kept_ref, came_ref, *out_refs):
+    for quad, out_ref in enumerate(out_refs):
+        out_ref[...] = kept_ref[quad] + came_ref[quad]
 
 
 def prepare_kernel(
@@ -203,20 +199,14 @@
         sigma_ref[video] = jnp.broadcast_to(sigma_now, sigma_ref.shape[1:])
 
 
-def finish_kernel(
-    kept_ref,
-    came_ref,
-    spread_ref,
-    means_ref,
-    gains_ref,
-    sigma_ref,
-    latents_ref,
-    denoised_ref,
-    merged_ref,
-):
+def finish_kernel(*refs):
+    spread_ref, means_ref, gains_ref, sigma_ref, latents_ref, denoised_ref, merged_ref = refs[-7:]
     videos, _, channels = latents_ref.shape
     for video in range(videos):
-        lanes = kept_ref[video] + came_ref[video]
+        terms = [ref[video] for ref in refs[:-7]]
+        while len(terms) > 1:
+            terms = [sum(terms[i : i + 2]) for i in range(0, len(terms), 2)]
+        lanes = terms[0]
         merged = jnp.concatenate([lanes[:, :channels], lanes[:, channels:]], axis=0)
         merged_ref[video] = means_ref[video] + gains_ref[video] * merged
         top = merged.astype(jnp.bfloat16)
@@ -306,24 +296,24 @@
     asked = [swap(part, steps[place] ^ 1) for place, part in enumerate((asked[0], *noted))]
     lent = [swap(held[0], 1)] + [swap(held[place], 1) for place in range(1, count)]
     part_shape = (videos, cap_half // 2, 2 * channels)
-    parts = pl.pallas_call(
+    kept, sent = pl.pallas_call(
         functools.partial(attend_kernel, score_scale=1.0 / math.sqrt(HD), steps=steps),
-        out_shape=[jax.ShapeDtypeStruct((2, *part_shape), f32)] * count,
+        out_shape=[jax.ShapeDtypeStruct((count, *part_shape), f32)] * 2,
         in_specs=[smem, smem] + [vmem] * (1 + 1 + 3 * count),
-        out_specs=[vmem] * count,
+        out_specs=[vmem] * 2,
         compiler_params=large,
         name="attend",
     )(seat, guidance, out_weight.T, home, *held, *lent, *asked)
+    came = swap(sent, 2)
+    parts = pl.pallas_call(
+        add_lines_kernel,
+        out_shape=[jax.ShapeDtypeStruct(part_shape, f32)] * count,
+        in_specs=[vmem] * 2,
+        out_specs=[vmem] * count,
+        compiler_params=small,
+        name="add_lines",
+    )(kept, came)
     parts = [swap(parts[quad], 4 * quad + 1) for quad in range(count)]
-    kept, sent = pl.pallas_call(
-        gather_kernel,
-        out_shape=[jax.ShapeDtypeStruct(part_shape, f32)] * 2,
-        in_specs=[vmem] * count,
-        out_specs=[vmem] * 2,
-        compiler_params=small,
-        name="gather",
-    )(*parts)
-    came = swap(sent, 2)
     prepared = pl.pallas_call(
         prepare_kernel,
         out_shape=(
@@ -343,11 +333,11 @@
             jax.ShapeDtypeStruct((videos, tokens, channels), f32),
             jax.ShapeDtypeStruct((videos, cap_half, channels), f32),
         ),
-        in_specs=[vmem] * 7,
+        in_specs=[vmem] * (count + 5),
         out_specs=(vmem, vmem),
         compiler_params=small,
         name="finish",
-    )(kept, came, *prepared, latents)
+    )(*parts, *prepared, latents)
 
 
 def solution(mesh):

time: 41.7 us -> 41.7 us (level)
  starting transfers between devices: 19.3 us -> 20.5 us
  waiting for transfers between devices: 15.1 us -> 13.9 us
    ppermute x19, starting transfers between devices: 19.3 us -> 20.5 us  [swap(): return lax.ppermute(part, 'seq', [(i, i ^ step) for i in range(groups)])]
    ppermute x19, waiting for transfers between devices: 15.1 us -> 13.9 us  [swap(): return lax.ppermute(part, 'seq', [(i, i ^ step) for i in range(groups)])]
where the time goes in v8:
time: 41.7 us; the launch traced here: 41.5 us
  starting transfers between devices  20.5 us (49%)
  waiting for transfers between devices  13.9 us (33%)
  Pallas kernels  4.49 us (11%)
  between operations  2.05 us (5%)
  local copies, waits for them, and re-layouts  0.58 us (1%)
    ppermute x19, starting transfers between devices, swap(): return lax.ppermute(part, 'seq', [(i, i ^ step) for i in range(groups)])  20.5 us
    ppermute x19, waiting for transfers between devices, swap(): return lax.ppermute(part, 'seq', [(i, i ^ step) for i in range(groups)])  13.9 us
    pallas_call x1, Pallas kernels, run(): pl.pallas_call(functools.partial(attend_kernel, score_scale=1.0 / math.sq...  1.23 us
    pallas_call x1, Pallas kernels, run(): pl.pallas_call(functools.partial(pack_keys_kernel, steps=steps), out_shap...  1.2 us
    pallas_call x1, Pallas kernels, run(): pl.pallas_call(functools.partial(pack_queries_kernel, steps=steps), out_s...  0.94 us
  transfers between devices with their start and end apart: 19, of which 9 were waited for; matrix products, arithmetic and copies ran while one was open for 0% of the time, Pallas kernels for 3%

profile of v8, /device:TPU:0, one launch (start us, length us, event | category | flops | bytes accessed | tf_op | source)
XLA Modules:
  0.0 41.5 jit_solution(9593089846019498836)
XLA Ops:
  0.6 1.2 %pack_keys.1 = (bf16[64,1024]{1,0:T(8,128)(2,1)S(1)}, bf16[64,1024]{1,0:T(8,128)(2,1)S(1)}, bf16[64,1024]{1,0:T(8,128)(2,1)S(1)}, bf16[64,1024]{1,0:T(8,128)(2,1)S(1)}) custom-call(s32[1]{0:T(128)} %bitcast.device_ref, bf16[32,4096]{1,0:T(8,128)(2,1)} %key_ref.1, bf16[32,4096]{1,0:T(8,128)(2,1)} %value_ref.1), custom_call_target="tpu_custom_call" | custom-call | tf_op jit(solution)/shard_map/pack_keys/pallas_call | solution.py:259
  1.9 4.1 %collective-permute-start.3 = (bf16[64,1024]{1,0:T(8,128)(2,1)S(1)}, bf16[64,1024]{1,0:T(8,128)(2,1)S(1)}, u32[]{:S(2)}, u32[]{:S(2)}) collective-permute-start(bf16[64,1024]{1,0:T(8,128)(2,1)S(1)} %get-tuple-element.29), channel_id=1, source_target_pairs={{0,6},{1,7},{2,4},{3,5},{4,2},{5,3},{6,0},{7,1},{8,14},{9,15},{10,... | collective-permute-start | bytes 393224 | tf_op jit(solution)/shard_map/ppermute | solution.py:249
  5.9 0.5 %collective-permute-start.4 = (bf16[64,1024]{1,0:T(8,128)(2,1)S(1)}, bf16[64,1024]{1,0:T(8,128)(2,1)S(1)}, u32[]{:S(2)}, u32[]{:S(2)}) collective-permute-start(bf16[64,1024]{1,0:T(8,128)(2,1)S(1)} %get-tuple-element.30), channel_id=1, source_target_pairs={{0,2},{1,3},{2,0},{3,1},{4,6},{5,7},{6,4},{7,5},{8,10},{9,11},{10,... | collective-permute-start | bytes 393224 | tf_op jit(solution)/shard_map/ppermute | solution.py:249
  6.4 0.1 collective-permute-start.5
  6.6 0.9 %pack_queries.1 = (bf16[64,512]{1,0:T(8,128)(2,1)S(1)}, bf16[72,512]{1,0:T(8,128)(2,1)S(1)}, bf16[72,512]{1,0:T(8,128)(2,1)S(1)}, bf16[72,512]{1,0:T(8,128)(2,1)S(1)}) custom-call(s32[1]{0:T(128)} %bitcast.device_ref, bf16[32,4096]{1,0:T(8,128)(2,1)} %query_ref.1), custom_call_target="tpu_custom_call" | custom-call | tf_op jit(solution)/shard_map/pack_queries/pallas_call | solution.py:268
  7.5 0.0 copy-start.2
  7.5 0.1 collective-permute-start.10
  7.6 0.6 %copy-done.2 = s32[1,64]{1,0:T(1,128)S(1)} copy-done((s32[1,64]{1,0:T(1,128)S(1)}, s32[1,64]{1,0:T(1,128)}, u32[]{:S(2)}) %copy-start.2) | copy-done | bytes 280
  8.2 1.2 %collective-permute-done.1.mate_dest_ref = s32[1,64]{1,0:T(1,128)S(1)} collective-permute-done((s32[1,64]{1,0:T(1,128)S(1)}, s32[1,64]{1,0:T(1,128)S(1)}, u32[]{:S(2)}, u32[]{:S(2)}) %collective-permute-start.1) | collective-permute-done | bytes 288 | tf_op jit(solution)/shard_map/ppermute | solution.py:249
  9.3 2.9 %collective-permute-start = (s32[1,64]{1,0:T(1,128)S(1)}, s32[1,64]{1,0:T(1,128)S(1)}, u32[]{:S(2)}, u32[]{:S(2)}) collective-permute-start(s32[1,64]{1,0:T(1,128)S(1)} %copy-done.2), channel_id=1, source_target_pairs={{0,8},{1,9},{2,10},{3,11},{4,12},{5,13},{6,14},{7,15},{8,0},{9,1},... | collective-permute-start | bytes 776 | tf_op jit(solution)/shard_map/ppermute | solution.py:249
  12.2 1.6 %collective-permute-done.other_ref = s32[1,64]{1,0:T(1,128)S(1)} collective-permute-done((s32[1,64]{1,0:T(1,128)S(1)}, s32[1,64]{1,0:T(1,128)S(1)}, u32[]{:S(2)}, u32[]{:S(2)}) %collective-permute-start) | collective-permute-done | bytes 288 | tf_op jit(solution)/shard_map/ppermute | solution.py:249
  13.8 1.2 %collective-permute-done.2.mate_other_ref = s32[1,64]{1,0:T(1,128)S(1)} collective-permute-done((s32[1,64]{1,0:T(1,128)S(1)}, s32[1,64]{1,0:T(1,128)S(1)}, u32[]{:S(2)}, u32[]{:S(2)}) %collective-permute-start.2) | collective-permute-done | bytes 288 | tf_op jit(solution)/shard_map/ppermute | solution.py:249
  15.0 0.2 note.1
  15.1 2.7 %collective-permute-start.11 = (bf16[72,512]{1,0:T(8,128)(2,1)S(1)}, bf16[72,512]{1,0:T(8,128)(2,1)S(1)}, u32[]{:S(2)}, u32[]{:S(2)}) collective-permute-start(bf16[72,512]{1,0:T(8,128)(2,1)S(1)} %get-tuple-element.33), channel_id=1, source_target_pairs={{0,7},{1,6},{2,5},{3,4},{4,3},{5,2},{6,1},{7,0},{8,15},{9,14},{10,... | collective-permute-start | bytes 221192 | tf_op jit(solution)/shard_map/ppermute | solution.py:249
  17.8 0.5 %collective-permute-start.12 = (bf16[72,512]{1,0:T(8,128)(2,1)S(1)}, bf16[72,512]{1,0:T(8,128)(2,1)S(1)}, u32[]{:S(2)}, u32[]{:S(2)}) collective-permute-start(bf16[72,512]{1,0:T(8,128)(2,1)S(1)} %get-tuple-element.34), channel_id=1, source_target_pairs={{0,3},{1,2},{2,1},{3,0},{4,7},{5,6},{6,5},{7,4},{8,11},{9,10},{10,... | collective-permute-start | bytes 221192 | tf_op jit(solution)/shard_map/ppermute | solution.py:249
  18.3 1.9 %collective-permute-done.11.refs_9_ = bf16[72,512]{1,0:T(8,128)(2,1)S(1)} collective-permute-done((bf16[72,512]{1,0:T(8,128)(2,1)S(1)}, bf16[72,512]{1,0:T(8,128)(2,1)S(1)}, u32[]{:S(2)}, u32[]{:S(2)}) %collective-permute-start.11) | collective-permute-done | bytes 73760 | tf_op jit(solution)/shard_map/ppermute | solution.py:249
  20.2 0.3 collective-permute-start.6
  20.5 0.2 collective-permute-start.7
  20.7 0.3 collective-permute-start.8
  21.0 0.2 collective-permute-start.9
  21.2 0.7 %collective-permute-done.12.refs_10_ = bf16[72,512]{1,0:T(8,128)(2,1)S(1)} collective-permute-done((bf16[72,512]{1,0:T(8,128)(2,1)S(1)}, bf16[72,512]{1,0:T(8,128)(2,1)S(1)}, u32[]{:S(2)}, u32[]{:S(2)}) %collective-permute-start.12) | collective-permute-done | bytes 73760 | tf_op jit(solution)/shard_map/ppermute | solution.py:249
  21.9 1.9 %collective-permute-start.13 = (bf16[72,512]{1,0:T(8,128)(2,1)S(1)}, bf16[72,512]{1,0:T(8,128)(2,1)S(1)}, u32[]{:S(2)}, u32[]{:S(2)}) collective-permute-start(bf16[72,512]{1,0:T(8,128)(2,1)S(1)} %get-tuple-element.35), channel_id=1, source_target_pairs={{0,5},{1,4},{2,7},{3,6},{4,1},{5,0},{6,3},{7,2},{8,13},{9,12},{10,... | collective-permute-start | bytes 221192 | tf_op jit(solution)/shard_map/ppermute | solution.py:249
  24.5 1.7 %collective-permute-done.13.refs_11_ = bf16[72,512]{1,0:T(8,128)(2,1)S(1)} collective-permute-done((bf16[72,512]{1,0:T(8,128)(2,1)S(1)}, bf16[72,512]{1,0:T(8,128)(2,1)S(1)}, u32[]{:S(2)}, u32[]{:S(2)}) %collective-permute-start.13) | collective-permute-done | bytes 73760 | tf_op jit(solution)/shard_map/ppermute | solution.py:249
  26.2 1.2 %attend.1 = (f32[4,1,8,128]{3,2,1,0:T(8,128)S(1)}, f32[4,1,8,128]{3,2,1,0:T(8,128)S(1)}) custom-call(s32[1]{0:T(128)} %bitcast.device_ref, f32[1]{0:T(128)S(6)} %copy.16.guidance_ref, bf16[64,4096]{1,0:T(8,128)(2,1)S(1)} %bitcast.2, bf16[8,128]{1,0:T(8,128)(2,1)S(1)} %get-tuple-element.27.home_ref, bf16[64,1024]{1,0:T(8,128)(2,1)S(1)} %get-tuple-element.28.refs_0_, ...), custom_call_target="tpu_custom_call" | custom-call | tf_op jit(solution)/shard_map/attend/pallas_call | solution.py:299
  27.5 2.2 %collective-permute-start.14 = (f32[4,1,8,128]{3,2,1,0:T(8,128)S(1)}, f32[4,1,8,128]{3,2,1,0:T(8,128)S(1)}, u32[]{:S(2)}, u32[]{:S(2)}) collective-permute-start(f32[4,1,8,128]{3,2,1,0:T(8,128)S(1)} %get-tuple-element.37), channel_id=1, source_target_pairs={{0,2},{1,3},{2,0},{3,1},{4,6},{5,7},{6,4},{7,5},{8,10},{9,11},{10,... | collective-permute-start | bytes 49160 | tf_op jit(solution)/shard_map/ppermute | solution.py:249
  29.6 1.7 %collective-permute-done.14.came_ref = f32[4,1,8,128]{3,2,1,0:T(8,128)S(1)} collective-permute-done((f32[4,1,8,128]{3,2,1,0:T(8,128)S(1)}, f32[4,1,8,128]{3,2,1,0:T(8,128)S(1)}, u32[]{:S(2)}, u32[]{:S(2)}) %collective-permute-start.14) | collective-permute-done | bytes 16416 | tf_op jit(solution)/shard_map/ppermute | solution.py:249
  31.4 2.2 %collective-permute-start.16 = (f32[1,8,128]{2,1,0:T(8,128)S(1)}, f32[1,8,128]{2,1,0:T(8,128)S(1)}, u32[]{:S(2)}, u32[]{:S(2)}) collective-permute-start(f32[1,8,128]{2,1,0:T(8,128)S(1)} %get-tuple-element.39), channel_id=1, source_target_pairs={{0,5},{1,4},{2,7},{3,6},{4,1},{5,0},{6,3},{7,2},{8,13},{9,12},{10,... | collective-permute-start | bytes 12296 | tf_op jit(solution)/shard_map/ppermute | solution.py:249
  33.6 2.3 %collective-permute-start.17 = (f32[1,8,128]{2,1,0:T(8,128)S(1)}, f32[1,8,128]{2,1,0:T(8,128)S(1)}, u32[]{:S(2)}, u32[]{:S(2)}) collective-permute-start(f32[1,8,128]{2,1,0:T(8,128)S(1)} %get-tuple-element.40), channel_id=1, source_target_pairs={{0,9},{1,8},{2,11},{3,10},{4,13},{5,12},{6,15},{7,14},{8,1},{9,0},... | collective-permute-start | bytes 12296 | tf_op jit(solution)/shard_map/ppermute | solution.py:249
  36.5 0.1 prepare.1
  36.7 0.9 %collective-permute-done.17.refs_2_ = f32[1,8,128]{2,1,0:T(8,128)S(1)} collective-permute-done((f32[1,8,128]{2,1,0:T(8,128)S(1)}, f32[1,8,128]{2,1,0:T(8,128)S(1)}, u32[]{:S(2)}, u32[]{:S(2)}) %collective-permute-start.17) | collective-permute-done | bytes 4128 | tf_op jit(solution)/shard_map/ppermute | solution.py:249
  37.5 3.2 %collective-permute-done.18.refs_3_ = f32[1,8,128]{2,1,0:T(8,128)S(1)} collective-permute-done((f32[1,8,128]{2,1,0:T(8,128)S(1)}, f32[1,8,128]{2,1,0:T(8,128)S(1)}, u32[]{:S(2)}, u32[]{:S(2)}) %collective-permute-start.18) | collective-permute-done | bytes 4128 | tf_op jit(solution)/shard_map/ppermute | solution.py:249
  40.7 0.8 %finish.1 = (f32[1,64,64]{2,1,0:T(8,128)}, f32[1,16,64]{2,1,0:T(8,128)}) custom-call(f32[1,8,128]{2,1,0:T(8,128)S(1)} %collective-permute-done.15.refs_0_, f32[1,8,128]{2,1,0:T(8,128)S(1)} %collective-permute-done.16.refs_1_, f32[1,8,128]{2,1,0:T(8,128)S(1)} %collective-permute-done.17.refs_2_, f32[1,8,128]{2,1,0:T(8,128)S(1)} %collective-permute-done.18.refs_3_, ...), custom_call_target="tpu_custom_call" | custom-call | tf_op jit(solution)/shard_map/finish/pallas_call | solution.py:330
  (19 shorter events, 0.1 us)
Async XLA Ops:
  0.6 25.6 %copy-start = (bf16[4096,64]{0,1:T(8,128)(2,1)S(1)}, bf16[4096,64]{0,1:T(8,128)(2,1)}, u32[]{:S(2)}) copy-start(bf16[4096,64]{0,1:T(8,128)(2,1)} %param.16) | copy-start | bytes 1572868
  1.9 18.6 %collective-permute-start.3 = (bf16[64,1024]{1,0:T(8,128)(2,1)S(1)}, bf16[64,1024]{1,0:T(8,128)(2,1)S(1)}, u32[]{:S(2)}, u32[]{:S(2)}) collective-permute-start(bf16[64,1024]{1,0:T(8,128)(2,1)S(1)} %get-tuple-element.29), channel_id=1, source_target_pairs={{0,6},{1,7},{2,4},{3,5},{4,2},{5,3},{6,0},{7,1},{8,14},{9,15},{10,... | collective-permute-start | bytes 393224 | tf_op jit(solution)/shard_map/ppermute | solution.py:249
  5.9 14.8 %collective-permute-start.4 = (bf16[64,1024]{1,0:T(8,128)(2,1)S(1)}, bf16[64,1024]{1,0:T(8,128)(2,1)S(1)}, u32[]{:S(2)}, u32[]{:S(2)}) collective-permute-start(bf16[64,1024]{1,0:T(8,128)(2,1)S(1)} %get-tuple-element.30), channel_id=1, source_target_pairs={{0,2},{1,3},{2,0},{3,1},{4,6},{5,7},{6,4},{7,5},{8,10},{9,11},{10,... | collective-permute-start | bytes 393224 | tf_op jit(solution)/shard_map/ppermute | solution.py:249
  6.4 14.6 %collective-permute-start.5 = (bf16[64,1024]{1,0:T(8,128)(2,1)S(1)}, bf16[64,1024]{1,0:T(8,128)(2,1)S(1)}, u32[]{:S(2)}, u32[]{:S(2)}) collective-permute-start(bf16[64,1024]{1,0:T(8,128)(2,1)S(1)} %get-tuple-element.31), channel_id=1, source_target_pairs={{0,4},{1,5},{2,6},{3,7},{4,0},{5,1},{6,2},{7,3},{8,12},{9,13},{10,... | collective-permute-start | bytes 393224 | tf_op jit(solution)/shard_map/ppermute | solution.py:249
  7.5 0.7 %copy-start.2 = (s32[1,64]{1,0:T(1,128)S(1)}, s32[1,64]{1,0:T(1,128)}, u32[]{:S(2)}) copy-start(s32[1,64]{1,0:T(1,128)} %dest_ref.1) | copy-start | bytes 772
  7.5 10.3 %collective-permute-start.10 = (bf16[64,512]{1,0:T(8,128)(2,1)S(1)}, bf16[64,512]{1,0:T(8,128)(2,1)S(1)}, u32[]{:S(2)}, u32[]{:S(2)}) collective-permute-start(bf16[64,512]{1,0:T(8,128)(2,1)S(1)} %get-tuple-element.32), channel_id=1, source_target_pairs={{0,1},{1,0},{2,3},{3,2},{4,5},{5,4},{6,7},{7,6},{8,9},{9,8},{10,11... | collective-permute-start | bytes 196616 | tf_op jit(solution)/shard_map/ppermute | solution.py:249
  8.2 1.2 %collective-permute-start.1 = (s32[1,64]{1,0:T(1,128)S(1)}, s32[1,64]{1,0:T(1,128)S(1)}, u32[]{:S(2)}, u32[]{:S(2)}) collective-permute-start(s32[1,64]{1,0:T(1,128)S(1)} %copy-done.2), channel_id=1, source_target_pairs={{0,1},{1,0},{2,3},{3,2},{4,5},{5,4},{6,7},{7,6},{8,9},{9,8},{10,11... | collective-permute-start | bytes 776 | tf_op jit(solution)/shard_map/ppermute | solution.py:249
  9.3 4.5 %collective-permute-start = (s32[1,64]{1,0:T(1,128)S(1)}, s32[1,64]{1,0:T(1,128)S(1)}, u32[]{:S(2)}, u32[]{:S(2)}) collective-permute-start(s32[1,64]{1,0:T(1,128)S(1)} %copy-done.2), channel_id=1, source_target_pairs={{0,8},{1,9},{2,10},{3,11},{4,12},{5,13},{6,14},{7,15},{8,0},{9,1},... | collective-permute-start | bytes 776 | tf_op jit(solution)/shard_map/ppermute | solution.py:249
  13.8 1.2 %collective-permute-start.2 = (s32[1,64]{1,0:T(1,128)S(1)}, s32[1,64]{1,0:T(1,128)S(1)}, u32[]{:S(2)}, u32[]{:S(2)}) collective-permute-start(s32[1,64]{1,0:T(1,128)S(1)} %collective-permute-done.other_ref), channel_id=1, source_target_pairs={{0,1},{1,0},{2,3},{3,2},{4,5},{5,4},{6,7},{7,6},{8,9},{9,8},{10,11... | collective-permute-start | bytes 776 | tf_op jit(solution)/shard_map/ppermute | solution.py:249
  15.1 5.0 %collective-permute-start.11 = (bf16[72,512]{1,0:T(8,128)(2,1)S(1)}, bf16[72,512]{1,0:T(8,128)(2,1)S(1)}, u32[]{:S(2)}, u32[]{:S(2)}) collective-permute-start(bf16[72,512]{1,0:T(8,128)(2,1)S(1)} %get-tuple-element.33), channel_id=1, source_target_pairs={{0,7},{1,6},{2,5},{3,4},{4,3},{5,2},{6,1},{7,0},{8,15},{9,14},{10,... | collective-permute-start | bytes 221192 | tf_op jit(solution)/shard_map/ppermute | solution.py:249
  17.8 4.0 %collective-permute-start.12 = (bf16[72,512]{1,0:T(8,128)(2,1)S(1)}, bf16[72,512]{1,0:T(8,128)(2,1)S(1)}, u32[]{:S(2)}, u32[]{:S(2)}) collective-permute-start(bf16[72,512]{1,0:T(8,128)(2,1)S(1)} %get-tuple-element.34), channel_id=1, source_target_pairs={{0,3},{1,2},{2,1},{3,0},{4,7},{5,6},{6,5},{7,4},{8,11},{9,10},{10,... | collective-permute-start | bytes 221192 | tf_op jit(solution)/shard_map/ppermute | solution.py:249
  20.2 6.0 %collective-permute-start.6 = (bf16[64,1024]{1,0:T(8,128)(2,1)S(1)}, bf16[64,1024]{1,0:T(8,128)(2,1)S(1)}, u32[]{:S(2)}, u32[]{:S(2)}) collective-permute-start(bf16[64,1024]{1,0:T(8,128)(2,1)S(1)} %get-tuple-element.28.refs_0_), channel_id=1, source_target_pairs={{0,1},{1,0},{2,3},{3,2},{4,5},{5,4},{6,7},{7,6},{8,9},{9,8},{10,11... | collective-permute-start | bytes 393224 | tf_op jit(solution)/shard_map/ppermute | solution.py:249
  20.5 5.7 %collective-permute-start.7 = (bf16[64,1024]{1,0:T(8,128)(2,1)S(1)}, bf16[64,1024]{1,0:T(8,128)(2,1)S(1)}, u32[]{:S(2)}, u32[]{:S(2)}) collective-permute-start(bf16[64,1024]{1,0:T(8,128)(2,1)S(1)} %collective-permute-done.3.refs_1_), channel_id=1, source_target_pairs={{0,1},{1,0},{2,3},{3,2},{4,5},{5,4},{6,7},{7,6},{8,9},{9,8},{10,11... | collective-permute-start | bytes 393224 | tf_op jit(solution)/shard_map/ppermute | solution.py:249
  20.7 5.5 %collective-permute-start.8 = (bf16[64,1024]{1,0:T(8,128)(2,1)S(1)}, bf16[64,1024]{1,0:T(8,128)(2,1)S(1)}, u32[]{:S(2)}, u32[]{:S(2)}) collective-permute-start(bf16[64,1024]{1,0:T(8,128)(2,1)S(1)} %collective-permute-done.4.refs_2_), channel_id=1, source_target_pairs={{0,1},{1,0},{2,3},{3,2},{4,5},{5,4},{6,7},{7,6},{8,9},{9,8},{10,11... | collective-permute-start | bytes 393224 | tf_op jit(solution)/shard_map/ppermute | solution.py:249
  21.0 5.2 %collective-permute-start.9 = (bf16[64,1024]{1,0:T(8,128)(2,1)S(1)}, bf16[64,1024]{1,0:T(8,128)(2,1)S(1)}, u32[]{:S(2)}, u32[]{:S(2)}) collective-permute-start(bf16[64,1024]{1,0:T(8,128)(2,1)S(1)} %collective-permute-done.5.refs_3_), channel_id=1, source_target_pairs={{0,1},{1,0},{2,3},{3,2},{4,5},{5,4},{6,7},{7,6},{8,9},{9,8},{10,11... | collective-permute-start | bytes 393224 | tf_op jit(solution)/shard_map/ppermute | solution.py:249
  21.9 4.3 %collective-permute-start.13 = (bf16[72,512]{1,0:T(8,128)(2,1)S(1)}, bf16[72,512]{1,0:T(8,128)(2,1)S(1)}, u32[]{:S(2)}, u32[]{:S(2)}) collective-permute-start(bf16[72,512]{1,0:T(8,128)(2,1)S(1)} %get-tuple-element.35), channel_id=1, source_target_pairs={{0,5},{1,4},{2,7},{3,6},{4,1},{5,0},{6,3},{7,2},{8,13},{9,12},{10,... | collective-permute-start | bytes 221192 | tf_op jit(solution)/shard_map/ppermute | solution.py:249
  27.4 9.0 %copy-start.1 = (f32[1,64,64]{2,1,0:T(8,128)S(1)}, f32[1,64,64]{2,1,0:T(8,128)}, u32[]{:S(2)}) copy-start(f32[1,64,64]{2,1,0:T(8,128)} %refs_8_.1) | copy-start | bytes 49156
  27.5 3.9 %collective-permute-start.14 = (f32[4,1,8,128]{3,2,1,0:T(8,128)S(1)}, f32[4,1,8,128]{3,2,1,0:T(8,128)S(1)}, u32[]{:S(2)}, u32[]{:S(2)}) collective-permute-start(f32[4,1,8,128]{3,2,1,0:T(8,128)S(1)} %get-tuple-element.37), channel_id=1, source_target_pairs={{0,2},{1,3},{2,0},{3,1},{4,6},{5,7},{6,4},{7,5},{8,10},{9,11},{10,... | collective-permute-start | bytes 49160 | tf_op jit(solution)/shard_map/ppermute | solution.py:249
  31.4 5.3 %collective-permute-start.15 = (f32[1,8,128]{2,1,0:T(8,128)S(1)}, f32[1,8,128]{2,1,0:T(8,128)S(1)}, u32[]{:S(2)}, u32[]{:S(2)}) collective-permute-start(f32[1,8,128]{2,1,0:T(8,128)S(1)} %get-tuple-element.38), channel_id=1, source_target_pairs={{0,1},{1,0},{2,3},{3,2},{4,5},{5,4},{6,7},{7,6},{8,9},{9,8},{10,11... | collective-permute-start | bytes 12296 | tf_op jit(solution)/shard_map/ppermute | solution.py:249
  31.4 5.3 %collective-permute-start.16 = (f32[1,8,128]{2,1,0:T(8,128)S(1)}, f32[1,8,128]{2,1,0:T(8,128)S(1)}, u32[]{:S(2)}, u32[]{:S(2)}) collective-permute-start(f32[1,8,128]{2,1,0:T(8,128)S(1)} %get-tuple-element.39), channel_id=1, source_target_pairs={{0,5},{1,4},{2,7},{3,6},{4,1},{5,0},{6,3},{7,2},{8,13},{9,12},{10,... | collective-permute-start | bytes 12296 | tf_op jit(solution)/shard_map/ppermute | solution.py:249
  33.6 3.9 %collective-permute-start.17 = (f32[1,8,128]{2,1,0:T(8,128)S(1)}, f32[1,8,128]{2,1,0:T(8,128)S(1)}, u32[]{:S(2)}, u32[]{:S(2)}) collective-permute-start(f32[1,8,128]{2,1,0:T(8,128)S(1)} %get-tuple-element.40), channel_id=1, source_target_pairs={{0,9},{1,8},{2,11},{3,10},{4,13},{5,12},{6,15},{7,14},{8,1},{9,0},... | collective-permute-start | bytes 12296 | tf_op jit(solution)/shard_map/ppermute | solution.py:249
  35.8 4.8 %collective-permute-start.18 = (f32[1,8,128]{2,1,0:T(8,128)S(1)}, f32[1,8,128]{2,1,0:T(8,128)S(1)}, u32[]{:S(2)}, u32[]{:S(2)}) collective-permute-start(f32[1,8,128]{2,1,0:T(8,128)S(1)} %get-tuple-element.41), channel_id=1, source_target_pairs={{0,13},{1,12},{2,15},{3,14},{4,9},{5,8},{6,11},{7,10},{8,5},{9,4},... | collective-permute-start | bytes 12296 | tf_op jit(solution)/shard_map/ppermute | solution.py:249
